TPU v7x, 32 devices: a whole 2x2x4 slice. The times are simulated.
32 devices in a mesh: wide: 8 (over y, x, core), narrow: 4 (over z).
Axes of the slice: x: 2, y: 2, z: 4, core: 2. Of those that a mesh axis runs over, the one named last changes fastest.
Arguments:
- start_field: float32 [64, 16384], P(None, ('wide', 'narrow')), may hold values from -6 to 6
- right_side: float32 [64, 16384], P(None, ('wide', 'narrow')), may hold values from -6 to 6
- element_scale: float32 [16384], P(('wide', 'narrow')), may hold values from 2 to 6
- face_scale: float32 [6, 16384], P(None, ('wide', 'narrow')), may hold values from 0.1 to 0.6
- face_nbr: int32 [6, 16384], P(None, ('wide', 'narrow')), may hold values from -1 to 767, as said below
- send_list: int32 [4, 2048], P(None, ('wide', 'narrow')), may hold values from 0 to 511, as said below
- counts: int32 [32], P(('wide', 'narrow')), may hold values from 256 to 512, as said below
- coarse_slot: int32 [16384], P(('wide', 'narrow')), may hold values from 0 to 511, as said below
- elem_block: float32 [64, 64], replicated, may hold values from -1.5 to 1.5
- smooth_block: float32 [64, 64], replicated, may hold values from -1.5 to 1.5
- face_blocks: float32 [6, 64, 64], replicated, may hold values from -0.375 to 0.375
- prolong: float32 [8, 64, 8], replicated, may hold values from -1 to 1
- coarse_scale: float32 [2048], P(('wide', 'narrow')), may hold values from 2 to 6
- coarse_face_scale: float32 [6, 2048], P(None, ('wide', 'narrow')), may hold values from 0.1 to 0.6
- coarse_nbr: int32 [6, 2048], P(None, ('wide', 'narrow')), may hold values from -1 to 127, as said below
- coarse_send: int32 [4, 512], P(None, ('wide', 'narrow')), may hold values from 0 to 63, as said below
- coarse_block: float32 [8, 8], replicated, may hold values from -1.5 to 1.5
- coarse_smooth: float32 [8, 8], replicated, may hold values from -1.5 to 1.5
- coarse_faces: float32 [6, 8, 8], replicated, may hold values from -0.9 to 0.9
Outputs:
- smoothed_field: float32 [64, 16384], P(None, ('wide', 'narrow'))
- coarse_correction: float32 [8, 2048], P(None, ('wide', 'narrow'))
Inputs may be any that keep to these rules, and one draw needn't show every extreme that they name: `face_nbr`: -1 marks a face without neighbour; a value below 512 names a slot of the same partition; 512 + d * 64 + j names the j-th element sent by the neighbouring partition in direction d. Each partition names every value from 512 to 767 on some face. `send_list`: row d holds, for each partition, 64 distinct local slots: row 0 goes to the partition one higher on wide, row 1 one lower on wide, rows 2 and 3 likewise on narrow, cyclically. `counts`: one partition has 512 active elements and one has 256. `coarse_slot`: within each partition a permutation of 0 to 511. `coarse_nbr`: as face_nbr, with 64 coarse elements and 16 sent in each direction. `coarse_send`: as send_list, 16 distinct local coarse elements for each partition and direction.
All inputs are finite; a program needn't handle non-finite values.
Results may differ from a plain program's by a relative error of at most 0.0003.
Values sent between devices are 32-bit elements; how exact they have to be, the bound alone decides.
No kernel may reach another device: no remote copies, remote signals or barrier semaphores. Data moves between devices by JAX's collectives and lax.ppermute only.
A program may use at most 64 MiB of HBM per device.

v0:
```python
import jax
import jax.numpy as jnp
from jax import lax
from jax.sharding import PartitionSpec as P

CS = 3


OMEGA = 0.7
COARSE_OMEGA = 0.6
HIGH = lax.Precision.HIGHEST


def passed_along(block, axis, distance):
    devices = range(lax.axis_size(axis))
    route = [((i - distance) % len(devices), i) for i in devices]
    return lax.ppermute(block, axis, route)


def product(left, right):
    return jnp.dot(left, right, preferred_element_type=jnp.float32, precision=HIGH)


def fine_ghosts(current, sends):
    pieces = []
    for direction, offset in ((0, 1), (1, -1)):
        packet = jnp.take(current, sends[direction], axis=1)
        pieces.append(passed_along(packet, "wide", offset))
    for direction, offset in ((2, 1), (3, -1)):
        packet = jnp.take(current, sends[direction], axis=1)
        pieces.append(passed_along(packet, "narrow", offset))
    return jnp.concatenate(pieces, axis=1)


def coarse_ghosts(current, sends):
    pieces = []
    for direction, offset in ((0, 1), (1, -1)):
        packet = jnp.take(current, sends[direction], axis=1)
        pieces.append(passed_along(packet, "wide", offset))
    for direction, offset in ((2, 1), (3, -1)):
        packet = jnp.take(current, sends[direction], axis=1)
        pieces.append(passed_along(packet, "narrow", offset))
    return jnp.concatenate(pieces, axis=1)


def apply_operator(current, ghosts, scale, face_scale, table, block, faces):
    extended = jnp.concatenate([current, ghosts], axis=1)
    result = scale[None, :] * product(block, current)
    for face_index in range(6):
        target = table[face_index]
        weight = jnp.where(target >= 0, face_scale[face_index], 0.0)
        gathered = jnp.take(extended, jnp.maximum(target, 0), axis=1)
        result = result + weight[None, :] * product(faces[face_index], gathered)
    return result


def smooth_step(current, residual, active, scale, block):
    return current + OMEGA * active[None, :] * product(block, residual) / scale[None, :]


def body(
    start_field,
    right_side,
    element_scale,
    face_scale,
    face_nbr,
    send_list,
    counts,
    coarse_slot,
    elem_block,
    smooth_block,
    face_blocks,
    prolong,
    coarse_scale,
    coarse_face_scale,
    coarse_nbr,
    coarse_send,
    coarse_block,
    coarse_smooth,
    coarse_faces,
):
    rows = start_field.shape[0]
    elements = start_field.shape[1]
    active = (jnp.arange(elements, dtype=jnp.int32) < counts[0]).astype(jnp.float32)
    start = start_field * active[None, :]
    source = right_side * active[None, :]

    def fine_apply(current):
        return apply_operator(
            current,
            fine_ghosts(current, send_list),
            element_scale,
            face_scale,
            face_nbr,
            elem_block,
            face_blocks,
        )

    first_residual = source - fine_apply(start)
    smoothed = smooth_step(start, first_residual, active, element_scale, smooth_block)
    fine_residual = source - fine_apply(smoothed)
    ordered = jnp.zeros_like(fine_residual).at[:, coarse_slot].set(fine_residual)
    ordered = ordered.reshape(rows, elements // 8, 8)
    coarse_rhs = jnp.einsum("kij,ick->jc", prolong, ordered, precision=HIGH)
    correction = COARSE_OMEGA * product(coarse_smooth, coarse_rhs) / coarse_scale[None, :]
    for sweep_index in range(CS - 1):
        correction = (
            correction
            + COARSE_OMEGA
            * product(
                coarse_smooth,
                coarse_rhs
                - apply_operator(
                    correction,
                    coarse_ghosts(correction, coarse_send),
                    coarse_scale,
                    coarse_face_scale,
                    coarse_nbr,
                    coarse_block,
                    coarse_faces,
                ),
            )
            / coarse_scale[None, :]
        )
    expanded = jnp.einsum("kij,jc->ick", prolong, correction, precision=HIGH).reshape(
        rows, elements
    )
    delta = active[None, :] * jnp.take(expanded, coarse_slot, axis=1)
    corrected = smoothed + delta
    final_residual = source - fine_apply(corrected)
    smoothed_field = smooth_step(corrected, final_residual, active, element_scale, smooth_block)
    return (smoothed_field, correction)


def solution(mesh):
    return jax.shard_map(
        body,
        mesh=mesh,
        in_specs=(
            P(None, ("wide", "narrow")),
            P(None, ("wide", "narrow")),
            P(("wide", "narrow")),
            P(None, ("wide", "narrow")),
            P(None, ("wide", "narrow")),
            P(None, ("wide", "narrow")),
            P(("wide", "narrow")),
            P(("wide", "narrow")),
            P(),
            P(),
            P(),
            P(),
            P(("wide", "narrow")),
            P(None, ("wide", "narrow")),
            P(None, ("wide", "narrow")),
            P(None, ("wide", "narrow")),
            P(),
            P(),
            P(),
        ),
        out_specs=(P(None, ("wide", "narrow")), P(None, ("wide", "narrow"))),
        check_vma=False,
    )
```

profile of v0, /device:TPU:0, one launch (start us, length us, event | category | flops | bytes accessed | tf_op | source)
XLA Modules:
  0.0 109.7 jit_solution(10182553072823631834)
XLA Ops:
  1.3 0.9 broadcast_multiply_fusion
  3.0 0.6 gather_fusion.2
  3.7 3.4 %collective-permute-start.1 = (f32[64,64]{1,0:T(8,128)S(1)}, f32[64,64]{1,0:T(8,128)S(1)}, u32[]{:S(2)}, u32[]{:S(2)}) collective-permute-start(f32[64,64]{1,0:T(8,128)S(1)} %select_bitcast_fusion.10), channel_id=1, source_target_pairs={{4,0},{8,4},{12,8},{16,12},{20,16},{24,20},{28,24},{0,28},{5,1},{9... | collective-permute-start | bytes 49160 | tf_op jit(solution)/shard_map/ppermute | solution.py:17
  7.8 1.6 %collective-permute-start.2 = (f32[64,64]{1,0:T(8,128)S(1)}, f32[64,64]{1,0:T(8,128)S(1)}, u32[]{:S(2)}, u32[]{:S(2)}) collective-permute-start(f32[64,64]{1,0:T(8,128)S(1)} %select_bitcast_fusion.9), channel_id=1, source_target_pairs={{3,0},{0,1},{1,2},{2,3},{7,4},{4,5},{5,6},{6,7},{11,8},{8,9},{9,10... | collective-permute-start | bytes 49160 | tf_op jit(solution)/shard_map/ppermute | solution.py:17
  9.4 0.6 gather_fusion.4
  10.1 2.3 %collective-permute-start.3 = (f32[64,64]{1,0:T(8,128)S(1)}, f32[64,64]{1,0:T(8,128)S(1)}, u32[]{:S(2)}, u32[]{:S(2)}) collective-permute-start(f32[64,64]{1,0:T(8,128)S(1)} %select_bitcast_fusion.8), channel_id=1, source_target_pairs={{1,0},{2,1},{3,2},{0,3},{5,4},{6,5},{7,6},{4,7},{9,8},{10,9},{11,1... | collective-permute-start | bytes 49160 | tf_op jit(solution)/shard_map/ppermute | solution.py:17
  13.2 0.6 copy-done.4
  14.0 0.6 copy-done.9
  14.7 0.7 copy-done.15
  15.5 0.7 copy-done.10
  16.2 0.7 copy-done.13
  17.6 1.0 gather_fusion.9
  18.7 1.0 gather_fusion.8
  19.7 1.0 gather_fusion.7
  20.8 1.0 gather_fusion.6
  21.8 1.0 gather_fusion.5
  22.9 1.0 gather_fusion.10
  28.6 0.6 gather_fusion.12
  29.2 0.6 gather_fusion.13
  29.8 0.6 gather_fusion.14
  30.4 0.6 gather_fusion.11
  31.1 1.6 %collective-permute-start.5 = (f32[64,64]{1,0:T(8,128)S(1)}, f32[64,64]{1,0:T(8,128)S(1)}, u32[]{:S(2)}, u32[]{:S(2)}) collective-permute-start(f32[64,64]{1,0:T(8,128)S(1)} %select_bitcast_fusion.6), channel_id=1, source_target_pairs={{4,0},{8,4},{12,8},{16,12},{20,16},{24,20},{28,24},{0,28},{5,1},{9... | collective-permute-start | bytes 49160 | tf_op jit(solution)/shard_map/ppermute | solution.py:17
  32.9 3.9 %collective-permute-start.7 = (f32[64,64]{1,0:T(8,128)S(1)}, f32[64,64]{1,0:T(8,128)S(1)}, u32[]{:S(2)}, u32[]{:S(2)}) collective-permute-start(f32[64,64]{1,0:T(8,128)S(1)} %select_bitcast_fusion.4), channel_id=1, source_target_pairs={{1,0},{2,1},{3,2},{0,3},{5,4},{6,5},{7,6},{4,7},{9,8},{10,9},{11,1... | collective-permute-start | bytes 49160 | tf_op jit(solution)/shard_map/ppermute | solution.py:17
  36.9 1.6 %collective-permute-done.6 = f32[64,64]{1,0:T(8,128)S(1)} collective-permute-done((f32[64,64]{1,0:T(8,128)S(1)}, f32[64,64]{1,0:T(8,128)S(1)}, u32[]{:S(2)}, u32[]{:S(2)}) %collective-permute-start.6) | collective-permute-done | bytes 16416 | tf_op jit(solution)/shard_map/ppermute | solution.py:17
  38.5 2.6 %collective-permute-done.4 = f32[64,64]{1,0:T(8,128)S(1)} collective-permute-done((f32[64,64]{1,0:T(8,128)S(1)}, f32[64,64]{1,0:T(8,128)S(1)}, u32[]{:S(2)}, u32[]{:S(2)}) %collective-permute-start.4) | collective-permute-done | bytes 16416 | tf_op jit(solution)/shard_map/ppermute | solution.py:17
  41.4 1.0 gather_fusion.19
  42.4 1.0 gather_fusion.18
  43.5 1.0 gather_fusion.17
  44.5 1.0 gather_fusion.16
  45.6 1.0 gather_fusion.15
  46.6 1.0 gather_fusion.20
  51.2 1.8 %scatter_custom_fusion = f32[64,512]{0,1:T(8,128)S(1)} fusion(s32[512]{0:T(512)S(1)} %compare_select_fusion.12, f32[512,64]{1,0:T(8,128)S(1)} %copy.122, f32[]{:T(128)} %constant.33.clone.1), kind=kCustom, calls=%fused_computation.203 | custom fusion | bytes 131076 | tf_op jit(solution)/shard_map/scatter | solution.py:102
  55.2 3.8 %collective-permute-start.11 = (f32[8,16]{1,0:T(8,128)S(1)}, f32[8,16]{1,0:T(8,128)S(1)}, u32[]{:S(2)}, u32[]{:S(2)}) collective-permute-start(f32[8,16]{1,0:T(8,128)S(1)} %select_bitcast_fusion.16), channel_id=1, source_target_pairs={{1,0},{2,1},{3,2},{0,3},{5,4},{6,5},{7,6},{4,7},{9,8},{10,9},{11,1... | collective-permute-start | bytes 1544 | tf_op jit(solution)/shard_map/ppermute | solution.py:17
  61.3 3.1 %collective-permute-done.8 = f32[8,16]{1,0:T(8,128)S(1)} collective-permute-done((f32[8,16]{1,0:T(8,128)S(1)}, f32[8,16]{1,0:T(8,128)S(1)}, u32[]{:S(2)}, u32[]{:S(2)}) %collective-permute-start.8) | collective-permute-done | bytes 544 | tf_op jit(solution)/shard_map/ppermute | solution.py:17
  64.6 0.6 gather_fusion.25
  65.2 0.6 gather_fusion.26
  65.8 0.6 gather_fusion.27
  66.4 0.6 gather_fusion.28
  67.0 0.6 gather_fusion.29
  67.6 0.6 gather_fusion.30
  72.5 3.8 %collective-permute-start.15 = (f32[8,16]{1,0:T(8,128)S(1)}, f32[8,16]{1,0:T(8,128)S(1)}, u32[]{:S(2)}, u32[]{:S(2)}) collective-permute-start(f32[8,16]{1,0:T(8,128)S(1)} %select_bitcast_fusion.12), channel_id=1, source_target_pairs={{1,0},{2,1},{3,2},{0,3},{5,4},{6,5},{7,6},{4,7},{9,8},{10,9},{11,1... | collective-permute-start | bytes 1544 | tf_op jit(solution)/shard_map/ppermute | solution.py:17
  76.6 1.3 %collective-permute-done.14 = f32[8,16]{1,0:T(8,128)S(1)} collective-permute-done((f32[8,16]{1,0:T(8,128)S(1)}, f32[8,16]{1,0:T(8,128)S(1)}, u32[]{:S(2)}, u32[]{:S(2)}) %collective-permute-start.14) | collective-permute-done | bytes 544 | tf_op jit(solution)/shard_map/ppermute | solution.py:17
  77.9 2.5 %collective-permute-done.12 = f32[8,16]{1,0:T(8,128)S(1)} collective-permute-done((f32[8,16]{1,0:T(8,128)S(1)}, f32[8,16]{1,0:T(8,128)S(1)}, u32[]{:S(2)}, u32[]{:S(2)}) %collective-permute-start.12) | collective-permute-done | bytes 544 | tf_op jit(solution)/shard_map/ppermute | solution.py:17
  80.5 0.6 gather_fusion.36
  81.1 0.6 gather_fusion.35
  81.7 0.6 gather_fusion.37
  82.3 0.6 gather_fusion.38
  82.9 0.6 gather_fusion.39
  83.5 0.6 gather_fusion.40
  86.5 1.0 gather_fusion
  87.8 0.6 gather_fusion.42
  88.4 0.6 gather_fusion.43
  89.0 0.6 gather_fusion.44
  89.6 0.6 gather_fusion.41
  90.6 3.9 %collective-permute-start.19 = (f32[64,64]{1,0:T(8,128)S(1)}, f32[64,64]{1,0:T(8,128)S(1)}, u32[]{:S(2)}, u32[]{:S(2)}) collective-permute-start(f32[64,64]{1,0:T(8,128)S(1)} %select_bitcast_fusion), channel_id=1, source_target_pairs={{1,0},{2,1},{3,2},{0,3},{5,4},{6,5},{7,6},{4,7},{9,8},{10,9},{11,1... | collective-permute-start | bytes 49160 | tf_op jit(solution)/shard_map/ppermute | solution.py:17
  94.6 1.8 %collective-permute-done.18 = f32[64,64]{1,0:T(8,128)S(1)} collective-permute-done((f32[64,64]{1,0:T(8,128)S(1)}, f32[64,64]{1,0:T(8,128)S(1)}, u32[]{:S(2)}, u32[]{:S(2)}) %collective-permute-start.18) | collective-permute-done | bytes 16416 | tf_op jit(solution)/shard_map/ppermute | solution.py:17
  96.5 2.4 %collective-permute-done.16 = f32[64,64]{1,0:T(8,128)S(1)} collective-permute-done((f32[64,64]{1,0:T(8,128)S(1)}, f32[64,64]{1,0:T(8,128)S(1)}, u32[]{:S(2)}, u32[]{:S(2)}) %collective-permute-start.16) | collective-permute-done | bytes 16416 | tf_op jit(solution)/shard_map/ppermute | solution.py:17
  99.1 1.0 gather_fusion.45
  100.2 1.0 gather_fusion.49
  101.2 1.0 gather_fusion.48
  102.3 1.0 gather_fusion.47
  103.3 1.0 gather_fusion.46
  104.3 1.0 gather_fusion.50
  108.8 0.9 fusion.30
  (205 shorter events, 28.1 us)
Async XLA Ops:
  0.6 26.4 %copy-start = (f32[64,64]{1,0:T(8,128)S(1)}, f32[64,64]{1,0:T(8,128)}, u32[]{:S(2)}) copy-start(f32[64,64]{1,0:T(8,128)} %param.35) | copy-start | bytes 49156
  0.6 0.7 copy-start.12
  2.3 0.7 copy-start.14
  3.7 13.2 %collective-permute-start.1 = (f32[64,64]{1,0:T(8,128)S(1)}, f32[64,64]{1,0:T(8,128)S(1)}, u32[]{:S(2)}, u32[]{:S(2)}) collective-permute-start(f32[64,64]{1,0:T(8,128)S(1)} %select_bitcast_fusion.10), channel_id=1, source_target_pairs={{4,0},{8,4},{12,8},{16,12},{20,16},{24,20},{28,24},{0,28},{5,1},{9... | collective-permute-start | bytes 49160 | tf_op jit(solution)/shard_map/ppermute | solution.py:17
  7.8 9.1 %collective-permute-start.2 = (f32[64,64]{1,0:T(8,128)S(1)}, f32[64,64]{1,0:T(8,128)S(1)}, u32[]{:S(2)}, u32[]{:S(2)}) collective-permute-start(f32[64,64]{1,0:T(8,128)S(1)} %select_bitcast_fusion.9), channel_id=1, source_target_pairs={{3,0},{0,1},{1,2},{2,3},{7,4},{4,5},{5,6},{6,7},{11,8},{8,9},{9,10... | collective-permute-start | bytes 49160 | tf_op jit(solution)/shard_map/ppermute | solution.py:17
  10.1 6.8 %collective-permute-start.3 = (f32[64,64]{1,0:T(8,128)S(1)}, f32[64,64]{1,0:T(8,128)S(1)}, u32[]{:S(2)}, u32[]{:S(2)}) collective-permute-start(f32[64,64]{1,0:T(8,128)S(1)} %select_bitcast_fusion.8), channel_id=1, source_target_pairs={{1,0},{2,1},{3,2},{0,3},{5,4},{6,5},{7,6},{4,7},{9,8},{10,9},{11,1... | collective-permute-start | bytes 49160 | tf_op jit(solution)/shard_map/ppermute | solution.py:17
  13.1 0.7 copy-start.4
  13.1 4.3 %collective-permute-start = (f32[64,64]{1,0:T(8,128)S(1)}, f32[64,64]{1,0:T(8,128)S(1)}, u32[]{:S(2)}, u32[]{:S(2)}) collective-permute-start(f32[64,64]{1,0:T(8,128)S(1)} %select_bitcast_fusion.11), channel_id=1, source_target_pairs={{28,0},{0,4},{4,8},{8,12},{12,16},{16,20},{20,24},{24,28},{29,1},{... | collective-permute-start | bytes 49160 | tf_op jit(solution)/shard_map/ppermute | solution.py:17
  13.9 0.7 copy-start.9
  14.7 0.7 copy-start.15
  15.4 0.7 copy-start.10
  16.1 0.7 copy-start.13
  22.9 1.1 copy-start.1
  26.5 0.9 copy-start.2
  26.5 0.9 copy-start.5
  27.4 0.8 copy-start.16
  31.1 5.9 %collective-permute-start.5 = (f32[64,64]{1,0:T(8,128)S(1)}, f32[64,64]{1,0:T(8,128)S(1)}, u32[]{:S(2)}, u32[]{:S(2)}) collective-permute-start(f32[64,64]{1,0:T(8,128)S(1)} %select_bitcast_fusion.6), channel_id=1, source_target_pairs={{4,0},{8,4},{12,8},{16,12},{20,16},{24,20},{28,24},{0,28},{5,1},{9... | collective-permute-start | bytes 49160 | tf_op jit(solution)/shard_map/ppermute | solution.py:17
  32.7 5.8 %collective-permute-start.6 = (f32[64,64]{1,0:T(8,128)S(1)}, f32[64,64]{1,0:T(8,128)S(1)}, u32[]{:S(2)}, u32[]{:S(2)}) collective-permute-start(f32[64,64]{1,0:T(8,128)S(1)} %select_bitcast_fusion.5), channel_id=1, source_target_pairs={{3,0},{0,1},{1,2},{2,3},{7,4},{4,5},{5,6},{6,7},{11,8},{8,9},{9,10... | collective-permute-start | bytes 49160 | tf_op jit(solution)/shard_map/ppermute | solution.py:17
  32.9 5.6 %collective-permute-start.7 = (f32[64,64]{1,0:T(8,128)S(1)}, f32[64,64]{1,0:T(8,128)S(1)}, u32[]{:S(2)}, u32[]{:S(2)}) collective-permute-start(f32[64,64]{1,0:T(8,128)S(1)} %select_bitcast_fusion.4), channel_id=1, source_target_pairs={{1,0},{2,1},{3,2},{0,3},{5,4},{6,5},{7,6},{4,7},{9,8},{10,9},{11,1... | collective-permute-start | bytes 49160 | tf_op jit(solution)/shard_map/ppermute | solution.py:17
  36.8 4.3 %collective-permute-start.4 = (f32[64,64]{1,0:T(8,128)S(1)}, f32[64,64]{1,0:T(8,128)S(1)}, u32[]{:S(2)}, u32[]{:S(2)}) collective-permute-start(f32[64,64]{1,0:T(8,128)S(1)} %select_bitcast_fusion.7), channel_id=1, source_target_pairs={{28,0},{0,4},{4,8},{8,12},{12,16},{16,20},{20,24},{24,28},{29,1},{... | collective-permute-start | bytes 49160 | tf_op jit(solution)/shard_map/ppermute | solution.py:17
  51.2 1.8 %copy-start.3 = (f32[8,64,8]{1,2,0:T(8,128)S(1)}, f32[8,64,8]{1,2,0:T(8,128)}, u32[]{:S(2)}) copy-start(f32[8,64,8]{1,2,0:T(8,128)} %param.38) | copy-start | bytes 49156
  53.0 0.7 copy-start.8
  53.0 0.7 copy-start.11
  54.5 6.7 %collective-permute-start.10 = (f32[8,16]{1,0:T(8,128)S(1)}, f32[8,16]{1,0:T(8,128)S(1)}, u32[]{:S(2)}, u32[]{:S(2)}) collective-permute-start(f32[8,16]{1,0:T(8,128)S(1)} %select_bitcast_fusion.17), channel_id=1, source_target_pairs={{3,0},{0,1},{1,2},{2,3},{7,4},{4,5},{5,6},{6,7},{11,8},{8,9},{9,10... | collective-permute-start | bytes 1544 | tf_op jit(solution)/shard_map/ppermute | solution.py:17
  55.2 6.1 %collective-permute-start.11 = (f32[8,16]{1,0:T(8,128)S(1)}, f32[8,16]{1,0:T(8,128)S(1)}, u32[]{:S(2)}, u32[]{:S(2)}) collective-permute-start(f32[8,16]{1,0:T(8,128)S(1)} %select_bitcast_fusion.16), channel_id=1, source_target_pairs={{1,0},{2,1},{3,2},{0,3},{5,4},{6,5},{7,6},{4,7},{9,8},{10,9},{11,1... | collective-permute-start | bytes 1544 | tf_op jit(solution)/shard_map/ppermute | solution.py:17
  59.6 1.7 %collective-permute-start.9 = (f32[8,16]{1,0:T(8,128)S(1)}, f32[8,16]{1,0:T(8,128)S(1)}, u32[]{:S(2)}, u32[]{:S(2)}) collective-permute-start(f32[8,16]{1,0:T(8,128)S(1)} %select_bitcast_fusion.18), channel_id=1, source_target_pairs={{4,0},{8,4},{12,8},{16,12},{20,16},{24,20},{28,24},{0,28},{5,1},{9... | collective-permute-start | bytes 1544 | tf_op jit(solution)/shard_map/ppermute | solution.py:17
  60.5 0.7 copy-start.7
  60.5 3.9 %collective-permute-start.8 = (f32[8,16]{1,0:T(8,128)S(1)}, f32[8,16]{1,0:T(8,128)S(1)}, u32[]{:S(2)}, u32[]{:S(2)}) collective-permute-start(f32[8,16]{1,0:T(8,128)S(1)} %select_bitcast_fusion.19), channel_id=1, source_target_pairs={{28,0},{0,4},{4,8},{8,12},{12,16},{16,20},{20,24},{24,28},{29,1},{... | collective-permute-start | bytes 1544 | tf_op jit(solution)/shard_map/ppermute | solution.py:17
  67.6 0.7 copy-start.17
  72.4 4.2 %collective-permute-start.13 = (f32[8,16]{1,0:T(8,128)S(1)}, f32[8,16]{1,0:T(8,128)S(1)}, u32[]{:S(2)}, u32[]{:S(2)}) collective-permute-start(f32[8,16]{1,0:T(8,128)S(1)} %select_bitcast_fusion.14), channel_id=1, source_target_pairs={{4,0},{8,4},{12,8},{16,12},{20,16},{24,20},{28,24},{0,28},{5,1},{9... | collective-permute-start | bytes 1544 | tf_op jit(solution)/shard_map/ppermute | solution.py:17
  72.5 5.4 %collective-permute-start.14 = (f32[8,16]{1,0:T(8,128)S(1)}, f32[8,16]{1,0:T(8,128)S(1)}, u32[]{:S(2)}, u32[]{:S(2)}) collective-permute-start(f32[8,16]{1,0:T(8,128)S(1)} %select_bitcast_fusion.13), channel_id=1, source_target_pairs={{3,0},{0,1},{1,2},{2,3},{7,4},{4,5},{5,6},{6,7},{11,8},{8,9},{9,10... | collective-permute-start | bytes 1544 | tf_op jit(solution)/shard_map/ppermute | solution.py:17
  72.5 5.3 %collective-permute-start.15 = (f32[8,16]{1,0:T(8,128)S(1)}, f32[8,16]{1,0:T(8,128)S(1)}, u32[]{:S(2)}, u32[]{:S(2)}) collective-permute-start(f32[8,16]{1,0:T(8,128)S(1)} %select_bitcast_fusion.12), channel_id=1, source_target_pairs={{1,0},{2,1},{3,2},{0,3},{5,4},{6,5},{7,6},{4,7},{9,8},{10,9},{11,1... | collective-permute-start | bytes 1544 | tf_op jit(solution)/shard_map/ppermute | solution.py:17
  76.4 3.9 %collective-permute-start.12 = (f32[8,16]{1,0:T(8,128)S(1)}, f32[8,16]{1,0:T(8,128)S(1)}, u32[]{:S(2)}, u32[]{:S(2)}) collective-permute-start(f32[8,16]{1,0:T(8,128)S(1)} %select_bitcast_fusion.15), channel_id=1, source_target_pairs={{28,0},{0,4},{4,8},{8,12},{12,16},{16,20},{20,24},{24,28},{29,1},{... | collective-permute-start | bytes 1544 | tf_op jit(solution)/shard_map/ppermute | solution.py:17
  85.7 0.6 copy-start.6
  90.3 4.3 %collective-permute-start.17 = (f32[64,64]{1,0:T(8,128)S(1)}, f32[64,64]{1,0:T(8,128)S(1)}, u32[]{:S(2)}, u32[]{:S(2)}) collective-permute-start(f32[64,64]{1,0:T(8,128)S(1)} %select_bitcast_fusion.2), channel_id=1, source_target_pairs={{4,0},{8,4},{12,8},{16,12},{20,16},{24,20},{28,24},{0,28},{5,1},{9... | collective-permute-start | bytes 49160 | tf_op jit(solution)/shard_map/ppermute | solution.py:17
  90.5 6.0 %collective-permute-start.18 = (f32[64,64]{1,0:T(8,128)S(1)}, f32[64,64]{1,0:T(8,128)S(1)}, u32[]{:S(2)}, u32[]{:S(2)}) collective-permute-start(f32[64,64]{1,0:T(8,128)S(1)} %select_bitcast_fusion.1), channel_id=1, source_target_pairs={{3,0},{0,1},{1,2},{2,3},{7,4},{4,5},{5,6},{6,7},{11,8},{8,9},{9,10... | collective-permute-start | bytes 49160 | tf_op jit(solution)/shard_map/ppermute | solution.py:17
  90.6 5.8 %collective-permute-start.19 = (f32[64,64]{1,0:T(8,128)S(1)}, f32[64,64]{1,0:T(8,128)S(1)}, u32[]{:S(2)}, u32[]{:S(2)}) collective-permute-start(f32[64,64]{1,0:T(8,128)S(1)} %select_bitcast_fusion), channel_id=1, source_target_pairs={{1,0},{2,1},{3,2},{0,3},{5,4},{6,5},{7,6},{4,7},{9,8},{10,9},{11,1... | collective-permute-start | bytes 49160 | tf_op jit(solution)/shard_map/ppermute | solution.py:17
  94.6 4.3 %collective-permute-start.16 = (f32[64,64]{1,0:T(8,128)S(1)}, f32[64,64]{1,0:T(8,128)S(1)}, u32[]{:S(2)}, u32[]{:S(2)}) collective-permute-start(f32[64,64]{1,0:T(8,128)S(1)} %select_bitcast_fusion.3), channel_id=1, source_target_pairs={{28,0},{0,4},{4,8},{8,12},{12,16},{16,20},{20,24},{24,28},{29,1},{... | collective-permute-start | bytes 49160 | tf_op jit(solution)/shard_map/ppermute | solution.py:17
where the time goes:
time: 110 us
  local copies, waits for them, and re-layouts  49.4 us (45%)
  starting transfers between devices  25.3 us (23%)
  waiting for transfers between devices  15.8 us (14%)
  matrix products  15.5 us (14%)
  between operations  2.34 us (2%)
  other arithmetic  1.36 us (1%)
    gather x30, local copies, waits for them, and re-layouts, apply_operator(): gathered = jnp.take(extended, jnp.maximum(target, 0), axis=1)  25.8 us
    ppermute x20, starting transfers between devices, passed_along(): return lax.ppermute(block, axis, route)  25.3 us
    ppermute x20, waiting for transfers between devices, passed_along(): return lax.ppermute(block, axis, route)  15.8 us
    dot_general x40, matrix products, product(): jnp.dot(left, right, preferred_element_type=jnp.float32, precision=HIGH)  14.8 us
    gather x24, local copies, waits for them, and re-layouts, fine_ghosts(): packet = jnp.take(current, sends[direction], axis=1)  8.05 us
    unnamed x36, local copies, waits for them, and re-layouts  5.54 us
    gather x16, local copies, waits for them, and re-layouts, coarse_ghosts(): packet = jnp.take(current, sends[direction], axis=1)  5.07 us
  transfers between devices with their start and end apart: 20, of which 8 were waited for; matrix products, arithmetic and copies ran while one was open for 5% of the time, Pallas kernels for 0%

commit v1 on v0

v1 whole, which is shorter than its diff:
```python
import functools

import jax
import jax.numpy as jnp
from jax import lax
from jax.experimental import pallas as pl
from jax.experimental.pallas import tpu as pltpu
from jax.sharding import PartitionSpec as P

OMEGA = 0.7
COARSE_OMEGA = 0.6
HIGH = lax.Precision.HIGHEST
LANES = 128
SUB = 8
FACES = 6
SF_W, RF_W, SF_N, RF_N, AT_W, AT_N = range(6)


def dot(left, right):
    return jnp.dot(left, right, preferred_element_type=jnp.float32, precision=HIGH)


def dot_t(left, right):
    return lax.dot_general(
        left, right, (((1,), (1,)), ((), ())), preferred_element_type=jnp.float32, precision=HIGH
    )


def lane_take(tile, index):
    return jnp.take_along_axis(tile, index, axis=1, mode="promise_in_bounds")


def pick(tiles, index):
    low = index & (LANES - 1)
    high = index >> 7
    found = lane_take(tiles[0], low)
    for place in range(1, len(tiles)):
        found = jnp.where(high == place, lane_take(tiles[place], low), found)
    return found


def rows8(row):
    return jnp.broadcast_to(row, (SUB, row.shape[1]))


def by_flag(flag, one, other):
    return jnp.where(flag != 0, one, other)


def activity(counts_ref, elements):
    lane = lax.broadcasted_iota(jnp.int32, (1, elements), 1)
    return lane < counts_ref[0]


def ordered_sends(flags_ref, send):
    out = []
    for base, flag in ((0, SF_W), (2, SF_N)):
        first, second = send[base : base + 1], send[base + 1 : base + 2]
        out.append(by_flag(flags_ref[flag], second, first))
        out.append(by_flag(flags_ref[flag], first, second))
    return out


def store_packets(outs, halves, row):
    size = outs[0].shape[1]
    for half, tile in enumerate(halves):
        outs[2 * half][row : row + SUB, :] = tile[:, :size]
        outs[2 * half + 1][row : row + SUB, :] = tile[:, size : 2 * size]


def pack(flags_ref, send, source_ref, outs, rows, elements):
    order = ordered_sends(flags_ref, send)
    index = [rows8(jnp.concatenate(order[:2], axis=1)), rows8(jnp.concatenate(order[2:], axis=1))]
    for row in range(0, rows, SUB):
        tiles = [source_ref[row : row + SUB, c : c + LANES] for c in range(0, elements, LANES)]
        store_packets(outs, [pick(tiles, which) for which in index], row)
    return index


def received(flags_ref, packets, row):
    tiles = []
    for base, flag in ((0, RF_W), (2, RF_N)):
        first = packets[base][row : row + SUB, :]
        second = packets[base + 1][row : row + SUB, :]
        tiles.append(
            jnp.concatenate(
                [by_flag(flags_ref[flag], second, first), by_flag(flags_ref[flag], first, second)], axis=1
            )
        )
    return tiles


def start_kernel(flags_ref, counts_ref, start_ref, slot_ref, send_ref, csend_ref, masked_ref, *outs):
    rows, elements = start_ref.shape
    active = activity(counts_ref, elements)
    masked_ref[...] = jnp.where(active, start_ref[...], 0.0)
    index = pack(flags_ref, send_ref[...], masked_ref, outs, rows, elements)
    slots = rows8(jnp.where(active, slot_ref[...], -1).astype(jnp.float32))
    tiles = [slots[:, c : c + LANES] for c in range(0, elements, LANES)]
    csend = csend_ref[...].astype(jnp.float32)
    blank = jnp.zeros((1, LANES // 2 - csend.shape[1]), jnp.float32)
    order = ordered_sends(flags_ref, csend)
    line = lax.broadcasted_iota(jnp.int32, (SUB, LANES), 0)
    halves = []
    for half in range(2):
        coarse = jnp.concatenate([order[2 * half], blank, order[2 * half + 1], blank], axis=1)
        halves.append(jnp.where(line == 0, pick(tiles, index[half]), rows8(coarse)))
    store_packets(outs, halves, rows)


def local_blocks(current_ref, scale_ref, fscale_ref, nbr_ref, g_ref):
    rows, elements = current_ref.shape
    for c in range(0, elements, LANES):
        cols = slice(c, c + LANES)
        g_ref[0:rows, cols] = current_ref[:, cols] * scale_ref[:, cols]
    for face in range(FACES):
        for c in range(0, elements, LANES):
            cols = slice(c, c + LANES)
            entry = nbr_ref[face : face + 1, cols]
            here = (entry >= 0) & (entry < elements)
            weight = rows8(jnp.where(here, fscale_ref[face : face + 1, cols], 0.0))
            index = rows8(jnp.where(here, entry, 0))
            for row in range(0, rows, SUB):
                tiles = [current_ref[row : row + SUB, k : k + LANES] for k in range(0, elements, LANES)]
                at = rows * (face + 1) + row
                g_ref[at : at + SUB, cols] = weight * pick(tiles, index)


def ghost_blocks(flags_ref, packets, rows, elements, fscale_ref, nbr_ref, g_ref):
    halves = [received(flags_ref, packets, row) for row in range(0, rows, SUB)]
    for face in range(FACES):
        for c in range(0, elements, LANES):
            cols = slice(c, c + LANES)
            entry = nbr_ref[face : face + 1, cols]
            there = entry >= elements
            weight = rows8(jnp.where(there, fscale_ref[face : face + 1, cols], 0.0))
            index = rows8(jnp.where(there, entry - elements, 0))
            for row in range(0, rows, SUB):
                at = rows * face + row
                g_ref[at : at + SUB, cols] = weight * pick(halves[row // SUB], index)


def first_local_kernel(
    counts_ref,
    start_ref,
    right_ref,
    scale_ref,
    fscale_ref,
    nbr_ref,
    elem_ref,
    smooth_ref,
    faces_ref,
    prolong_ref,
    csmooth_ref,
    part_ref,
    folded_ref,
    lead_ref,
    relax_ref,
    source_ref,
    g_ref,
):
    rows, elements = start_ref.shape
    active = activity(counts_ref, elements)
    source_ref[...] = jnp.where(active, right_ref[...], 0.0)
    relax_ref[...] = jnp.where(active, OMEGA / scale_ref[...], 0.0)
    kids, _, cdof = prolong_ref.shape
    lead_ref[rows:, :] = smooth_ref[...]
    for kid in range(kids):
        lead_ref[kid * cdof : (kid + 1) * cdof, :] = dot_t(csmooth_ref[...], prolong_ref[kid])
    lead = lead_ref[...]
    folded_ref[:, 0:rows] = dot(lead, elem_ref[...])
    for face in range(FACES):
        folded_ref[:, rows * (face + 1) : rows * (face + 2)] = dot(lead, faces_ref[face])
    local_blocks(start_ref, scale_ref, fscale_ref, nbr_ref, g_ref)
    change = dot(smooth_ref[...], source_ref[...]) - dot(folded_ref[rows:, :], g_ref[...])
    part_ref[...] = start_ref[...] + relax_ref[...] * change


def smoothed_kernel(
    flags_ref, part_ref, relax_ref, folded_ref, fscale_ref, nbr_ref, send_ref, p0, p1, p2, p3, smoothed_ref, *rest
):
    outs, g_ref = rest[:4], rest[4]
    rows, elements = part_ref.shape
    ghost_blocks(flags_ref, (p0, p1, p2, p3), rows, elements, fscale_ref, nbr_ref, g_ref)
    smoothed_ref[...] = part_ref[...] - relax_ref[...] * dot(folded_ref[rows:, rows:], g_ref[...])
    pack(flags_ref, send_ref[...], smoothed_ref, outs, rows, elements)


def second_local_kernel(
    flags_ref,
    counts_ref,
    smoothed_ref,
    source_ref,
    scale_ref,
    fscale_ref,
    nbr_ref,
    lead_ref,
    folded_ref,
    prolong_ref,
    slot_ref,
    cscale_ref,
    cfscale_ref,
    cnbr_ref,
    p0,
    p1,
    p2,
    p3,
    value_ref,
    spread_ref,
    prol_ref,
    place_ref,
    child_ref,
    weight_ref,
    table_ref,
    g_ref,
    *,
    mesh_shape,
    sent,
):
    rows, elements = smoothed_ref.shape
    wides, narrows = mesh_shape
    kids, _, cdof = prolong_ref.shape
    coarse = cscale_ref.shape[1]
    local_blocks(smoothed_ref, scale_ref, fscale_ref, nbr_ref, g_ref)
    value_ref[...] = dot(lead_ref[...], source_ref[...]) - dot(folded_ref[...], g_ref[...])

    for kid in range(kids):
        prol_ref[:, kid * cdof : (kid + 1) * cdof] = prolong_ref[kid]
    prol = prol_ref[...]
    for block in range(FACES + 1):
        cols = slice(rows * block, rows * (block + 1))
        spread_ref[:, cols] = dot(folded_ref[rows:, cols], prol)

    active = activity(counts_ref, elements)
    own = jnp.where(active, slot_ref[...], -1)
    halves = received(flags_ref, (p0, p1, p2, p3), rows)
    tiles = [rows8(own[:, c : c + LANES].astype(jnp.float32)) for c in range(0, elements, LANES)]
    tiles += [rows8(half[0:1]) for half in halves]
    line = lax.broadcasted_iota(jnp.int32, (SUB, LANES), 0)
    blank = jnp.zeros((SUB - FACES, LANES), jnp.int32)
    side = halves[0].shape[1] // 2
    for c in range(0, elements, LANES):
        cols = slice(c, c + LANES)
        entry = jnp.concatenate([nbr_ref[:, cols], blank], axis=0)
        slot = pick(tiles, jnp.maximum(entry, 0)).astype(jnp.int32)
        slot = jnp.where(line == FACES, rows8(own[:, cols]), slot)
        live = (slot >= 0) & (entry >= 0)
        slot = jnp.where(live, slot, 0)
        group = jnp.where(entry >= elements, 1 + (entry - elements) // side, 0)
        place_ref[:, cols] = group * coarse + slot // kids
        child_ref[:, cols] = slot % kids
        weight = jnp.concatenate([fscale_ref[:, cols], scale_ref[:, cols], scale_ref[:, cols]], axis=0)
        weight_ref[:, cols] = jnp.where(live, weight, 0.0)

    wide, narrow = flags_ref[AT_W], flags_ref[AT_N]
    me = wide * narrows + narrow
    owners = (
        lax.rem(wide + wides - 1, wides) * narrows + narrow,
        lax.rem(wide + 1, wides) * narrows + narrow,
        wide * narrows + lax.rem(narrow + narrows - 1, narrows),
        wide * narrows + lax.rem(narrow + 1, narrows),
    )
    entry = jnp.concatenate([cnbr_ref[...], jnp.zeros((SUB - FACES, coarse), jnp.int32)], axis=0)
    remote = entry - coarse
    direction = remote // sent
    offset = jnp.maximum(remote - direction * sent, 0)
    wanted = jnp.clip(jnp.where(direction == 1, side, jnp.where(direction == 3, side, 0)) + offset, 0, LANES - 1)
    pad = jnp.zeros((SUB, LANES - coarse), jnp.int32)
    wanted = jnp.concatenate([wanted, pad], axis=1) if coarse < LANES else wanted
    lists = [rows8(half[1:2]) for half in halves]
    first = lane_take(lists[0], wanted)[:, :coarse].astype(jnp.int32)
    second = lane_take(lists[1], wanted)[:, :coarse].astype(jnp.int32)
    there = jnp.where(direction < 2, first, second)
    owner = jnp.where(
        direction == 0,
        owners[0],
        jnp.where(direction == 1, owners[1], jnp.where(direction == 2, owners[2], owners[3])),
    )
    target = jnp.where(entry < coarse, me * coarse + entry, owner * coarse + there)
    ones = jnp.zeros((SUB - FACES, coarse), jnp.float32)
    cweight = jnp.concatenate([cfscale_ref[...] * (COARSE_OMEGA / cscale_ref[...]), ones], axis=0)
    table_ref[0:SUB, :] = jnp.where(entry >= 0, target, 0).astype(jnp.float32)
    table_ref[SUB:, :] = jnp.where(entry >= 0, cweight, 0.0)


def restrict_kernel(
    flags_ref,
    value_ref,
    smoothed_ref,
    relax_ref,
    folded_ref,
    fscale_ref,
    nbr_ref,
    slot_ref,
    cscale_ref,
    table_ref,
    p0,
    p1,
    p2,
    p3,
    base_ref,
    message_ref,
    g_ref,
    *,
    kids,
):
    rows, elements = smoothed_ref.shape
    coarse = cscale_ref.shape[1]
    ghost_blocks(flags_ref, (p0, p1, p2, p3), rows, elements, fscale_ref, nbr_ref, g_ref)
    value = value_ref[...] - dot(folded_ref[:, rows:], g_ref[...])
    base_ref[...] = smoothed_ref[...] + relax_ref[...] * value[rows:, :]
    slot = slot_ref[...]
    child = rows8(slot % kids)
    step = rows // kids
    summed = jnp.where(child == 0, value[0:step, :], 0.0)
    for kid in range(1, kids):
        summed = jnp.where(child == kid, value[kid * step : (kid + 1) * step, :], summed)
    member = lax.broadcasted_iota(jnp.int32, (coarse, elements), 0) == slot // kids
    first = dot_t(summed, member.astype(jnp.float32)) * (COARSE_OMEGA / cscale_ref[...])
    upper = jnp.concatenate([first, table_ref[0:SUB, :]], axis=1)
    lower = jnp.concatenate([table_ref[SUB:, :], jnp.zeros_like(first)], axis=1)
    for device in range(message_ref.shape[0]):
        message_ref[device, 0:SUB, :] = upper
        message_ref[device, SUB:, :] = lower


def neighbourhood(mesh_shape, reach):
    wides, narrows = mesh_shape
    seen, found = set(), []
    near = [(0, 0), (-1, 0), (1, 0), (0, -1), (0, 1)]
    found.extend(near)
    seen.update((w % wides, n % narrows) for w, n in near)
    counts = [1, len(found)]
    for distance in range(2, reach + 1):
        for w in range(-distance, distance + 1):
            for n in {distance - abs(w), abs(w) - distance}:
                key = (w % wides, n % narrows)
                if key not in seen:
                    seen.add(key)
                    found.append((w, n))
        counts.append(len(found))
    return found, counts


def paired(pieces):
    if len(pieces) % 2:
        pieces = pieces + [pieces[0]]
    return [jnp.concatenate(pieces[i : i + 2], axis=1) for i in range(0, len(pieces), 2)]


def finish_kernel(
    flags_ref,
    message_ref,
    base_ref,
    relax_ref,
    prol_ref,
    spread_ref,
    place_ref,
    child_ref,
    weight_ref,
    cblock_ref,
    csmooth_ref,
    cfaces_ref,
    field_ref,
    correction_ref,
    folded_ref,
    cg_ref,
    g_ref,
    *,
    mesh_shape,
    kids,
):
    rows, elements = base_ref.shape
    cdof, coarse = correction_ref.shape
    wides, narrows = mesh_shape
    offsets, counts = neighbourhood(mesh_shape, 3)
    parts = []
    for w, n in offsets:
        at_w = lax.rem(flags_ref[AT_W] + (w % wides), wides)
        at_n = lax.rem(flags_ref[AT_N] + (n % narrows), narrows)
        parts.append(at_w * narrows + at_n)
    csmooth = csmooth_ref[...]
    own = COARSE_OMEGA * dot(csmooth, cblock_ref[...])
    for face in range(FACES):
        folded_ref[:, face * cdof : (face + 1) * cdof] = dot(csmooth, cfaces_ref[face])
    folded = folded_ref[...]

    blocks = wides * narrows
    lane = lax.broadcasted_iota(jnp.int32, (SUB, LANES), 1)
    ranks = []
    for base in range(0, blocks, LANES):
        rank = jnp.zeros((SUB, LANES), jnp.int32)
        for position, part in reversed(list(enumerate(parts))):
            rank = jnp.where(lane + base == part, position, rank)
        ranks.append(rank)

    uppers = [message_ref[part, 0:SUB, :] for part in parts]
    first = paired([upper[:, :coarse] for upper in uppers])
    current = first
    for sweep, count in ((1, counts[2]), (2, counts[1])):
        following = []
        targets = paired([uppers[i][:, coarse:] for i in range(count)])
        weights = paired([message_ref[parts[i], SUB:, :coarse] for i in range(count)])
        for t in range(len(targets)):
            target = targets[t].astype(jnp.int32)
            index = pick(ranks, target // coarse) * coarse + target % coarse
            for face in range(FACES):
                chosen = pick(current, rows8(index[face : face + 1]))
                cg_ref[face * cdof : (face + 1) * cdof, t * LANES : (t + 1) * LANES] = (
                    rows8(weights[t][face : face + 1]) * chosen
                )
        width = len(targets) * LANES
        pulled = dot(folded, cg_ref[:, :width])
        inner = dot(own, jnp.concatenate(current[: len(targets)], axis=1))
        for t in range(len(targets)):
            cols = slice(t * LANES, (t + 1) * LANES)
            following.append(current[t] + first[t] - inner[:, cols] - pulled[:, cols])
        current = following
    correction_ref[...] = current[0][:, :coarse]

    for c in range(0, elements, LANES):
        cols = slice(c, c + LANES)
        for row in range(FACES + 1):
            block = 0 if row == FACES else row + 1
            chosen = pick(current, rows8(place_ref[row : row + 1, cols]))
            child = rows8(child_ref[row : row + 1, cols])
            if row == FACES:
                live = rows8(jnp.where(weight_ref[row : row + 1, cols] > 0.0, 1.0, 0.0)) * chosen
                for kid in range(kids):
                    at = (FACES + 1) * rows + kid * cdof
                    g_ref[at : at + cdof, cols] = jnp.where(child == kid, live, 0.0)
            chosen = rows8(weight_ref[row : row + 1, cols]) * chosen
            for kid in range(kids):
                at = block * rows + kid * cdof
                g_ref[at : at + cdof, cols] = jnp.where(child == kid, chosen, 0.0)
    split = (FACES + 1) * rows
    change = dot(spread_ref[...], g_ref[0:split, :])
    delta = dot(prol_ref[...], g_ref[split:, :])
    field_ref[...] = base_ref[...] + delta - relax_ref[...] * change


def swap_routes(size):
    if size % 2:
        return [[(i, (i + 1) % size) for i in range(size)], [(i, (i - 1) % size) for i in range(size)]]
    return [
        [(i, i + 1 if i % 2 == 0 else i - 1) for i in range(size)],
        [(i, (i - 1 if i % 2 == 0 else i + 1) % size) for i in range(size)],
    ]


def exchange(packets):
    moved = []
    for base, axis in ((0, "wide"), (2, "narrow")):
        for half, route in enumerate(swap_routes(lax.axis_size(axis))):
            moved.append(lax.ppermute(packets[base + half], axis, route))
    return moved


def position_flags():
    flags = []
    for axis in ("wide", "narrow"):
        at = lax.axis_index(axis)
        if lax.axis_size(axis) % 2:
            flags += [jnp.int32(0), jnp.int32(0)]
        else:
            flags += [at % 2, 1 - at % 2]
    return jnp.stack(flags + [lax.axis_index("wide"), lax.axis_index("narrow")]).astype(jnp.int32)


SMEM = pl.BlockSpec(memory_space=pltpu.SMEM)
VMEM = pl.BlockSpec(memory_space=pltpu.VMEM)


def call(kernel, name, scalars, arrays, shapes, scratch=(), flops=0):
    outs = [jax.ShapeDtypeStruct(shape, dtype) for shape, dtype in shapes]
    moved = sum(x.size * 4 for x in arrays)
    return pl.pallas_call(
        kernel,
        name=name,
        out_shape=outs,
        in_specs=[SMEM] * len(scalars) + [VMEM] * len(arrays),
        out_specs=[VMEM] * len(outs),
        scratch_shapes=[pltpu.VMEM(shape, jnp.float32) for shape in scratch],
        cost_estimate=pl.CostEstimate(flops=flops, bytes_accessed=moved, transcendentals=0),
    )(*scalars, *arrays)


def body(
    start_field,
    right_side,
    element_scale,
    face_scale,
    face_nbr,
    send_list,
    counts,
    coarse_slot,
    elem_block,
    smooth_block,
    face_blocks,
    prolong,
    coarse_scale,
    coarse_face_scale,
    coarse_nbr,
    coarse_send,
    coarse_block,
    coarse_smooth,
    coarse_faces,
):
    rows, elements = start_field.shape
    kids, _, cdof = prolong.shape
    coarse = coarse_scale.shape[0]
    sent = send_list.shape[1]
    mesh_shape = (lax.axis_size("wide"), lax.axis_size("narrow"))
    devices = mesh_shape[0] * mesh_shape[1]
    f32, i32 = jnp.float32, jnp.int32
    scale = element_scale.reshape(1, elements)
    slot = coarse_slot.reshape(1, elements)
    cscale = coarse_scale.reshape(1, coarse)
    flags = position_flags()
    blocks = (FACES + 1) * rows

    start, *packets = call(
        start_kernel,
        "start",
        (flags, counts),
        (start_field, slot, send_list, coarse_send),
        [((rows, elements), f32)] + [((rows + SUB, sent), f32)] * 4,
    )
    first_ghosts = exchange(packets)
    part, folded, lead, relax, source = call(
        first_local_kernel,
        "first_local",
        (counts,),
        (
            start,
            right_side,
            scale,
            face_scale,
            face_nbr,
            elem_block,
            smooth_block,
            face_blocks,
            prolong,
            coarse_smooth,
        ),
        [
            ((rows, elements), f32),
            ((2 * rows, blocks), f32),
            ((2 * rows, rows), f32),
            ((1, elements), f32),
            ((rows, elements), f32),
        ],
        [(blocks, elements)],
        flops=2 * blocks * rows * elements,
    )
    smoothed, *packets = call(
        smoothed_kernel,
        "smoothed",
        (flags,),
        (part, relax, folded, face_scale, face_nbr, send_list, *first_ghosts),
        [((rows, elements), f32)] + [((rows, sent), f32)] * 4,
        [(blocks - rows, elements)],
        flops=2 * blocks * rows * elements,
    )
    second_ghosts = exchange(packets)
    value, spread, prol, place, child, weight, table = call(
        functools.partial(second_local_kernel, mesh_shape=mesh_shape, sent=coarse_send.shape[1]),
        "second_local",
        (flags, counts),
        (
            smoothed,
            source,
            scale,
            face_scale,
            face_nbr,
            lead,
            folded,
            prolong,
            slot,
            cscale,
            coarse_face_scale,
            coarse_nbr,
            *first_ghosts,
        ),
        [
            ((2 * rows, elements), f32),
            ((rows, blocks), f32),
            ((rows, kids * cdof), f32),
            ((SUB, elements), i32),
            ((SUB, elements), i32),
            ((SUB, elements), f32),
            ((2 * SUB, coarse), f32),
        ],
        [(blocks, elements)],
        flops=4 * blocks * rows * elements,
    )
    base, message = call(
        functools.partial(restrict_kernel, kids=kids),
        "restrict",
        (flags,),
        (value, smoothed, relax, folded, face_scale, face_nbr, slot, cscale, table, *second_ghosts),
        [((rows, elements), f32), ((devices, 2 * SUB, 2 * coarse), f32)],
        [(blocks - rows, elements)],
        flops=4 * blocks * rows * elements,
    )
    gathered = lax.all_to_all(message, ("wide", "narrow"), 0, 0)
    needed = -(-neighbourhood(mesh_shape, 3)[1][2] // 2) * 2 * coarse
    return tuple(
        call(
            functools.partial(finish_kernel, mesh_shape=mesh_shape, kids=kids),
            "finish",
            (flags,),
            (
                gathered,
                base,
                relax,
                prol,
                spread,
                place,
                child,
                weight,
                coarse_block,
                coarse_smooth,
                coarse_faces,
            ),
            [((rows, elements), f32), ((cdof, coarse), f32)],
            [(cdof, FACES * cdof), (FACES * cdof, needed), (blocks + rows, elements)],
            flops=2 * blocks * rows * elements,
        )
    )


def solution(mesh):
    both = ("wide", "narrow")
    return jax.shard_map(
        body,
        mesh=mesh,
        in_specs=(
            P(None, both),
            P(None, both),
            P(both),
            P(None, both),
            P(None, both),
            P(None, both),
            P(both),
            P(both),
            P(),
            P(),
            P(),
            P(),
            P(both),
            P(None, both),
            P(None, both),
            P(None, both),
            P(),
            P(),
            P(),
        ),
        out_specs=(P(None, both), P(None, both)),
        check_vma=False,
    )
```

time: 110 us -> 49.6 us (0.45)
  local copies, waits for them, and re-layouts: 49.4 us -> 2.6 us
  Pallas kernels: 0 us -> 20.2 us
  matrix products: 15.5 us -> 0 us
  starting transfers between devices: 25.3 us -> 10.3 us
  waiting for transfers between devices: 15.8 us -> 1.26 us
  blocking collectives: 0 us -> 13.5 us
  other arithmetic: 1.36 us -> 0 us
    gather x72 -> x0, local copies, waits for them, and re-layouts: 40.1 us -> none  [the longest x30 25.8 us: apply_operator(): gathered = jnp.take(extended, jnp.maximum(target, 0), axis=1)]
    pallas_call x0 -> x6, Pallas kernels: none -> 20.2 us  [call(): pl.pallas_call(kernel, name=name, out_shape=outs, in_specs=[SMEM] * len(s...]
    dot_general x42 -> x0, matrix products: 15.5 us -> none  [the longest x40 14.8 us: product(): jnp.dot(left, right, preferred_element_type=jnp.float32, precision=HIGH)]
    ppermute x20 -> x8, starting transfers between devices: 25.3 us -> 10.3 us  [exchange(): moved.append(lax.ppermute(packets[base + half], axis, route))]
    ppermute x20 -> x8, waiting for transfers between devices: 15.8 us -> 1.26 us  [exchange(): moved.append(lax.ppermute(packets[base + half], axis, route))]
    all_to_all x0 -> x1, blocking collectives: none -> 13.5 us  [body(): gathered = lax.all_to_all(message, ('wide', 'narrow'), 0, 0)]
    unnamed x36 -> x19, local copies, waits for them, and re-layouts: 5.54 us -> 2.03 us
    scatter x1 -> x0, local copies, waits for them, and re-layouts: 1.77 us -> none  [body(): jnp.zeros_like(fine_residual).at[:, coarse_slot].set(fine_residual)]
  transfers between devices with their start and end apart: 20 -> 8, of which waited for: 8 -> 1; matrix products, arithmetic and copies ran while one was open for 5% -> 2% of each run, Pallas kernels for 0% -> 15%
where the time goes in v1:
time: 49.6 us; the launch traced here: 49.3 us
  Pallas kernels  20.2 us (41%)
  blocking collectives  13.5 us (27%)
  starting transfers between devices  10.3 us (21%)
  local copies, waits for them, and re-layouts  2.6 us (5%)
  between operations  1.41 us (3%)
  waiting for transfers between devices  1.26 us (3%)
    pallas_call x6, Pallas kernels, call(): pl.pallas_call(kernel, name=name, out_shape=outs, in_specs=[SMEM] * len(s...  20.2 us
    all_to_all x1, blocking collectives, body(): gathered = lax.all_to_all(message, ('wide', 'narrow'), 0, 0)  13.5 us
    ppermute x8, starting transfers between devices, exchange(): moved.append(lax.ppermute(packets[base + half], axis, route))  10.3 us
    unnamed x19, local copies, waits for them, and re-layouts  2.03 us
    ppermute x8, waiting for transfers between devices, exchange(): moved.append(lax.ppermute(packets[base + half], axis, route))  1.26 us
  transfers between devices with their start and end apart: 8, of which 1 were waited for; matrix products, arithmetic and copies ran while one was open for 2% of the time, Pallas kernels for 15%

profile of v1, /device:TPU:0, one launch (start us, length us, event | category | flops | bytes accessed | tf_op | source)
XLA Modules:
  0.0 49.3 jit_solution(3333000940112228394)
XLA Ops:
  1.3 0.6 %stack.27.flags_ref = s32[6]{0:T(128)} concatenate(s32[1]{0:T(128)} %bitcast, s32[1]{0:T(128)} %bitcast.1, s32[1]{0:T(128)} %bitcast.2, s32[1]{0:T(128)} %bitcast.3, s32[1]{0:T(128)} %bitcast.4, s32[1]{0:T(128)} %bitcast.5), dimensions={0} | concatenate | bytes 48 | tf_op jit(solution)/shard_map/stack | solution.py:467
  1.9 0.0 copy-start.4
  1.9 1.9 %start.1 = (f32[64,512]{1,0:T(8,128)}, f32[72,64]{1,0:T(8,128)}, f32[72,64]{1,0:T(8,128)}, f32[72,64]{1,0:T(8,128)}, f32[72,64]{1,0:T(8,128)}) custom-call(s32[6]{0:T(128)} %stack.27.flags_ref, s32[1]{0:T(128)S(6)} %copy.23.counts_ref, f32[64,512]{1,0:T(8,128)} %start_ref.1, s32[1,512]{1,0:T(1,128)} %bitcast.9, s32[4,64]{1,0:T(4,128)} %send_ref.3, ...), custom_call_target="tpu_custom_call" | custom-call | bytes 134400 | tf_op jit(solution)/shard_map/start/pallas_call | solution.py:477
  3.8 0.5 %collective-permute-start = (f32[72,64]{1,0:T(8,128)}, f32[72,64]{1,0:T(8,128)S(1)}, u32[]{:S(2)}, u32[]{:S(2)}) collective-permute-start(f32[72,64]{1,0:T(8,128)} %get-tuple-element.30), channel_id=1, source_target_pairs={{0,4},{4,0},{8,12},{12,8},{16,20},{20,16},{24,28},{28,24},{1,5},{5... | collective-permute-start | bytes 55304 | tf_op jit(solution)/shard_map/ppermute | solution.py:455
  4.3 3.5 %collective-permute-start.1 = (f32[72,64]{1,0:T(8,128)}, f32[72,64]{1,0:T(8,128)S(1)}, u32[]{:S(2)}, u32[]{:S(2)}) collective-permute-start(f32[72,64]{1,0:T(8,128)} %get-tuple-element.31), channel_id=1, source_target_pairs={{0,28},{4,8},{8,4},{12,16},{16,12},{20,24},{24,20},{28,0},{1,29},{... | collective-permute-start | bytes 55304 | tf_op jit(solution)/shard_map/ppermute | solution.py:455
  7.8 1.6 %collective-permute-start.2 = (f32[72,64]{1,0:T(8,128)}, f32[72,64]{1,0:T(8,128)S(1)}, u32[]{:S(2)}, u32[]{:S(2)}) collective-permute-start(f32[72,64]{1,0:T(8,128)} %get-tuple-element.32), channel_id=1, source_target_pairs={{0,1},{1,0},{2,3},{3,2},{4,5},{5,4},{6,7},{7,6},{8,9},{9,8},{10,11... | collective-permute-start | bytes 55304 | tf_op jit(solution)/shard_map/ppermute | solution.py:455
  9.4 2.5 %collective-permute-start.3 = (f32[72,64]{1,0:T(8,128)}, f32[72,64]{1,0:T(8,128)S(1)}, u32[]{:S(2)}, u32[]{:S(2)}) collective-permute-start(f32[72,64]{1,0:T(8,128)} %get-tuple-element.33), channel_id=1, source_target_pairs={{0,3},{1,2},{2,1},{3,0},{4,7},{5,6},{6,5},{7,4},{8,11},{9,10},{10,... | collective-permute-start | bytes 55304 | tf_op jit(solution)/shard_map/ppermute | solution.py:455
  11.9 0.0 copy-done.4
  11.9 0.8 %copy.21.prolong_ref = f32[8,64,8]{2,1,0:T(8,128)} copy(f32[8,64,8]{1,2,0:T(8,128)S(1)} %copy-done.4) | data formatting | bytes 32768 | tf_op args[11]
  12.7 3.6 %first_local.1 = (f32[64,512]{1,0:T(8,128)}, f32[128,448]{1,0:T(8,128)}, f32[128,64]{1,0:T(8,128)}, f32[1,512]{1,0:T(1,128)}, f32[64,512]{1,0:T(8,128)}) custom-call(s32[1]{0:T(128)S(6)} %copy.23.counts_ref, f32[64,512]{1,0:T(8,128)} %get-tuple-element.26.start_ref, f32[64,512]{1,0:T(8,128)} %right_ref.1, f32[1,512]{1,0:T(1,128)} %bitcast.12, ...), custom_call_target="tpu_custom_call" | custom-call | flops 29360128 | bytes 436480 | tf_op jit(solution)/shard_map/first_local/pallas_call | solution.py:477
  16.3 0.0 collective-permute-done.p0
  16.3 0.0 copy-start
  16.3 0.0 collective-permute-done.1.p1
  16.4 0.0 copy-start.1
  16.4 0.0 collective-permute-done.2.p2
  16.4 0.0 copy-start.2
  16.4 0.0 collective-permute-done.3.p3
  16.4 0.0 copy-start.3
  16.4 0.5 %copy-done = f32[72,64]{1,0:T(8,128)} copy-done((f32[72,64]{1,0:T(8,128)}, f32[72,64]{1,0:T(8,128)S(1)}, u32[]{:S(2)}) %copy-start) | copy-done | bytes 18456
  16.9 0.0 copy-done.1
  17.0 0.0 copy-done.2
  17.0 0.0 copy-done.3
  17.0 3.0 %smoothed.1 = (f32[64,512]{1,0:T(8,128)}, f32[64,64]{1,0:T(8,128)}, f32[64,64]{1,0:T(8,128)}, f32[64,64]{1,0:T(8,128)}, f32[64,64]{1,0:T(8,128)}) custom-call(s32[6]{0:T(128)} %stack.27.flags_ref, f32[64,512]{1,0:T(8,128)} %get-tuple-element.27.part_ref, f32[1,512]{1,0:T(1,128)} %get-tuple-element.28.relax_ref, f32[128,448]{1,0:T(8,128)} %get-tuple-element.29.folded_ref, ...), custom_call_target="tpu_custom_call" | custom-call | flops 29360128 | bytes 461824 | tf_op jit(solution)/shard_map/smoothed/pallas_call | solution.py:477
  20.0 0.0 collective-permute-start.4
  20.0 0.6 %collective-permute-start.5 = (f32[64,64]{1,0:T(8,128)}, f32[64,64]{1,0:T(8,128)S(1)}, u32[]{:S(2)}, u32[]{:S(2)}) collective-permute-start(f32[64,64]{1,0:T(8,128)} %get-tuple-element.40), channel_id=1, source_target_pairs={{0,28},{4,8},{8,4},{12,16},{16,12},{20,24},{24,20},{28,0},{1,29},{... | collective-permute-start | bytes 49160 | tf_op jit(solution)/shard_map/ppermute | solution.py:455
  20.6 0.7 %collective-permute-start.6 = (f32[64,64]{1,0:T(8,128)}, f32[64,64]{1,0:T(8,128)S(1)}, u32[]{:S(2)}, u32[]{:S(2)}) collective-permute-start(f32[64,64]{1,0:T(8,128)} %get-tuple-element.41), channel_id=1, source_target_pairs={{0,1},{1,0},{2,3},{3,2},{4,5},{5,4},{6,7},{7,6},{8,9},{9,8},{10,11... | collective-permute-start | bytes 49160 | tf_op jit(solution)/shard_map/ppermute | solution.py:455
  21.3 0.9 %collective-permute-start.7 = (f32[64,64]{1,0:T(8,128)}, f32[64,64]{1,0:T(8,128)S(1)}, u32[]{:S(2)}, u32[]{:S(2)}) collective-permute-start(f32[64,64]{1,0:T(8,128)} %get-tuple-element.42), channel_id=1, source_target_pairs={{0,3},{1,2},{2,1},{3,0},{4,7},{5,6},{6,5},{7,4},{8,11},{9,10},{10,... | collective-permute-start | bytes 49160 | tf_op jit(solution)/shard_map/ppermute | solution.py:455
  22.2 3.7 %second_local.1 = (f32[128,512]{1,0:T(8,128)}, f32[64,448]{1,0:T(8,128)}, f32[64,64]{1,0:T(8,128)}, s32[8,512]{1,0:T(8,128)}, s32[8,512]{1,0:T(8,128)}, /*index=5*/f32[8,512]{1,0:T(8,128)}, f32[16,64]{1,0:T(8,128)}) custom-call(s32[6]{0:T(128)} %stack.27.flags_ref, s32[1]{0:T(128)S(6)} %copy.23.counts_ref, f32[64,512]{1,0:T(8,128)} %get-tuple-element.34.smoothed_ref, ...), custom_call_target="tpu_custom_call" | custom-call | flops 58720256 | bytes 646400 | tf_op jit(solution)/shard_map/second_local/pallas_call | solution.py:477
  25.9 0.0 collective-permute-done.4.p0
  25.9 0.0 copy-start.5
  25.9 0.0 collective-permute-done.5.p1
  25.9 0.0 copy-start.6
  25.9 0.0 collective-permute-done.6.p2
  26.0 0.0 copy-start.7
  26.0 1.2 %collective-permute-done.7.p3 = f32[64,64]{1,0:T(8,128)S(1)} collective-permute-done((f32[64,64]{1,0:T(8,128)}, f32[64,64]{1,0:T(8,128)S(1)}, u32[]{:S(2)}, u32[]{:S(2)}) %collective-permute-start.7) | collective-permute-done | bytes 16416 | tf_op jit(solution)/shard_map/ppermute | solution.py:455
  27.2 0.0 copy-start.8
  27.2 0.0 copy-done.5
  27.2 0.0 copy-done.6
  27.2 0.0 copy-done.7
  27.2 0.6 %copy-done.8 = f32[64,64]{1,0:T(8,128)} copy-done((f32[64,64]{1,0:T(8,128)}, f32[64,64]{1,0:T(8,128)S(1)}, u32[]{:S(2)}) %copy-start.8) | copy-done | bytes 16408
  27.8 3.3 %restrict.1 = (f32[64,512]{1,0:T(8,128)}, f32[32,16,128]{2,1,0:T(8,128)}) custom-call(s32[6]{0:T(128)} %stack.27.flags_ref, f32[128,512]{1,0:T(8,128)} %get-tuple-element.37.value_ref, f32[64,512]{1,0:T(8,128)} %get-tuple-element.34.smoothed_ref, f32[1,512]{1,0:T(1,128)} %get-tuple-element.28.relax_ref, f32[128,448]{1,0:T(8,128)} %get-tuple-element.29.folded_ref, ...), custom_call_target="tpu_custom_call" | custom-call | flops 58720256 | bytes 721152 | tf_op jit(solution)/shard_map/restrict/pallas_call | solution.py:477
  31.1 13.5 %all_to_all.5.message_ref = f32[32,16,128]{2,1,0:T(8,128)} all-to-all(f32[32,16,128]{2,1,0:T(8,128)} %get-tuple-element.43), channel_id=1, replica_groups=mesh['wide'=8,'narrow'=4] {'wide','narrow'}, dimensions={0} | all-to-all | bytes 524288 | tf_op jit(solution)/shard_map/all_to_all | solution.py:606
  44.7 4.6 %finish.1 = (f32[64,512]{1,0:T(8,128)}, f32[8,64]{1,0:T(8,128)}) custom-call(s32[6]{0:T(128)} %stack.27.flags_ref, f32[32,16,128]{2,1,0:T(8,128)} %all_to_all.5.message_ref, f32[64,512]{1,0:T(8,128)} %get-tuple-element.44.base_ref, f32[1,512]{1,0:T(1,128)} %get-tuple-element.28.relax_ref, f32[64,64]{1,0:T(8,128)} %get-tuple-element.45.prol_ref, ...), custom_call_target="tpu_custom_call" | custom-call | flops 29360128 | bytes 577536 | tf_op jit(solution)/shard_map/finish/pallas_call | solution.py:477
Async XLA Ops:
  1.9 10.0 %copy-start.4 = (f32[8,64,8]{1,2,0:T(8,128)S(1)}, f32[8,64,8]{1,2,0:T(8,128)}, u32[]{:S(2)}) copy-start(f32[8,64,8]{1,2,0:T(8,128)} %param.30) | copy-start | bytes 49156
  3.8 12.6 %collective-permute-start = (f32[72,64]{1,0:T(8,128)}, f32[72,64]{1,0:T(8,128)S(1)}, u32[]{:S(2)}, u32[]{:S(2)}) collective-permute-start(f32[72,64]{1,0:T(8,128)} %get-tuple-element.30), channel_id=1, source_target_pairs={{0,4},{4,0},{8,12},{12,8},{16,20},{20,16},{24,28},{28,24},{1,5},{5... | collective-permute-start | bytes 55304 | tf_op jit(solution)/shard_map/ppermute | solution.py:455
  4.3 12.1 %collective-permute-start.1 = (f32[72,64]{1,0:T(8,128)}, f32[72,64]{1,0:T(8,128)S(1)}, u32[]{:S(2)}, u32[]{:S(2)}) collective-permute-start(f32[72,64]{1,0:T(8,128)} %get-tuple-element.31), channel_id=1, source_target_pairs={{0,28},{4,8},{8,4},{12,16},{16,12},{20,24},{24,20},{28,0},{1,29},{... | collective-permute-start | bytes 55304 | tf_op jit(solution)/shard_map/ppermute | solution.py:455
  7.8 8.6 %collective-permute-start.2 = (f32[72,64]{1,0:T(8,128)}, f32[72,64]{1,0:T(8,128)S(1)}, u32[]{:S(2)}, u32[]{:S(2)}) collective-permute-start(f32[72,64]{1,0:T(8,128)} %get-tuple-element.32), channel_id=1, source_target_pairs={{0,1},{1,0},{2,3},{3,2},{4,5},{5,4},{6,7},{7,6},{8,9},{9,8},{10,11... | collective-permute-start | bytes 55304 | tf_op jit(solution)/shard_map/ppermute | solution.py:455
  9.4 7.0 %collective-permute-start.3 = (f32[72,64]{1,0:T(8,128)}, f32[72,64]{1,0:T(8,128)S(1)}, u32[]{:S(2)}, u32[]{:S(2)}) collective-permute-start(f32[72,64]{1,0:T(8,128)} %get-tuple-element.33), channel_id=1, source_target_pairs={{0,3},{1,2},{2,1},{3,0},{4,7},{5,6},{6,5},{7,4},{8,11},{9,10},{10,... | collective-permute-start | bytes 55304 | tf_op jit(solution)/shard_map/ppermute | solution.py:455
  16.3 0.6 %copy-start = (f32[72,64]{1,0:T(8,128)}, f32[72,64]{1,0:T(8,128)S(1)}, u32[]{:S(2)}) copy-start(f32[72,64]{1,0:T(8,128)S(1)} %collective-permute-done.p0) | copy-start | bytes 55300
  16.4 0.6 %copy-start.1 = (f32[72,64]{1,0:T(8,128)}, f32[72,64]{1,0:T(8,128)S(1)}, u32[]{:S(2)}) copy-start(f32[72,64]{1,0:T(8,128)S(1)} %collective-permute-done.1.p1) | copy-start | bytes 55300
  16.4 0.6 %copy-start.2 = (f32[72,64]{1,0:T(8,128)}, f32[72,64]{1,0:T(8,128)S(1)}, u32[]{:S(2)}) copy-start(f32[72,64]{1,0:T(8,128)S(1)} %collective-permute-done.2.p2) | copy-start | bytes 55300
  16.4 0.6 %copy-start.3 = (f32[72,64]{1,0:T(8,128)}, f32[72,64]{1,0:T(8,128)S(1)}, u32[]{:S(2)}) copy-start(f32[72,64]{1,0:T(8,128)S(1)} %collective-permute-done.3.p3) | copy-start | bytes 55300
  20.0 6.0 %collective-permute-start.4 = (f32[64,64]{1,0:T(8,128)}, f32[64,64]{1,0:T(8,128)S(1)}, u32[]{:S(2)}, u32[]{:S(2)}) collective-permute-start(f32[64,64]{1,0:T(8,128)} %get-tuple-element.39), channel_id=1, source_target_pairs={{0,4},{4,0},{8,12},{12,8},{16,20},{20,16},{24,28},{28,24},{1,5},{5... | collective-permute-start | bytes 49160 | tf_op jit(solution)/shard_map/ppermute | solution.py:455
  20.0 6.0 %collective-permute-start.5 = (f32[64,64]{1,0:T(8,128)}, f32[64,64]{1,0:T(8,128)S(1)}, u32[]{:S(2)}, u32[]{:S(2)}) collective-permute-start(f32[64,64]{1,0:T(8,128)} %get-tuple-element.40), channel_id=1, source_target_pairs={{0,28},{4,8},{8,4},{12,16},{16,12},{20,24},{24,20},{28,0},{1,29},{... | collective-permute-start | bytes 49160 | tf_op jit(solution)/shard_map/ppermute | solution.py:455
  20.6 5.3 %collective-permute-start.6 = (f32[64,64]{1,0:T(8,128)}, f32[64,64]{1,0:T(8,128)S(1)}, u32[]{:S(2)}, u32[]{:S(2)}) collective-permute-start(f32[64,64]{1,0:T(8,128)} %get-tuple-element.41), channel_id=1, source_target_pairs={{0,1},{1,0},{2,3},{3,2},{4,5},{5,4},{6,7},{7,6},{8,9},{9,8},{10,11... | collective-permute-start | bytes 49160 | tf_op jit(solution)/shard_map/ppermute | solution.py:455
  21.3 5.9 %collective-permute-start.7 = (f32[64,64]{1,0:T(8,128)}, f32[64,64]{1,0:T(8,128)S(1)}, u32[]{:S(2)}, u32[]{:S(2)}) collective-permute-start(f32[64,64]{1,0:T(8,128)} %get-tuple-element.42), channel_id=1, source_target_pairs={{0,3},{1,2},{2,1},{3,0},{4,7},{5,6},{6,5},{7,4},{8,11},{9,10},{10,... | collective-permute-start | bytes 49160 | tf_op jit(solution)/shard_map/ppermute | solution.py:455
  25.9 1.3 %copy-start.5 = (f32[64,64]{1,0:T(8,128)}, f32[64,64]{1,0:T(8,128)S(1)}, u32[]{:S(2)}) copy-start(f32[64,64]{1,0:T(8,128)S(1)} %collective-permute-done.4.p0) | copy-start | bytes 49156
  25.9 1.3 %copy-start.6 = (f32[64,64]{1,0:T(8,128)}, f32[64,64]{1,0:T(8,128)S(1)}, u32[]{:S(2)}) copy-start(f32[64,64]{1,0:T(8,128)S(1)} %collective-permute-done.5.p1) | copy-start | bytes 49156
  26.0 1.3 %copy-start.7 = (f32[64,64]{1,0:T(8,128)}, f32[64,64]{1,0:T(8,128)S(1)}, u32[]{:S(2)}) copy-start(f32[64,64]{1,0:T(8,128)S(1)} %collective-permute-done.6.p2) | copy-start | bytes 49156
  27.2 0.6 %copy-start.8 = (f32[64,64]{1,0:T(8,128)}, f32[64,64]{1,0:T(8,128)S(1)}, u32[]{:S(2)}) copy-start(f32[64,64]{1,0:T(8,128)S(1)} %collective-permute-done.7.p3) | copy-start | bytes 49156

commit v2 on v1

--- a/solution.py
+++ b/solution.py
@@ -13,7 +13,7 @@
 LANES = 128
 SUB = 8
 FACES = 6
-SF_W, RF_W, SF_N, RF_N, AT_W, AT_N = range(6)
+GRANT = 16 * 1024 * 1024
 
 
 def dot(left, right):
@@ -43,8 +43,11 @@
     return jnp.broadcast_to(row, (SUB, row.shape[1]))
 
 
-def by_flag(flag, one, other):
-    return jnp.where(flag != 0, one, other)
+def swapped(axis, one, other):
+    if lax.axis_size(axis) % 2:
+        return one, other
+    odd = lax.rem(lax.axis_index(axis), 2) != 0
+    return jnp.where(odd, other, one), jnp.where(odd, one, other)
 
 
 def activity(counts_ref, elements):
@@ -52,12 +55,10 @@
     return lane < counts_ref[0]
 
 
-def ordered_sends(flags_ref, send):
+def ordered_sends(send):
     out = []
-    for base, flag in ((0, SF_W), (2, SF_N)):
-        first, second = send[base : base + 1], send[base + 1 : base + 2]
-        out.append(by_flag(flags_ref[flag], second, first))
-        out.append(by_flag(flags_ref[flag], first, second))
+    for base, axis in ((0, "wide"), (2, "narrow")):
+        out.extend(swapped(axis, send[base : base + 1], send[base + 1 : base + 2]))
     return out
 
 
@@ -68,8 +69,8 @@
         outs[2 * half + 1][row : row + SUB, :] = tile[:, size : 2 * size]
 
 
-def pack(flags_ref, send, source_ref, outs, rows, elements):
-    order = ordered_sends(flags_ref, send)
+def pack(send, source_ref, outs, rows, elements):
+    order = ordered_sends(send)
     index = [rows8(jnp.concatenate(order[:2], axis=1)), rows8(jnp.concatenate(order[2:], axis=1))]
     for row in range(0, rows, SUB):
         tiles = [source_ref[row : row + SUB, c : c + LANES] for c in range(0, elements, LANES)]
@@ -77,35 +78,45 @@
     return index
 
 
-def received(flags_ref, packets, row):
+def received(packets, row):
     tiles = []
-    for base, flag in ((0, RF_W), (2, RF_N)):
+    for base, axis in ((0, "wide"), (2, "narrow")):
         first = packets[base][row : row + SUB, :]
         second = packets[base + 1][row : row + SUB, :]
-        tiles.append(
-            jnp.concatenate(
-                [by_flag(flags_ref[flag], second, first), by_flag(flags_ref[flag], first, second)], axis=1
-            )
-        )
+        if lax.axis_size(axis) % 2 == 0:
+            first, second = swapped(axis, second, first)
+        tiles.append(jnp.concatenate([first, second], axis=1))
     return tiles
 
 
-def start_kernel(flags_ref, counts_ref, start_ref, slot_ref, send_ref, csend_ref, masked_ref, *outs):
+def start_kernel(counts_ref, *refs, carried):
+    given, refs = refs[: carried + 3], refs[carried + 3 :]
+    masked_ref, outs, kept = refs[0], refs[1:5], refs[5 : 5 + carried]
+    start_ref, send_ref, csend_ref, sems = refs[5 + carried :]
+    slot_ref = kept[0]
+    held = (start_ref, send_ref, csend_ref, *kept)
+    copies = [pltpu.make_async_copy(here, there, sems.at[i]) for i, (here, there) in enumerate(zip(given, held))]
+    for copy in copies:
+        copy.start()
+    for copy in copies[:4]:
+        copy.wait()
     rows, elements = start_ref.shape
     active = activity(counts_ref, elements)
     masked_ref[...] = jnp.where(active, start_ref[...], 0.0)
-    index = pack(flags_ref, send_ref[...], masked_ref, outs, rows, elements)
+    index = pack(send_ref[...], masked_ref, outs, rows, elements)
     slots = rows8(jnp.where(active, slot_ref[...], -1).astype(jnp.float32))
     tiles = [slots[:, c : c + LANES] for c in range(0, elements, LANES)]
     csend = csend_ref[...].astype(jnp.float32)
     blank = jnp.zeros((1, LANES // 2 - csend.shape[1]), jnp.float32)
-    order = ordered_sends(flags_ref, csend)
+    order = ordered_sends(csend)
     line = lax.broadcasted_iota(jnp.int32, (SUB, LANES), 0)
     halves = []
     for half in range(2):
         coarse = jnp.concatenate([order[2 * half], blank, order[2 * half + 1], blank], axis=1)
         halves.append(jnp.where(line == 0, pick(tiles, index[half]), rows8(coarse)))
     store_packets(outs, halves, rows)
+    for copy in copies[4:]:
+        copy.wait()
 
 
 def local_blocks(current_ref, scale_ref, fscale_ref, nbr_ref, g_ref):
@@ -126,8 +137,8 @@
                 g_ref[at : at + SUB, cols] = weight * pick(tiles, index)
 
 
-def ghost_blocks(flags_ref, packets, rows, elements, fscale_ref, nbr_ref, g_ref):
-    halves = [received(flags_ref, packets, row) for row in range(0, rows, SUB)]
+def ghost_blocks(packets, rows, elements, fscale_ref, nbr_ref, g_ref):
+    halves = [received(packets, row) for row in range(0, rows, SUB)]
     for face in range(FACES):
         for c in range(0, elements, LANES):
             cols = slice(c, c + LANES)
@@ -163,10 +174,10 @@
     active = activity(counts_ref, elements)
     source_ref[...] = jnp.where(active, right_ref[...], 0.0)
     relax_ref[...] = jnp.where(active, OMEGA / scale_ref[...], 0.0)
-    kids, _, cdof = prolong_ref.shape
+    cdof = csmooth_ref.shape[0]
     lead_ref[rows:, :] = smooth_ref[...]
-    for kid in range(kids):
-        lead_ref[kid * cdof : (kid + 1) * cdof, :] = dot_t(csmooth_ref[...], prolong_ref[kid])
+    for at in range(0, prolong_ref.shape[0], cdof):
+        lead_ref[at : at + cdof, :] = dot(csmooth_ref[...], prolong_ref[at : at + cdof, :])
     lead = lead_ref[...]
     folded_ref[:, 0:rows] = dot(lead, elem_ref[...])
     for face in range(FACES):
@@ -177,17 +188,16 @@
 
 
 def smoothed_kernel(
-    flags_ref, part_ref, relax_ref, folded_ref, fscale_ref, nbr_ref, send_ref, p0, p1, p2, p3, smoothed_ref, *rest
+    part_ref, relax_ref, folded_ref, fscale_ref, nbr_ref, send_ref, p0, p1, p2, p3, smoothed_ref, *rest
 ):
     outs, g_ref = rest[:4], rest[4]
     rows, elements = part_ref.shape
-    ghost_blocks(flags_ref, (p0, p1, p2, p3), rows, elements, fscale_ref, nbr_ref, g_ref)
+    ghost_blocks((p0, p1, p2, p3), rows, elements, fscale_ref, nbr_ref, g_ref)
     smoothed_ref[...] = part_ref[...] - relax_ref[...] * dot(folded_ref[rows:, rows:], g_ref[...])
-    pack(flags_ref, send_ref[...], smoothed_ref, outs, rows, elements)
+    pack(send_ref[...], smoothed_ref, outs, rows, elements)
 
 
 def second_local_kernel(
-    flags_ref,
     counts_ref,
     smoothed_ref,
     source_ref,
@@ -216,16 +226,15 @@
     *,
     mesh_shape,
     sent,
+    kids,
 ):
     rows, elements = smoothed_ref.shape
     wides, narrows = mesh_shape
-    kids, _, cdof = prolong_ref.shape
     coarse = cscale_ref.shape[1]
     local_blocks(smoothed_ref, scale_ref, fscale_ref, nbr_ref, g_ref)
     value_ref[...] = dot(lead_ref[...], source_ref[...]) - dot(folded_ref[...], g_ref[...])
 
-    for kid in range(kids):
-        prol_ref[:, kid * cdof : (kid + 1) * cdof] = prolong_ref[kid]
+    prol_ref[...] = prolong_ref[...].T
     prol = prol_ref[...]
     for block in range(FACES + 1):
         cols = slice(rows * block, rows * (block + 1))
@@ -233,7 +242,7 @@
 
     active = activity(counts_ref, elements)
     own = jnp.where(active, slot_ref[...], -1)
-    halves = received(flags_ref, (p0, p1, p2, p3), rows)
+    halves = received((p0, p1, p2, p3), rows)
     tiles = [rows8(own[:, c : c + LANES].astype(jnp.float32)) for c in range(0, elements, LANES)]
     tiles += [rows8(half[0:1]) for half in halves]
     line = lax.broadcasted_iota(jnp.int32, (SUB, LANES), 0)
@@ -252,7 +261,7 @@
         weight = jnp.concatenate([fscale_ref[:, cols], scale_ref[:, cols], scale_ref[:, cols]], axis=0)
         weight_ref[:, cols] = jnp.where(live, weight, 0.0)
 
-    wide, narrow = flags_ref[AT_W], flags_ref[AT_N]
+    wide, narrow = lax.axis_index("wide"), lax.axis_index("narrow")
     me = wide * narrows + narrow
     owners = (
         lax.rem(wide + wides - 1, wides) * narrows + narrow,
@@ -284,7 +293,6 @@
 
 
 def restrict_kernel(
-    flags_ref,
     value_ref,
     smoothed_ref,
     relax_ref,
@@ -306,7 +314,7 @@
 ):
     rows, elements = smoothed_ref.shape
     coarse = cscale_ref.shape[1]
-    ghost_blocks(flags_ref, (p0, p1, p2, p3), rows, elements, fscale_ref, nbr_ref, g_ref)
+    ghost_blocks((p0, p1, p2, p3), rows, elements, fscale_ref, nbr_ref, g_ref)
     value = value_ref[...] - dot(folded_ref[:, rows:], g_ref[...])
     base_ref[...] = smoothed_ref[...] + relax_ref[...] * value[rows:, :]
     slot = slot_ref[...]
@@ -349,7 +357,6 @@
 
 
 def finish_kernel(
-    flags_ref,
     message_ref,
     base_ref,
     relax_ref,
@@ -376,8 +383,8 @@
     offsets, counts = neighbourhood(mesh_shape, 3)
     parts = []
     for w, n in offsets:
-        at_w = lax.rem(flags_ref[AT_W] + (w % wides), wides)
-        at_n = lax.rem(flags_ref[AT_N] + (n % narrows), narrows)
+        at_w = lax.rem(lax.axis_index("wide") + (w % wides), wides)
+        at_n = lax.rem(lax.axis_index("narrow") + (n % narrows), narrows)
         parts.append(at_w * narrows + at_n)
     csmooth = csmooth_ref[...]
     own = COARSE_OMEGA * dot(csmooth, cblock_ref[...])
@@ -456,31 +463,24 @@
     return moved
 
 
-def position_flags():
-    flags = []
-    for axis in ("wide", "narrow"):
-        at = lax.axis_index(axis)
-        if lax.axis_size(axis) % 2:
-            flags += [jnp.int32(0), jnp.int32(0)]
-        else:
-            flags += [at % 2, 1 - at % 2]
-    return jnp.stack(flags + [lax.axis_index("wide"), lax.axis_index("narrow")]).astype(jnp.int32)
-
-
 SMEM = pl.BlockSpec(memory_space=pltpu.SMEM)
 VMEM = pl.BlockSpec(memory_space=pltpu.VMEM)
-
-
-def call(kernel, name, scalars, arrays, shapes, scratch=(), flops=0):
+HBM = pl.BlockSpec(memory_space=pltpu.HBM)
+
+
+def call(kernel, name, scalars, arrays, shapes, scratch=(), flops=0, space=VMEM):
     outs = [jax.ShapeDtypeStruct(shape, dtype) for shape, dtype in shapes]
+    if space is HBM:
+        arrays = [pltpu.with_memory_space_constraint(x, pltpu.HBM) for x in arrays]
     moved = sum(x.size * 4 for x in arrays)
     return pl.pallas_call(
         kernel,
         name=name,
         out_shape=outs,
-        in_specs=[SMEM] * len(scalars) + [VMEM] * len(arrays),
+        in_specs=[SMEM] * len(scalars) + [space] * len(arrays),
         out_specs=[VMEM] * len(outs),
-        scratch_shapes=[pltpu.VMEM(shape, jnp.float32) for shape in scratch],
+        scratch_shapes=[pltpu.VMEM(x, jnp.float32) if isinstance(x, tuple) else x for x in scratch],
+        compiler_params=pltpu.CompilerParams(vmem_limit_bytes=GRANT),
         cost_estimate=pl.CostEstimate(flops=flops, bytes_accessed=moved, transcendentals=0),
     )(*scalars, *arrays)
 
@@ -508,6 +508,7 @@
 ):
     rows, elements = start_field.shape
     kids, _, cdof = prolong.shape
+    prolong = prolong.transpose(0, 2, 1).reshape(kids * cdof, rows)
     coarse = coarse_scale.shape[0]
     sent = send_list.shape[1]
     mesh_shape = (lax.axis_size("wide"), lax.axis_size("narrow"))
@@ -516,16 +517,59 @@
     scale = element_scale.reshape(1, elements)
     slot = coarse_slot.reshape(1, elements)
     cscale = coarse_scale.reshape(1, coarse)
-    flags = position_flags()
     blocks = (FACES + 1) * rows
 
-    start, *packets = call(
-        start_kernel,
+    kept = (
+        slot,
+        right_side,
+        scale,
+        face_scale,
+        face_nbr,
+        elem_block,
+        smooth_block,
+        face_blocks,
+        prolong,
+        cscale,
+        coarse_face_scale,
+        coarse_nbr,
+        coarse_block,
+        coarse_smooth,
+        coarse_faces,
+        send_list,
+    )
+    start, *brought = call(
+        functools.partial(start_kernel, carried=len(kept)),
         "start",
-        (flags, counts),
-        (start_field, slot, send_list, coarse_send),
-        [((rows, elements), f32)] + [((rows + SUB, sent), f32)] * 4,
-    )
+        (counts,),
+        (start_field, send_list, coarse_send, *kept),
+        [((rows, elements), f32)] + [((rows + SUB, sent), f32)] * 4 + [(x.shape, x.dtype) for x in kept],
+        [
+            pltpu.VMEM(start_field.shape, f32),
+            pltpu.VMEM(send_list.shape, i32),
+            pltpu.VMEM(coarse_send.shape, i32),
+            pltpu.SemaphoreType.DMA((len(kept) + 3,)),
+        ],
+        space=HBM,
+    )
+    packets = brought[:4]
+    (
+        slot,
+        right_side,
+        scale,
+        face_scale,
+        face_nbr,
+        elem_block,
+        smooth_block,
+        face_blocks,
+        prolong,
+        cscale,
+        coarse_face_scale,
+        coarse_nbr,
+        coarse_block,
+        coarse_smooth,
+        coarse_faces,
+        send_list,
+    ) = brought[4:]
     first_ghosts = exchange(packets)
     part, folded, lead, relax, source = call(
         first_local_kernel,
@@ -556,7 +600,7 @@
     smoothed, *packets = call(
         smoothed_kernel,
         "smoothed",
-        (flags,),
+        (),
         (part, relax, folded, face_scale, face_nbr, send_list, *first_ghosts),
         [((rows, elements), f32)] + [((rows, sent), f32)] * 4,
         [(blocks - rows, elements)],
@@ -564,9 +608,9 @@
     )
     second_ghosts = exchange(packets)
     value, spread, prol, place, child, weight, table = call(
-        functools.partial(second_local_kernel, mesh_shape=mesh_shape, sent=coarse_send.shape[1]),
+        functools.partial(second_local_kernel, mesh_shape=mesh_shape, sent=coarse_send.shape[1], kids=kids),
         "second_local",
-        (flags, counts),
+        (counts,),
         (
             smoothed,
             source,
@@ -597,7 +641,7 @@
     base, message = call(
         functools.partial(restrict_kernel, kids=kids),
         "restrict",
-        (flags,),
+        (),
         (value, smoothed, relax, folded, face_scale, face_nbr, slot, cscale, table, *second_ghosts),
         [((rows, elements), f32), ((devices, 2 * SUB, 2 * coarse), f32)],
         [(blocks - rows, elements)],
@@ -609,7 +653,7 @@
         call(
             functools.partial(finish_kernel, mesh_shape=mesh_shape, kids=kids),
             "finish",
-            (flags,),
+            (),
             (
                 gathered,
                 base,

time: 49.6 us -> 41.1 us (0.83)
  Pallas kernels: 20.2 us -> 11.1 us
  local copies, waits for them, and re-layouts: 2.6 us -> 0 us
  waiting for transfers between devices: 1.26 us -> 3.03 us
  starting transfers between devices: 10.3 us -> 11.3 us
  blocking collectives: 13.5 us -> 14.1 us
    pallas_call x6, Pallas kernels: 20.2 us -> 11.1 us  [call(): pl.pallas_call(kernel, name=name, out_shape=outs, in_specs=[SMEM] * len(s...]
    unnamed x19 -> x0, local copies, waits for them, and re-layouts: 2.03 us -> none
    ppermute x8, waiting for transfers between devices: 1.26 us -> 3.03 us  [exchange(): moved.append(lax.ppermute(packets[base + half], axis, route))]
    ppermute x8, starting transfers between devices: 10.3 us -> 11.3 us  [exchange(): moved.append(lax.ppermute(packets[base + half], axis, route))]
    all_to_all x1, blocking collectives: 13.5 us -> 14.1 us  [body(): gathered = lax.all_to_all(message, ('wide', 'narrow'), 0, 0)]
    another operation x1 -> x0, local copies, waits for them, and re-layouts: 0.57 us -> none  [position_flags(): jnp.stack(flags + [lax.axis_index('wide'), lax.axis_index('narrow')])]
  transfers between devices with their start and end apart: 8 -> 8, of which waited for: 1 -> 2; matrix products, arithmetic and copies ran while one was open for 2% -> 0% of each run, Pallas kernels for 15% -> 8%
where the time goes in v2:
time: 41.1 us; the launch traced here: 40.9 us
  blocking collectives  14.1 us (34%)
  starting transfers between devices  11.3 us (27%)
  Pallas kernels  11.1 us (27%)
  waiting for transfers between devices  3.03 us (7%)
  between operations  1.38 us (3%)
    all_to_all x1, blocking collectives, body(): gathered = lax.all_to_all(message, ('wide', 'narrow'), 0, 0)  14.1 us
    ppermute x8, starting transfers between devices, exchange(): moved.append(lax.ppermute(packets[base + half], axis, route))  11.3 us
    pallas_call x6, Pallas kernels, call(): pl.pallas_call(kernel, name=name, out_shape=outs, in_specs=[SMEM] * len(s...  11.1 us
    ppermute x8, waiting for transfers between devices, exchange(): moved.append(lax.ppermute(packets[base + half], axis, route))  3.03 us
  transfers between devices with their start and end apart: 8, of which 2 were waited for; matrix products, arithmetic and copies ran while one was open for 0% of the time, Pallas kernels for 8%

profile of v2, /device:TPU:0, one launch (start us, length us, event | category | flops | bytes accessed | tf_op | source)
XLA Modules:
  0.0 40.9 jit_solution(16444837532274915769)
XLA Ops:
  1.3 1.5 %start.1 = (f32[64,512]{1,0:T(8,128)S(1)}, f32[72,64]{1,0:T(8,128)S(1)}, f32[72,64]{1,0:T(8,128)S(1)}, f32[72,64]{1,0:T(8,128)S(1)}, f32[72,64]{1,0:T(8,128)S(1)...) custom-call(s32[1]{0:T(128)S(6)} %copy.21.counts_ref, ...), custom_call_target="tpu_custom_call" | custom-call | bytes 445952 | tf_op jit(solution)/shard_map/start/pallas_call | solution.py:476
  2.8 0.6 %collective-permute-start = (f32[72,64]{1,0:T(8,128)S(1)}, f32[72,64]{1,0:T(8,128)S(1)}, u32[]{:S(2)}, u32[]{:S(2)}) collective-permute-start(f32[72,64]{1,0:T(8,128)S(1)} %get-tuple-element.56), channel_id=1, source_target_pairs={{0,4},{4,0},{8,12},{12,8},{16,20},{20,16},{24,28},{28,24},{1,5},{5... | collective-permute-start | bytes 55304 | tf_op jit(solution)/shard_map/ppermute | solution.py:462
  3.3 3.5 %collective-permute-start.1 = (f32[72,64]{1,0:T(8,128)S(1)}, f32[72,64]{1,0:T(8,128)S(1)}, u32[]{:S(2)}, u32[]{:S(2)}) collective-permute-start(f32[72,64]{1,0:T(8,128)S(1)} %get-tuple-element.57), channel_id=1, source_target_pairs={{0,28},{4,8},{8,4},{12,16},{16,12},{20,24},{24,20},{28,0},{1,29},{... | collective-permute-start | bytes 55304 | tf_op jit(solution)/shard_map/ppermute | solution.py:462
  6.9 1.6 %collective-permute-start.2 = (f32[72,64]{1,0:T(8,128)S(1)}, f32[72,64]{1,0:T(8,128)S(1)}, u32[]{:S(2)}, u32[]{:S(2)}) collective-permute-start(f32[72,64]{1,0:T(8,128)S(1)} %get-tuple-element.58), channel_id=1, source_target_pairs={{0,1},{1,0},{2,3},{3,2},{4,5},{5,4},{6,7},{7,6},{8,9},{9,8},{10,11... | collective-permute-start | bytes 55304 | tf_op jit(solution)/shard_map/ppermute | solution.py:462
  8.4 2.5 %collective-permute-start.3 = (f32[72,64]{1,0:T(8,128)S(1)}, f32[72,64]{1,0:T(8,128)S(1)}, u32[]{:S(2)}, u32[]{:S(2)}) collective-permute-start(f32[72,64]{1,0:T(8,128)S(1)} %get-tuple-element.59), channel_id=1, source_target_pairs={{0,3},{1,2},{2,1},{3,0},{4,7},{5,6},{6,5},{7,4},{8,11},{9,10},{10,... | collective-permute-start | bytes 55304 | tf_op jit(solution)/shard_map/ppermute | solution.py:462
  10.9 1.6 %first_local.1 = (f32[64,512]{1,0:T(8,128)S(1)}, f32[128,448]{1,0:T(8,128)S(1)}, f32[128,64]{1,0:T(8,128)S(1)}, f32[1,512]{1,0:T(1,128)S(1)}, f32[64,512]{1,0:T(8,128)S(1)}) custom-call(s32[1]{0:T(128)S(6)} %copy.21.counts_ref, f32[64,512]{1,0:T(8,128)S(1)} %get-tuple-element.42.start_ref, f32[64,512]{1,0:T(8,128)S(1)} %get-tuple-element.43.right_ref, ...), custom_call_target="tpu_custom_call" | custom-call | flops 29360128 | bytes 436480 | tf_op jit(solution)/shard_map/first_local/pallas_call | solution.py:476
  12.5 0.0 collective-permute-done.p0
  12.5 0.0 collective-permute-done.1.p1
  12.5 0.0 collective-permute-done.2.p2
  12.5 1.7 %collective-permute-done.3.p3 = f32[72,64]{1,0:T(8,128)S(1)} collective-permute-done((f32[72,64]{1,0:T(8,128)S(1)}, f32[72,64]{1,0:T(8,128)S(1)}, u32[]{:S(2)}, u32[]{:S(2)}) %collective-permute-start.3) | collective-permute-done | bytes 18464 | tf_op jit(solution)/shard_map/ppermute | solution.py:462
  14.2 1.3 %smoothed.1 = (f32[64,512]{1,0:T(8,128)S(1)}, f32[64,64]{1,0:T(8,128)S(1)}, f32[64,64]{1,0:T(8,128)S(1)}, f32[64,64]{1,0:T(8,128)S(1)}, f32[64,64]{1,0:T(8,128)S(1)}) custom-call(f32[64,512]{1,0:T(8,128)S(1)} %get-tuple-element.52.part_ref, f32[1,512]{1,0:T(1,128)S(1)} %get-tuple-element.53.relax_ref, f32[128,448]{1,0:T(8,128)S(1)} %get-tuple-element.54.folded_ref, ...), custom_call_target="tpu_custom_call" | custom-call | flops 29360128 | bytes 461824 | tf_op jit(solution)/shard_map/smoothed/pallas_call | solution.py:476
  15.4 0.0 collective-permute-start.4
  15.5 0.6 %collective-permute-start.5 = (f32[64,64]{1,0:T(8,128)S(1)}, f32[64,64]{1,0:T(8,128)S(1)}, u32[]{:S(2)}, u32[]{:S(2)}) collective-permute-start(f32[64,64]{1,0:T(8,128)S(1)} %get-tuple-element.70), channel_id=1, source_target_pairs={{0,28},{4,8},{8,4},{12,16},{16,12},{20,24},{24,20},{28,0},{1,29},{... | collective-permute-start | bytes 49160 | tf_op jit(solution)/shard_map/ppermute | solution.py:462
  16.1 0.0 collective-permute-start.6
  16.1 2.5 %collective-permute-start.7 = (f32[64,64]{1,0:T(8,128)S(1)}, f32[64,64]{1,0:T(8,128)S(1)}, u32[]{:S(2)}, u32[]{:S(2)}) collective-permute-start(f32[64,64]{1,0:T(8,128)S(1)} %get-tuple-element.72), channel_id=1, source_target_pairs={{0,3},{1,2},{2,1},{3,0},{4,7},{5,6},{6,5},{7,4},{8,11},{9,10},{10,... | collective-permute-start | bytes 49160 | tf_op jit(solution)/shard_map/ppermute | solution.py:462
  18.6 1.8 %second_local.1 = (f32[128,512]{1,0:T(8,128)S(1)}, f32[64,448]{1,0:T(8,128)S(1)}, f32[64,64]{1,0:T(8,128)S(1)}, s32[8,512]{1,0:T(8,128)S(1)}, s32[8,512]{1,0:T(8...) custom-call(s32[1]{0:T(128)S(6)} %copy.21.counts_ref, f32[64,512]{1,0:T(8,128)S(1)} %get-tuple-element.60.smoothed_ref, ...), custom_call_target="tpu_custom_call" | custom-call | flops 58720256 | bytes 646400 | tf_op jit(solution)/shard_map/second_local/pallas_call | solution.py:476
  20.5 0.0 collective-permute-done.4.p0
  20.5 0.0 collective-permute-done.5.p1
  20.5 0.0 collective-permute-done.6.p2
  20.5 1.4 %collective-permute-done.7.p3 = f32[64,64]{1,0:T(8,128)S(1)} collective-permute-done((f32[64,64]{1,0:T(8,128)S(1)}, f32[64,64]{1,0:T(8,128)S(1)}, u32[]{:S(2)}, u32[]{:S(2)}) %collective-permute-start.7) | collective-permute-done | bytes 16416 | tf_op jit(solution)/shard_map/ppermute | solution.py:462
  21.9 1.5 %restrict.1 = (f32[64,512]{1,0:T(8,128)S(1)}, f32[32,16,128]{2,1,0:T(8,128)S(1)}) custom-call(f32[128,512]{1,0:T(8,128)S(1)} %get-tuple-element.67.value_ref, f32[64,512]{1,0:T(8,128)S(1)} %get-tuple-element.60.smoothed_ref, f32[1,512]{1,0:T(1,128)S(1)} %get-tuple-element.53.relax_ref, f32[128,448]{1,0:T(8,128)S(1)} %get-tuple-element.54.folded_ref, ...), custom_call_target="tpu_custom_call" | custom-call | flops 58720256 | bytes 721152 | tf_op jit(solution)/shard_map/restrict/pallas_call | solution.py:476
  23.4 14.1 %all_to_all.5.message_ref = f32[32,16,128]{2,1,0:T(8,128)S(1)} all-to-all(f32[32,16,128]{2,1,0:T(8,128)S(1)} %get-tuple-element.73), channel_id=1, replica_groups=mesh['wide'=8,'narrow'=4] {'wide','narrow'}, dimensions={0} | all-to-all | bytes 524288 | tf_op jit(solution)/shard_map/all_to_all | solution.py:650
  37.5 3.5 %finish.1 = (f32[64,512]{1,0:T(8,128)}, f32[8,64]{1,0:T(8,128)}) custom-call(f32[32,16,128]{2,1,0:T(8,128)S(1)} %all_to_all.5.message_ref, f32[64,512]{1,0:T(8,128)S(1)} %get-tuple-element.74.base_ref, f32[1,512]{1,0:T(1,128)S(1)} %get-tuple-element.53.relax_ref, f32[64,64]{1,0:T(8,128)S(1)} %get-tuple-element.75.prol_ref, ...), custom_call_target="tpu_custom_call" | custom-call | flops 29360128 | bytes 577536 | tf_op jit(solution)/shard_map/finish/pallas_call | solution.py:476
Async XLA Ops:
  2.8 9.8 %collective-permute-start = (f32[72,64]{1,0:T(8,128)S(1)}, f32[72,64]{1,0:T(8,128)S(1)}, u32[]{:S(2)}, u32[]{:S(2)}) collective-permute-start(f32[72,64]{1,0:T(8,128)S(1)} %get-tuple-element.56), channel_id=1, source_target_pairs={{0,4},{4,0},{8,12},{12,8},{16,20},{20,16},{24,28},{28,24},{1,5},{5... | collective-permute-start | bytes 55304 | tf_op jit(solution)/shard_map/ppermute | solution.py:462
  3.3 9.2 %collective-permute-start.1 = (f32[72,64]{1,0:T(8,128)S(1)}, f32[72,64]{1,0:T(8,128)S(1)}, u32[]{:S(2)}, u32[]{:S(2)}) collective-permute-start(f32[72,64]{1,0:T(8,128)S(1)} %get-tuple-element.57), channel_id=1, source_target_pairs={{0,28},{4,8},{8,4},{12,16},{16,12},{20,24},{24,20},{28,0},{1,29},{... | collective-permute-start | bytes 55304 | tf_op jit(solution)/shard_map/ppermute | solution.py:462
  6.9 5.7 %collective-permute-start.2 = (f32[72,64]{1,0:T(8,128)S(1)}, f32[72,64]{1,0:T(8,128)S(1)}, u32[]{:S(2)}, u32[]{:S(2)}) collective-permute-start(f32[72,64]{1,0:T(8,128)S(1)} %get-tuple-element.58), channel_id=1, source_target_pairs={{0,1},{1,0},{2,3},{3,2},{4,5},{5,4},{6,7},{7,6},{8,9},{9,8},{10,11... | collective-permute-start | bytes 55304 | tf_op jit(solution)/shard_map/ppermute | solution.py:462
  8.4 5.8 %collective-permute-start.3 = (f32[72,64]{1,0:T(8,128)S(1)}, f32[72,64]{1,0:T(8,128)S(1)}, u32[]{:S(2)}, u32[]{:S(2)}) collective-permute-start(f32[72,64]{1,0:T(8,128)S(1)} %get-tuple-element.59), channel_id=1, source_target_pairs={{0,3},{1,2},{2,1},{3,0},{4,7},{5,6},{6,5},{7,4},{8,11},{9,10},{10,... | collective-permute-start | bytes 55304 | tf_op jit(solution)/shard_map/ppermute | solution.py:462
  15.4 5.0 %collective-permute-start.4 = (f32[64,64]{1,0:T(8,128)S(1)}, f32[64,64]{1,0:T(8,128)S(1)}, u32[]{:S(2)}, u32[]{:S(2)}) collective-permute-start(f32[64,64]{1,0:T(8,128)S(1)} %get-tuple-element.69), channel_id=1, source_target_pairs={{0,4},{4,0},{8,12},{12,8},{16,20},{20,16},{24,28},{28,24},{1,5},{5... | collective-permute-start | bytes 49160 | tf_op jit(solution)/shard_map/ppermute | solution.py:462
  15.5 5.0 %collective-permute-start.5 = (f32[64,64]{1,0:T(8,128)S(1)}, f32[64,64]{1,0:T(8,128)S(1)}, u32[]{:S(2)}, u32[]{:S(2)}) collective-permute-start(f32[64,64]{1,0:T(8,128)S(1)} %get-tuple-element.70), channel_id=1, source_target_pairs={{0,28},{4,8},{8,4},{12,16},{16,12},{20,24},{24,20},{28,0},{1,29},{... | collective-permute-start | bytes 49160 | tf_op jit(solution)/shard_map/ppermute | solution.py:462
  16.1 4.4 %collective-permute-start.6 = (f32[64,64]{1,0:T(8,128)S(1)}, f32[64,64]{1,0:T(8,128)S(1)}, u32[]{:S(2)}, u32[]{:S(2)}) collective-permute-start(f32[64,64]{1,0:T(8,128)S(1)} %get-tuple-element.71), channel_id=1, source_target_pairs={{0,1},{1,0},{2,3},{3,2},{4,5},{5,4},{6,7},{7,6},{8,9},{9,8},{10,11... | collective-permute-start | bytes 49160 | tf_op jit(solution)/shard_map/ppermute | solution.py:462
  16.1 5.7 %collective-permute-start.7 = (f32[64,64]{1,0:T(8,128)S(1)}, f32[64,64]{1,0:T(8,128)S(1)}, u32[]{:S(2)}, u32[]{:S(2)}) collective-permute-start(f32[64,64]{1,0:T(8,128)S(1)} %get-tuple-element.72), channel_id=1, source_target_pairs={{0,3},{1,2},{2,1},{3,0},{4,7},{5,6},{6,5},{7,4},{8,11},{9,10},{10,... | collective-permute-start | bytes 49160 | tf_op jit(solution)/shard_map/ppermute | solution.py:462

commit v3 on v2

--- a/solution.py
+++ b/solution.py
@@ -6,6 +6,7 @@
 from jax.experimental import pallas as pl
 from jax.experimental.pallas import tpu as pltpu
 from jax.sharding import PartitionSpec as P
+
 
 OMEGA = 0.7
 COARSE_OMEGA = 0.6
@@ -404,7 +405,7 @@
     uppers = [message_ref[part, 0:SUB, :] for part in parts]
     first = paired([upper[:, :coarse] for upper in uppers])
     current = first
-    for sweep, count in ((1, counts[2]), (2, counts[1])):
+    for count in (counts[2], counts[1]):
         following = []
         targets = paired([uppers[i][:, coarse:] for i in range(count)])
         weights = paired([message_ref[parts[i], SUB:, :coarse] for i in range(count)])
@@ -468,14 +469,13 @@
 HBM = pl.BlockSpec(memory_space=pltpu.HBM)
 
 
-def call(kernel, name, scalars, arrays, shapes, scratch=(), flops=0, space=VMEM):
+def call(kernel, scalars, arrays, shapes, scratch=(), flops=0, space=VMEM):
     outs = [jax.ShapeDtypeStruct(shape, dtype) for shape, dtype in shapes]
     if space is HBM:
         arrays = [pltpu.with_memory_space_constraint(x, pltpu.HBM) for x in arrays]
     moved = sum(x.size * 4 for x in arrays)
     return pl.pallas_call(
         kernel,
-        name=name,
         out_shape=outs,
         in_specs=[SMEM] * len(scalars) + [space] * len(arrays),
         out_specs=[VMEM] * len(outs),
@@ -539,7 +539,6 @@
     )
     start, *brought = call(
         functools.partial(start_kernel, carried=len(kept)),
-        "start",
         (counts,),
         (start_field, send_list, coarse_send, *kept),
         [((rows, elements), f32)] + [((rows + SUB, sent), f32)] * 4 + [(x.shape, x.dtype) for x in kept],
@@ -573,7 +572,6 @@
     first_ghosts = exchange(packets)
     part, folded, lead, relax, source = call(
         first_local_kernel,
-        "first_local",
         (counts,),
         (
             start,
@@ -599,7 +597,6 @@
     )
     smoothed, *packets = call(
         smoothed_kernel,
-        "smoothed",
         (),
         (part, relax, folded, face_scale, face_nbr, send_list, *first_ghosts),
         [((rows, elements), f32)] + [((rows, sent), f32)] * 4,
@@ -609,7 +606,6 @@
     second_ghosts = exchange(packets)
     value, spread, prol, place, child, weight, table = call(
         functools.partial(second_local_kernel, mesh_shape=mesh_shape, sent=coarse_send.shape[1], kids=kids),
-        "second_local",
         (counts,),
         (
             smoothed,
@@ -640,7 +636,6 @@
     )
     base, message = call(
         functools.partial(restrict_kernel, kids=kids),
-        "restrict",
         (),
         (value, smoothed, relax, folded, face_scale, face_nbr, slot, cscale, table, *second_ghosts),
         [((rows, elements), f32), ((devices, 2 * SUB, 2 * coarse), f32)],
@@ -652,7 +647,6 @@
     return tuple(
         call(
             functools.partial(finish_kernel, mesh_shape=mesh_shape, kids=kids),
-            "finish",
             (),
             (
                 gathered,
@@ -676,6 +670,7 @@
 
 def solution(mesh):
     both = ("wide", "narrow")
+
     return jax.shard_map(
         body,
         mesh=mesh,

time: 41.1 us -> 41.1 us (level)
  no operation moved by 1% of the time
where the time goes in v3:
time: 41.1 us; the launch traced here: 40.9 us
  blocking collectives  14.1 us (34%)
  starting transfers between devices  11.3 us (27%)
  Pallas kernels  11.1 us (27%)
  waiting for transfers between devices  3.03 us (7%)
  between operations  1.38 us (3%)
    all_to_all x1, blocking collectives, body(): gathered = lax.all_to_all(message, ('wide', 'narrow'), 0, 0)  14.1 us
    ppermute x8, starting transfers between devices, exchange(): moved.append(lax.ppermute(packets[base + half], axis, route))  11.3 us
    pallas_call x6, Pallas kernels, call(): pl.pallas_call(kernel, out_shape=outs, in_specs=[SMEM] * len(scalars) + [...  11.1 us
    ppermute x8, waiting for transfers between devices, exchange(): moved.append(lax.ppermute(packets[base + half], axis, route))  3.03 us
  transfers between devices with their start and end apart: 8, of which 2 were waited for; matrix products, arithmetic and copies ran while one was open for 0% of the time, Pallas kernels for 8%

profile of v3, /device:TPU:0, one launch (start us, length us, event | category | flops | bytes accessed | tf_op | source)
XLA Modules:
  0.0 40.9 jit_solution(16444837532274915769)
XLA Ops:
  1.3 1.5 %shard_map.194 = (f32[64,512]{1,0:T(8,128)S(1)}, f32[72,64]{1,0:T(8,128)S(1)}, f32[72,64]{1,0:T(8,128)S(1)}, f32[72,64]{1,0:T(8,128)S(1)}, f32[72,64]{1,0:T(8,12...) custom-call(s32[1]{0:T(128)S(6)} %copy.21.counts_ref, ...), custom_call_target="tpu_custom_call" | custom-call | bytes 445952 | tf_op jit(solution)/shard_map/pallas_call | solution.py:477
  2.8 0.6 %collective-permute-start = (f32[72,64]{1,0:T(8,128)S(1)}, f32[72,64]{1,0:T(8,128)S(1)}, u32[]{:S(2)}, u32[]{:S(2)}) collective-permute-start(f32[72,64]{1,0:T(8,128)S(1)} %get-tuple-element.56), channel_id=1, source_target_pairs={{0,4},{4,0},{8,12},{12,8},{16,20},{20,16},{24,28},{28,24},{1,5},{5... | collective-permute-start | bytes 55304 | tf_op jit(solution)/shard_map/ppermute | solution.py:463
  3.3 3.5 %collective-permute-start.1 = (f32[72,64]{1,0:T(8,128)S(1)}, f32[72,64]{1,0:T(8,128)S(1)}, u32[]{:S(2)}, u32[]{:S(2)}) collective-permute-start(f32[72,64]{1,0:T(8,128)S(1)} %get-tuple-element.57), channel_id=1, source_target_pairs={{0,28},{4,8},{8,4},{12,16},{16,12},{20,24},{24,20},{28,0},{1,29},{... | collective-permute-start | bytes 55304 | tf_op jit(solution)/shard_map/ppermute | solution.py:463
  6.9 1.6 %collective-permute-start.2 = (f32[72,64]{1,0:T(8,128)S(1)}, f32[72,64]{1,0:T(8,128)S(1)}, u32[]{:S(2)}, u32[]{:S(2)}) collective-permute-start(f32[72,64]{1,0:T(8,128)S(1)} %get-tuple-element.58), channel_id=1, source_target_pairs={{0,1},{1,0},{2,3},{3,2},{4,5},{5,4},{6,7},{7,6},{8,9},{9,8},{10,11... | collective-permute-start | bytes 55304 | tf_op jit(solution)/shard_map/ppermute | solution.py:463
  8.4 2.5 %collective-permute-start.3 = (f32[72,64]{1,0:T(8,128)S(1)}, f32[72,64]{1,0:T(8,128)S(1)}, u32[]{:S(2)}, u32[]{:S(2)}) collective-permute-start(f32[72,64]{1,0:T(8,128)S(1)} %get-tuple-element.59), channel_id=1, source_target_pairs={{0,3},{1,2},{2,1},{3,0},{4,7},{5,6},{6,5},{7,4},{8,11},{9,10},{10,... | collective-permute-start | bytes 55304 | tf_op jit(solution)/shard_map/ppermute | solution.py:463
  10.9 1.6 %shard_map.195 = (f32[64,512]{1,0:T(8,128)S(1)}, f32[128,448]{1,0:T(8,128)S(1)}, f32[128,64]{1,0:T(8,128)S(1)}, f32[1,512]{1,0:T(1,128)S(1)}, f32[64,512]{1,0:T(8,128)S(1)}) custom-call(s32[1]{0:T(128)S(6)} %copy.21.counts_ref, f32[64,512]{1,0:T(8,128)S(1)} %get-tuple-element.42.start_ref, f32[64,512]{1,0:T(8,128)S(1)} %get-tuple-element.43.right_ref, ...), custom_call_target="tpu_custom_call" | custom-call | flops 29360128 | bytes 436480 | tf_op jit(solution)/shard_map/pallas_call | solution.py:477
  12.5 0.0 collective-permute-done.p0
  12.5 0.0 collective-permute-done.1.p1
  12.5 0.0 collective-permute-done.2.p2
  12.5 1.7 %collective-permute-done.3.p3 = f32[72,64]{1,0:T(8,128)S(1)} collective-permute-done((f32[72,64]{1,0:T(8,128)S(1)}, f32[72,64]{1,0:T(8,128)S(1)}, u32[]{:S(2)}, u32[]{:S(2)}) %collective-permute-start.3) | collective-permute-done | bytes 18464 | tf_op jit(solution)/shard_map/ppermute | solution.py:463
  14.2 1.3 %shard_map.196 = (f32[64,512]{1,0:T(8,128)S(1)}, f32[64,64]{1,0:T(8,128)S(1)}, f32[64,64]{1,0:T(8,128)S(1)}, f32[64,64]{1,0:T(8,128)S(1)}, f32[64,64]{1,0:T(8,128)S(1)}) custom-call(f32[64,512]{1,0:T(8,128)S(1)} %get-tuple-element.52.part_ref, f32[1,512]{1,0:T(1,128)S(1)} %get-tuple-element.53.relax_ref, f32[128,448]{1,0:T(8,128)S(1)} %get-tuple-element.54.folded_ref, ...), custom_call_target="tpu_custom_call" | custom-call | flops 29360128 | bytes 461824 | tf_op jit(solution)/shard_map/pallas_call | solution.py:477
  15.4 0.0 collective-permute-start.4
  15.5 0.6 %collective-permute-start.5 = (f32[64,64]{1,0:T(8,128)S(1)}, f32[64,64]{1,0:T(8,128)S(1)}, u32[]{:S(2)}, u32[]{:S(2)}) collective-permute-start(f32[64,64]{1,0:T(8,128)S(1)} %get-tuple-element.70), channel_id=1, source_target_pairs={{0,28},{4,8},{8,4},{12,16},{16,12},{20,24},{24,20},{28,0},{1,29},{... | collective-permute-start | bytes 49160 | tf_op jit(solution)/shard_map/ppermute | solution.py:463
  16.1 0.0 collective-permute-start.6
  16.1 2.5 %collective-permute-start.7 = (f32[64,64]{1,0:T(8,128)S(1)}, f32[64,64]{1,0:T(8,128)S(1)}, u32[]{:S(2)}, u32[]{:S(2)}) collective-permute-start(f32[64,64]{1,0:T(8,128)S(1)} %get-tuple-element.72), channel_id=1, source_target_pairs={{0,3},{1,2},{2,1},{3,0},{4,7},{5,6},{6,5},{7,4},{8,11},{9,10},{10,... | collective-permute-start | bytes 49160 | tf_op jit(solution)/shard_map/ppermute | solution.py:463
  18.6 1.8 %shard_map.197 = (f32[128,512]{1,0:T(8,128)S(1)}, f32[64,448]{1,0:T(8,128)S(1)}, f32[64,64]{1,0:T(8,128)S(1)}, s32[8,512]{1,0:T(8,128)S(1)}, s32[8,512]{1,0:T(8,...) custom-call(s32[1]{0:T(128)S(6)} %copy.21.counts_ref, f32[64,512]{1,0:T(8,128)S(1)} %get-tuple-element.60.smoothed_ref, ...), custom_call_target="tpu_custom_call" | custom-call | flops 58720256 | bytes 646400 | tf_op jit(solution)/shard_map/pallas_call | solution.py:477
  20.5 0.0 collective-permute-done.4.p0
  20.5 0.0 collective-permute-done.5.p1
  20.5 0.0 collective-permute-done.6.p2
  20.5 1.4 %collective-permute-done.7.p3 = f32[64,64]{1,0:T(8,128)S(1)} collective-permute-done((f32[64,64]{1,0:T(8,128)S(1)}, f32[64,64]{1,0:T(8,128)S(1)}, u32[]{:S(2)}, u32[]{:S(2)}) %collective-permute-start.7) | collective-permute-done | bytes 16416 | tf_op jit(solution)/shard_map/ppermute | solution.py:463
  21.9 1.5 %shard_map.198 = (f32[64,512]{1,0:T(8,128)S(1)}, f32[32,16,128]{2,1,0:T(8,128)S(1)}) custom-call(f32[128,512]{1,0:T(8,128)S(1)} %get-tuple-element.67.value_ref, f32[64,512]{1,0:T(8,128)S(1)} %get-tuple-element.60.smoothed_ref, f32[1,512]{1,0:T(1,128)S(1)} %get-tuple-element.53.relax_ref, f32[128,448]{1,0:T(8,128)S(1)} %get-tuple-element.54.folded_ref, ...), custom_call_target="tpu_custom_call" | custom-call | flops 58720256 | bytes 721152 | tf_op jit(solution)/shard_map/pallas_call | solution.py:477
  23.4 14.1 %all_to_all.5.message_ref = f32[32,16,128]{2,1,0:T(8,128)S(1)} all-to-all(f32[32,16,128]{2,1,0:T(8,128)S(1)} %get-tuple-element.73), channel_id=1, replica_groups=mesh['wide'=8,'narrow'=4] {'wide','narrow'}, dimensions={0} | all-to-all | bytes 524288 | tf_op jit(solution)/shard_map/all_to_all | solution.py:645
  37.5 3.5 %shard_map.199 = (f32[64,512]{1,0:T(8,128)}, f32[8,64]{1,0:T(8,128)}) custom-call(f32[32,16,128]{2,1,0:T(8,128)S(1)} %all_to_all.5.message_ref, f32[64,512]{1,0:T(8,128)S(1)} %get-tuple-element.74.base_ref, f32[1,512]{1,0:T(1,128)S(1)} %get-tuple-element.53.relax_ref, f32[64,64]{1,0:T(8,128)S(1)} %get-tuple-element.75.prol_ref, ...), custom_call_target="tpu_custom_call" | custom-call | flops 29360128 | bytes 577536 | tf_op jit(solution)/shard_map/pallas_call | solution.py:477
Async XLA Ops:
  2.8 9.8 %collective-permute-start = (f32[72,64]{1,0:T(8,128)S(1)}, f32[72,64]{1,0:T(8,128)S(1)}, u32[]{:S(2)}, u32[]{:S(2)}) collective-permute-start(f32[72,64]{1,0:T(8,128)S(1)} %get-tuple-element.56), channel_id=1, source_target_pairs={{0,4},{4,0},{8,12},{12,8},{16,20},{20,16},{24,28},{28,24},{1,5},{5... | collective-permute-start | bytes 55304 | tf_op jit(solution)/shard_map/ppermute | solution.py:463
  3.3 9.2 %collective-permute-start.1 = (f32[72,64]{1,0:T(8,128)S(1)}, f32[72,64]{1,0:T(8,128)S(1)}, u32[]{:S(2)}, u32[]{:S(2)}) collective-permute-start(f32[72,64]{1,0:T(8,128)S(1)} %get-tuple-element.57), channel_id=1, source_target_pairs={{0,28},{4,8},{8,4},{12,16},{16,12},{20,24},{24,20},{28,0},{1,29},{... | collective-permute-start | bytes 55304 | tf_op jit(solution)/shard_map/ppermute | solution.py:463
  6.9 5.7 %collective-permute-start.2 = (f32[72,64]{1,0:T(8,128)S(1)}, f32[72,64]{1,0:T(8,128)S(1)}, u32[]{:S(2)}, u32[]{:S(2)}) collective-permute-start(f32[72,64]{1,0:T(8,128)S(1)} %get-tuple-element.58), channel_id=1, source_target_pairs={{0,1},{1,0},{2,3},{3,2},{4,5},{5,4},{6,7},{7,6},{8,9},{9,8},{10,11... | collective-permute-start | bytes 55304 | tf_op jit(solution)/shard_map/ppermute | solution.py:463
  8.4 5.8 %collective-permute-start.3 = (f32[72,64]{1,0:T(8,128)S(1)}, f32[72,64]{1,0:T(8,128)S(1)}, u32[]{:S(2)}, u32[]{:S(2)}) collective-permute-start(f32[72,64]{1,0:T(8,128)S(1)} %get-tuple-element.59), channel_id=1, source_target_pairs={{0,3},{1,2},{2,1},{3,0},{4,7},{5,6},{6,5},{7,4},{8,11},{9,10},{10,... | collective-permute-start | bytes 55304 | tf_op jit(solution)/shard_map/ppermute | solution.py:463
  15.4 5.0 %collective-permute-start.4 = (f32[64,64]{1,0:T(8,128)S(1)}, f32[64,64]{1,0:T(8,128)S(1)}, u32[]{:S(2)}, u32[]{:S(2)}) collective-permute-start(f32[64,64]{1,0:T(8,128)S(1)} %get-tuple-element.69), channel_id=1, source_target_pairs={{0,4},{4,0},{8,12},{12,8},{16,20},{20,16},{24,28},{28,24},{1,5},{5... | collective-permute-start | bytes 49160 | tf_op jit(solution)/shard_map/ppermute | solution.py:463
  15.5 5.0 %collective-permute-start.5 = (f32[64,64]{1,0:T(8,128)S(1)}, f32[64,64]{1,0:T(8,128)S(1)}, u32[]{:S(2)}, u32[]{:S(2)}) collective-permute-start(f32[64,64]{1,0:T(8,128)S(1)} %get-tuple-element.70), channel_id=1, source_target_pairs={{0,28},{4,8},{8,4},{12,16},{16,12},{20,24},{24,20},{28,0},{1,29},{... | collective-permute-start | bytes 49160 | tf_op jit(solution)/shard_map/ppermute | solution.py:463
  16.1 4.4 %collective-permute-start.6 = (f32[64,64]{1,0:T(8,128)S(1)}, f32[64,64]{1,0:T(8,128)S(1)}, u32[]{:S(2)}, u32[]{:S(2)}) collective-permute-start(f32[64,64]{1,0:T(8,128)S(1)} %get-tuple-element.71), channel_id=1, source_target_pairs={{0,1},{1,0},{2,3},{3,2},{4,5},{5,4},{6,7},{7,6},{8,9},{9,8},{10,11... | collective-permute-start | bytes 49160 | tf_op jit(solution)/shard_map/ppermute | solution.py:463
  16.1 5.7 %collective-permute-start.7 = (f32[64,64]{1,0:T(8,128)S(1)}, f32[64,64]{1,0:T(8,128)S(1)}, u32[]{:S(2)}, u32[]{:S(2)}) collective-permute-start(f32[64,64]{1,0:T(8,128)S(1)} %get-tuple-element.72), channel_id=1, source_target_pairs={{0,3},{1,2},{2,1},{3,0},{4,7},{5,6},{6,5},{7,4},{8,11},{9,10},{10,... | collective-permute-start | bytes 49160 | tf_op jit(solution)/shard_map/ppermute | solution.py:463

commit v4 on v3

--- a/solution.py
+++ b/solution.py
@@ -10,15 +10,16 @@
 
 OMEGA = 0.7
 COARSE_OMEGA = 0.6
-HIGH = lax.Precision.HIGHEST
+HIGH = lax.Precision.HIGH
+HIGHEST = lax.Precision.HIGHEST
 LANES = 128
 SUB = 8
 FACES = 6
 GRANT = 16 * 1024 * 1024
 
 
-def dot(left, right):
-    return jnp.dot(left, right, preferred_element_type=jnp.float32, precision=HIGH)
+def dot(left, right, precision=HIGH):
+    return jnp.dot(left, right, preferred_element_type=jnp.float32, precision=precision)
 
 
 def dot_t(left, right):
@@ -79,27 +80,30 @@
     return index
 
 
+def in_order(axis, first, second):
+    if lax.axis_size(axis) % 2:
+        return first, second
+    return swapped(axis, second, first)
+
+
 def received(packets, row):
     tiles = []
     for base, axis in ((0, "wide"), (2, "narrow")):
-        first = packets[base][row : row + SUB, :]
-        second = packets[base + 1][row : row + SUB, :]
-        if lax.axis_size(axis) % 2 == 0:
-            first, second = swapped(axis, second, first)
-        tiles.append(jnp.concatenate([first, second], axis=1))
+        pair = [packet[row : row + SUB, :] for packet in packets[base : base + 2]]
+        tiles.append(jnp.concatenate(in_order(axis, *pair), axis=1))
     return tiles
 
 
 def start_kernel(counts_ref, *refs, carried):
-    given, refs = refs[: carried + 3], refs[carried + 3 :]
+    given, refs = refs[: carried + 2], refs[carried + 2 :]
     masked_ref, outs, kept = refs[0], refs[1:5], refs[5 : 5 + carried]
-    start_ref, send_ref, csend_ref, sems = refs[5 + carried :]
-    slot_ref = kept[0]
-    held = (start_ref, send_ref, csend_ref, *kept)
+    start_ref, send_ref, sems = refs[5 + carried :]
+    slot_ref, cnbr_ref, csend_ref = kept[:3]
+    held = (start_ref, send_ref, *kept)
     copies = [pltpu.make_async_copy(here, there, sems.at[i]) for i, (here, there) in enumerate(zip(given, held))]
     for copy in copies:
         copy.start()
-    for copy in copies[:4]:
+    for copy in copies[:5]:
         copy.wait()
     rows, elements = start_ref.shape
     active = activity(counts_ref, elements)
@@ -110,13 +114,14 @@
     csend = csend_ref[...].astype(jnp.float32)
     blank = jnp.zeros((1, LANES // 2 - csend.shape[1]), jnp.float32)
     order = ordered_sends(csend)
-    line = lax.broadcasted_iota(jnp.int32, (SUB, LANES), 0)
+    table = cnbr_ref[...].astype(jnp.float32)
+    table = jnp.concatenate([table, table], axis=1)
     halves = []
     for half in range(2):
         coarse = jnp.concatenate([order[2 * half], blank, order[2 * half + 1], blank], axis=1)
-        halves.append(jnp.where(line == 0, pick(tiles, index[half]), rows8(coarse)))
+        halves.append(jnp.concatenate([pick(tiles, index[half])[0:1], coarse, table], axis=0))
     store_packets(outs, halves, rows)
-    for copy in copies[4:]:
+    for copy in copies[5:]:
         copy.wait()
 
 
@@ -194,8 +199,15 @@
     outs, g_ref = rest[:4], rest[4]
     rows, elements = part_ref.shape
     ghost_blocks((p0, p1, p2, p3), rows, elements, fscale_ref, nbr_ref, g_ref)
-    smoothed_ref[...] = part_ref[...] - relax_ref[...] * dot(folded_ref[rows:, rows:], g_ref[...])
+    smoothed_ref[...] = part_ref[...] - relax_ref[...] * dot(folded_ref[rows:, rows:], g_ref[...], HIGHEST)
     pack(send_ref[...], smoothed_ref, outs, rows, elements)
+    packets = (p0, p1, p2, p3)
+    for slot, axis in enumerate(("wide", "wide", "narrow", "narrow")):
+        straight = slot if lax.axis_size(axis) % 2 else slot ^ 1
+        relayed = (straight, 2, 3) if axis == "wide" else (straight,)
+        for place, which in enumerate(relayed):
+            at = rows + SUB * place
+            outs[slot][at : at + SUB, :] = packets[which][rows : rows + SUB, :]
 
 
 def second_local_kernel(
@@ -212,6 +224,7 @@
     cscale_ref,
     cfscale_ref,
     cnbr_ref,
+    csend_ref,
     p0,
     p1,
     p2,
@@ -225,12 +238,9 @@
     table_ref,
     g_ref,
     *,
-    mesh_shape,
-    sent,
     kids,
 ):
     rows, elements = smoothed_ref.shape
-    wides, narrows = mesh_shape
     coarse = cscale_ref.shape[1]
     local_blocks(smoothed_ref, scale_ref, fscale_ref, nbr_ref, g_ref)
     value_ref[...] = dot(lead_ref[...], source_ref[...]) - dot(folded_ref[...], g_ref[...])
@@ -262,35 +272,12 @@
         weight = jnp.concatenate([fscale_ref[:, cols], scale_ref[:, cols], scale_ref[:, cols]], axis=0)
         weight_ref[:, cols] = jnp.where(live, weight, 0.0)
 
-    wide, narrow = lax.axis_index("wide"), lax.axis_index("narrow")
-    me = wide * narrows + narrow
-    owners = (
-        lax.rem(wide + wides - 1, wides) * narrows + narrow,
-        lax.rem(wide + 1, wides) * narrows + narrow,
-        wide * narrows + lax.rem(narrow + narrows - 1, narrows),
-        wide * narrows + lax.rem(narrow + 1, narrows),
-    )
-    entry = jnp.concatenate([cnbr_ref[...], jnp.zeros((SUB - FACES, coarse), jnp.int32)], axis=0)
-    remote = entry - coarse
-    direction = remote // sent
-    offset = jnp.maximum(remote - direction * sent, 0)
-    wanted = jnp.clip(jnp.where(direction == 1, side, jnp.where(direction == 3, side, 0)) + offset, 0, LANES - 1)
-    pad = jnp.zeros((SUB, LANES - coarse), jnp.int32)
-    wanted = jnp.concatenate([wanted, pad], axis=1) if coarse < LANES else wanted
-    lists = [rows8(half[1:2]) for half in halves]
-    first = lane_take(lists[0], wanted)[:, :coarse].astype(jnp.int32)
-    second = lane_take(lists[1], wanted)[:, :coarse].astype(jnp.int32)
-    there = jnp.where(direction < 2, first, second)
-    owner = jnp.where(
-        direction == 0,
-        owners[0],
-        jnp.where(direction == 1, owners[1], jnp.where(direction == 2, owners[2], owners[3])),
-    )
-    target = jnp.where(entry < coarse, me * coarse + entry, owner * coarse + there)
-    ones = jnp.zeros((SUB - FACES, coarse), jnp.float32)
-    cweight = jnp.concatenate([cfscale_ref[...] * (COARSE_OMEGA / cscale_ref[...]), ones], axis=0)
-    table_ref[0:SUB, :] = jnp.where(entry >= 0, target, 0).astype(jnp.float32)
-    table_ref[SUB:, :] = jnp.where(entry >= 0, cweight, 0.0)
+    cweight = jnp.where(cnbr_ref[...] >= 0, cfscale_ref[...] * (COARSE_OMEGA / cscale_ref[...]), 0.0)
+    sends = jnp.concatenate([csend_ref[i : i + 1].astype(jnp.float32) for i in range(csend_ref.shape[0])], axis=1)
+    spare = coarse - sends.shape[1]
+    if spare:
+        sends = jnp.concatenate([sends, jnp.zeros((1, spare), jnp.float32)], axis=1)
+    table_ref[...] = jnp.concatenate([cweight, sends, sends], axis=0)
 
 
 def restrict_kernel(
@@ -326,11 +313,9 @@
         summed = jnp.where(child == kid, value[kid * step : (kid + 1) * step, :], summed)
     member = lax.broadcasted_iota(jnp.int32, (coarse, elements), 0) == slot // kids
     first = dot_t(summed, member.astype(jnp.float32)) * (COARSE_OMEGA / cscale_ref[...])
-    upper = jnp.concatenate([first, table_ref[0:SUB, :]], axis=1)
-    lower = jnp.concatenate([table_ref[SUB:, :], jnp.zeros_like(first)], axis=1)
+    message = jnp.concatenate([first, table_ref[...]], axis=1)
     for device in range(message_ref.shape[0]):
-        message_ref[device, 0:SUB, :] = upper
-        message_ref[device, SUB:, :] = lower
+        message_ref[device] = message
 
 
 def neighbourhood(mesh_shape, reach):
@@ -342,13 +327,30 @@
     counts = [1, len(found)]
     for distance in range(2, reach + 1):
         for w in range(-distance, distance + 1):
-            for n in {distance - abs(w), abs(w) - distance}:
+            for n in (distance - abs(w), abs(w) - distance):
                 key = (w % wides, n % narrows)
                 if key not in seen:
                     seen.add(key)
                     found.append((w, n))
         counts.append(len(found))
     return found, counts
+
+
+def neighbour_tables(row, own_ref, near, far):
+    def brought(packets, axis, at):
+        base = 0 if axis == "wide" else 2
+        return in_order(axis, *(packet[at : at + SUB, :] for packet in packets[base : base + 2]))
+
+    own = own_ref[...].astype(jnp.float32)
+    found = {(0, 0): jnp.concatenate([jnp.zeros((SUB - FACES, own.shape[1]), jnp.float32), own], axis=0)}
+    found[-1, 0], found[1, 0] = brought(near, "wide", row)
+    found[0, -1], found[0, 1] = brought(near, "narrow", row)
+    found[-2, 0], found[2, 0] = brought(far, "wide", row)
+    found[0, -2], found[0, 2] = brought(far, "narrow", row)
+    one, two = brought(far, "wide", row + SUB), brought(far, "wide", row + 2 * SUB)
+    for side in range(2):
+        found[2 * side - 1, -1], found[2 * side - 1, 1] = in_order("narrow", one[side], two[side])
+    return found
 
 
 def paired(pieces):
@@ -369,6 +371,15 @@
     cblock_ref,
     csmooth_ref,
     cfaces_ref,
+    cnbr_ref,
+    p0,
+    p1,
+    p2,
+    p3,
+    q0,
+    q1,
+    q2,
+    q3,
     field_ref,
     correction_ref,
     folded_ref,
@@ -377,6 +388,7 @@
     *,
     mesh_shape,
     kids,
+    sent,
 ):
     rows, elements = base_ref.shape
     cdof, coarse = correction_ref.shape
@@ -393,34 +405,48 @@
         folded_ref[:, face * cdof : (face + 1) * cdof] = dot(csmooth, cfaces_ref[face])
     folded = folded_ref[...]
 
-    blocks = wides * narrows
-    lane = lax.broadcasted_iota(jnp.int32, (SUB, LANES), 1)
-    ranks = []
-    for base in range(0, blocks, LANES):
-        rank = jnp.zeros((SUB, LANES), jnp.int32)
-        for position, part in reversed(list(enumerate(parts))):
-            rank = jnp.where(lane + base == part, position, rank)
-        ranks.append(rank)
-
-    uppers = [message_ref[part, 0:SUB, :] for part in parts]
-    first = paired([upper[:, :coarse] for upper in uppers])
+    tables = neighbour_tables(rows, cnbr_ref, (p0, p1, p2, p3), (q0, q1, q2, q3))
+    ranks = {}
+    for rank, (w, n) in reversed(list(enumerate(offsets))):
+        ranks[w % wides, n % narrows] = rank
+    beside = [
+        [ranks[(w + dw) % wides, (n + dn) % narrows] * coarse for dw, dn in offsets[1:5]] for w, n in offsets[: counts[2]]
+    ]
+    messages = [message_ref[part] for part in parts]
+    first = paired([message[:, :coarse] for message in messages])
+    extras = paired([message[:, coarse:] for message in messages])
+    lists = [rows8(extra[FACES : FACES + 1]) for extra in extras]
+    entries = paired([tables[offset] for offset in offsets[: counts[2]]])
+    left = lax.broadcasted_iota(jnp.int32, (SUB, LANES), 1) < coarse
+    indices = []
+    for t, entry in enumerate(entries):
+        pair = [2 * t, min(2 * t + 1, counts[2] - 1)]
+        entry = jnp.maximum(entry.astype(jnp.int32), 0)
+        remote = entry - coarse
+        base = [jnp.where(left, beside[pair[0]][d], beside[pair[1]][d]) for d in range(4)]
+        owner = jnp.where(
+            remote < 2 * sent,
+            jnp.where(remote < sent, base[0], base[1]),
+            jnp.where(remote < 3 * sent, base[2], base[3]),
+        )
+        home = jnp.where(left, pair[0] * coarse, pair[1] * coarse)
+        there = pick(lists, owner + jnp.maximum(remote, 0)).astype(jnp.int32)
+        indices.append(jnp.where(remote < 0, home + entry, owner + there))
+
     current = first
     for count in (counts[2], counts[1]):
         following = []
-        targets = paired([uppers[i][:, coarse:] for i in range(count)])
-        weights = paired([message_ref[parts[i], SUB:, :coarse] for i in range(count)])
-        for t in range(len(targets)):
-            target = targets[t].astype(jnp.int32)
-            index = pick(ranks, target // coarse) * coarse + target % coarse
+        tiles = -(-count // 2)
+        for t in range(tiles):
             for face in range(FACES):
-                chosen = pick(current, rows8(index[face : face + 1]))
+                row = SUB - FACES + face
+                chosen = pick(current, rows8(indices[t][row : row + 1]))
                 cg_ref[face * cdof : (face + 1) * cdof, t * LANES : (t + 1) * LANES] = (
-                    rows8(weights[t][face : face + 1]) * chosen
+                    rows8(extras[t][face : face + 1]) * chosen
                 )
-        width = len(targets) * LANES
-        pulled = dot(folded, cg_ref[:, :width])
-        inner = dot(own, jnp.concatenate(current[: len(targets)], axis=1))
-        for t in range(len(targets)):
+        pulled = dot(folded, cg_ref[:, : tiles * LANES])
+        inner = dot(own, jnp.concatenate(current[:tiles], axis=1))
+        for t in range(tiles):
             cols = slice(t * LANES, (t + 1) * LANES)
             following.append(current[t] + first[t] - inner[:, cols] - pulled[:, cols])
         current = following
@@ -521,6 +547,8 @@
 
     kept = (
         slot,
+        coarse_nbr,
+        coarse_send,
         right_side,
         scale,
         face_scale,
@@ -531,7 +559,6 @@
         prolong,
         cscale,
         coarse_face_scale,
-        coarse_nbr,
         coarse_block,
         coarse_smooth,
         coarse_faces,
@@ -540,19 +567,20 @@
     start, *brought = call(
         functools.partial(start_kernel, carried=len(kept)),
         (counts,),
-        (start_field, send_list, coarse_send, *kept),
+        (start_field, send_list, *kept),
         [((rows, elements), f32)] + [((rows + SUB, sent), f32)] * 4 + [(x.shape, x.dtype) for x in kept],
         [
             pltpu.VMEM(start_field.shape, f32),
             pltpu.VMEM(send_list.shape, i32),
-            pltpu.VMEM(coarse_send.shape, i32),
-            pltpu.SemaphoreType.DMA((len(kept) + 3,)),
+            pltpu.SemaphoreType.DMA((len(kept) + 2,)),
         ],
         space=HBM,
     )
     packets = brought[:4]
     (
         slot,
+        coarse_nbr,
+        coarse_send,
         right_side,
         scale,
         face_scale,
@@ -563,7 +591,6 @@
         prolong,
         cscale,
         coarse_face_scale,
-        coarse_nbr,
         coarse_block,
         coarse_smooth,
         coarse_faces,
@@ -599,13 +626,13 @@
         smoothed_kernel,
         (),
         (part, relax, folded, face_scale, face_nbr, send_list, *first_ghosts),
-        [((rows, elements), f32)] + [((rows, sent), f32)] * 4,
+        [((rows, elements), f32)] + [((rows + 3 * SUB, sent), f32)] * 2 + [((rows + SUB, sent), f32)] * 2,
         [(blocks - rows, elements)],
         flops=2 * blocks * rows * elements,
     )
     second_ghosts = exchange(packets)
     value, spread, prol, place, child, weight, table = call(
-        functools.partial(second_local_kernel, mesh_shape=mesh_shape, sent=coarse_send.shape[1], kids=kids),
+        functools.partial(second_local_kernel, kids=kids),
         (counts,),
         (
             smoothed,
@@ -620,6 +647,7 @@
             cscale,
             coarse_face_scale,
             coarse_nbr,
+            coarse_send,
             *first_ghosts,
         ),
         [
@@ -629,7 +657,7 @@
             ((SUB, elements), i32),
             ((SUB, elements), i32),
             ((SUB, elements), f32),
-            ((2 * SUB, coarse), f32),
+            ((SUB, coarse), f32),
         ],
         [(blocks, elements)],
         flops=4 * blocks * rows * elements,
@@ -638,7 +666,7 @@
         functools.partial(restrict_kernel, kids=kids),
         (),
         (value, smoothed, relax, folded, face_scale, face_nbr, slot, cscale, table, *second_ghosts),
-        [((rows, elements), f32), ((devices, 2 * SUB, 2 * coarse), f32)],
+        [((rows, elements), f32), ((devices, SUB, 2 * coarse), f32)],
         [(blocks - rows, elements)],
         flops=4 * blocks * rows * elements,
     )
@@ -646,7 +674,7 @@
     needed = -(-neighbourhood(mesh_shape, 3)[1][2] // 2) * 2 * coarse
     return tuple(
         call(
-            functools.partial(finish_kernel, mesh_shape=mesh_shape, kids=kids),
+            functools.partial(finish_kernel, mesh_shape=mesh_shape, kids=kids, sent=coarse_send.shape[1]),
             (),
             (
                 gathered,
@@ -660,6 +688,9 @@
                 coarse_block,
                 coarse_smooth,
                 coarse_faces,
+                coarse_nbr,
+                *first_ghosts,
+                *second_ghosts,
             ),
             [((rows, elements), f32), ((cdof, coarse), f32)],
             [(cdof, FACES * cdof), (FACES * cdof, needed), (blocks + rows, elements)],

time: 41.1 us -> 38.5 us (0.937)
  blocking collectives: 14.1 us -> 12.3 us
  Pallas kernels: 11.1 us -> 9.6 us
  waiting for transfers between devices: 3.03 us -> 3.8 us
    all_to_all x1, blocking collectives: 14.1 us -> 12.3 us  [body(): gathered = lax.all_to_all(message, ('wide', 'narrow'), 0, 0)]
    pallas_call x6, Pallas kernels: 11.1 us -> 9.6 us  [call(): pl.pallas_call(kernel, out_shape=outs, in_specs=[SMEM] * len(scalars) + [...]
    ppermute x8, waiting for transfers between devices: 3.03 us -> 3.8 us  [exchange(): moved.append(lax.ppermute(packets[base + half], axis, route))]
  transfers between devices with their start and end apart: 8 -> 8, of which waited for: 2 -> 3; matrix products, arithmetic and copies ran while one was open for 0% -> 0% of each run, Pallas kernels for 8% -> 7%
where the time goes in v4:
time: 38.5 us; the launch traced here: 38.3 us
  blocking collectives  12.3 us (32%)
  starting transfers between devices  11.3 us (29%)
  Pallas kernels  9.6 us (25%)
  waiting for transfers between devices  3.8 us (10%)
  between operations  1.35 us (4%)
    all_to_all x1, blocking collectives, body(): gathered = lax.all_to_all(message, ('wide', 'narrow'), 0, 0)  12.3 us
    ppermute x8, starting transfers between devices, exchange(): moved.append(lax.ppermute(packets[base + half], axis, route))  11.3 us
    pallas_call x6, Pallas kernels, call(): pl.pallas_call(kernel, out_shape=outs, in_specs=[SMEM] * len(scalars) + [...  9.6 us
    ppermute x8, waiting for transfers between devices, exchange(): moved.append(lax.ppermute(packets[base + half], axis, route))  3.8 us
  transfers between devices with their start and end apart: 8, of which 3 were waited for; matrix products, arithmetic and copies ran while one was open for 0% of the time, Pallas kernels for 7%

profile of v4, /device:TPU:0, one launch (start us, length us, event | category | flops | bytes accessed | tf_op | source)
XLA Modules:
  0.0 38.3 jit_solution(6270483644531356699)
XLA Ops:
  1.3 1.4 %shard_map.194 = (f32[64,512]{1,0:T(8,128)S(1)}, f32[72,64]{1,0:T(8,128)S(1)}, f32[72,64]{1,0:T(8,128)S(1)}, f32[72,64]{1,0:T(8,128)S(1)}, f32[72,64]{1,0:T(8,12...) custom-call(s32[1]{0:T(128)S(6)} %copy.21.counts_ref, ...), custom_call_target="tpu_custom_call" | custom-call | bytes 445952 | tf_op jit(solution)/shard_map/pallas_call | solution.py:503
  2.7 0.6 %collective-permute-start = (f32[72,64]{1,0:T(8,128)S(1)}, f32[72,64]{1,0:T(8,128)S(1)}, u32[]{:S(2)}, u32[]{:S(2)}) collective-permute-start(f32[72,64]{1,0:T(8,128)S(1)} %get-tuple-element.57), channel_id=1, source_target_pairs={{0,4},{4,0},{8,12},{12,8},{16,20},{20,16},{24,28},{28,24},{1,5},{5... | collective-permute-start | bytes 55304 | tf_op jit(solution)/shard_map/ppermute | solution.py:489
  3.3 3.5 %collective-permute-start.1 = (f32[72,64]{1,0:T(8,128)S(1)}, f32[72,64]{1,0:T(8,128)S(1)}, u32[]{:S(2)}, u32[]{:S(2)}) collective-permute-start(f32[72,64]{1,0:T(8,128)S(1)} %get-tuple-element.58), channel_id=1, source_target_pairs={{0,28},{4,8},{8,4},{12,16},{16,12},{20,24},{24,20},{28,0},{1,29},{... | collective-permute-start | bytes 55304 | tf_op jit(solution)/shard_map/ppermute | solution.py:489
  6.8 1.6 %collective-permute-start.2 = (f32[72,64]{1,0:T(8,128)S(1)}, f32[72,64]{1,0:T(8,128)S(1)}, u32[]{:S(2)}, u32[]{:S(2)}) collective-permute-start(f32[72,64]{1,0:T(8,128)S(1)} %get-tuple-element.59), channel_id=1, source_target_pairs={{0,1},{1,0},{2,3},{3,2},{4,5},{5,4},{6,7},{7,6},{8,9},{9,8},{10,11... | collective-permute-start | bytes 55304 | tf_op jit(solution)/shard_map/ppermute | solution.py:489
  8.4 2.5 %collective-permute-start.3 = (f32[72,64]{1,0:T(8,128)S(1)}, f32[72,64]{1,0:T(8,128)S(1)}, u32[]{:S(2)}, u32[]{:S(2)}) collective-permute-start(f32[72,64]{1,0:T(8,128)S(1)} %get-tuple-element.60), channel_id=1, source_target_pairs={{0,3},{1,2},{2,1},{3,0},{4,7},{5,6},{6,5},{7,4},{8,11},{9,10},{10,... | collective-permute-start | bytes 55304 | tf_op jit(solution)/shard_map/ppermute | solution.py:489
  10.9 1.4 %shard_map.195 = (f32[64,512]{1,0:T(8,128)S(1)}, f32[128,448]{1,0:T(8,128)S(1)}, f32[128,64]{1,0:T(8,128)S(1)}, f32[1,512]{1,0:T(1,128)S(1)}, f32[64,512]{1,0:T(8,128)S(1)}) custom-call(s32[1]{0:T(128)S(6)} %copy.21.counts_ref, f32[64,512]{1,0:T(8,128)S(1)} %get-tuple-element.43.start_ref, f32[64,512]{1,0:T(8,128)S(1)} %get-tuple-element.44.right_ref, ...), custom_call_target="tpu_custom_call" | custom-call | flops 29360128 | bytes 436480 | tf_op jit(solution)/shard_map/pallas_call | solution.py:503
  12.3 0.0 collective-permute-done.p0
  12.3 0.0 collective-permute-done.1.p1
  12.3 0.0 collective-permute-done.2.p2
  12.3 1.9 %collective-permute-done.3.p3 = f32[72,64]{1,0:T(8,128)S(1)} collective-permute-done((f32[72,64]{1,0:T(8,128)S(1)}, f32[72,64]{1,0:T(8,128)S(1)}, u32[]{:S(2)}, u32[]{:S(2)}) %collective-permute-start.3) | collective-permute-done | bytes 18464 | tf_op jit(solution)/shard_map/ppermute | solution.py:489
  14.2 1.3 %shard_map.196 = (f32[64,512]{1,0:T(8,128)S(1)}, f32[88,64]{1,0:T(8,128)S(1)}, f32[88,64]{1,0:T(8,128)S(1)}, f32[72,64]{1,0:T(8,128)S(1)}, f32[72,64]{1,0:T(8,128)S(1)}) custom-call(f32[64,512]{1,0:T(8,128)S(1)} %get-tuple-element.53.part_ref, f32[1,512]{1,0:T(1,128)S(1)} %get-tuple-element.54.relax_ref, f32[128,448]{1,0:T(8,128)S(1)} %get-tuple-element.55.folded_ref, ...), custom_call_target="tpu_custom_call" | custom-call | flops 29360128 | bytes 461824 | tf_op jit(solution)/shard_map/pallas_call | solution.py:503
  15.4 0.0 collective-permute-start.4
  15.5 0.6 %collective-permute-start.5 = (f32[88,64]{1,0:T(8,128)S(1)}, f32[88,64]{1,0:T(8,128)S(1)}, u32[]{:S(2)}, u32[]{:S(2)}) collective-permute-start(f32[88,64]{1,0:T(8,128)S(1)} %get-tuple-element.72), channel_id=1, source_target_pairs={{0,28},{4,8},{8,4},{12,16},{16,12},{20,24},{24,20},{28,0},{1,29},{... | collective-permute-start | bytes 67592 | tf_op jit(solution)/shard_map/ppermute | solution.py:489
  16.1 0.0 collective-permute-start.6
  16.1 2.5 %collective-permute-start.7 = (f32[72,64]{1,0:T(8,128)S(1)}, f32[72,64]{1,0:T(8,128)S(1)}, u32[]{:S(2)}, u32[]{:S(2)}) collective-permute-start(f32[72,64]{1,0:T(8,128)S(1)} %get-tuple-element.74), channel_id=1, source_target_pairs={{0,3},{1,2},{2,1},{3,0},{4,7},{5,6},{6,5},{7,4},{8,11},{9,10},{10,... | collective-permute-start | bytes 55304 | tf_op jit(solution)/shard_map/ppermute | solution.py:489
  18.6 1.4 %shard_map.197 = (f32[128,512]{1,0:T(8,128)S(1)}, f32[64,448]{1,0:T(8,128)S(1)}, f32[64,64]{1,0:T(8,128)S(1)}, s32[8,512]{1,0:T(8,128)S(1)}, s32[8,512]{1,0:T(8,...) custom-call(s32[1]{0:T(128)S(6)} %copy.21.counts_ref, f32[64,512]{1,0:T(8,128)S(1)} %get-tuple-element.61.smoothed_ref, ...), custom_call_target="tpu_custom_call" | custom-call | flops 58720256 | bytes 646656 | tf_op jit(solution)/shard_map/pallas_call | solution.py:503
  20.0 0.1 collective-permute-done.6.p2.q2
  20.1 1.9 %collective-permute-done.7.p3.q3 = f32[72,64]{1,0:T(8,128)S(1)} collective-permute-done((f32[72,64]{1,0:T(8,128)S(1)}, f32[72,64]{1,0:T(8,128)S(1)}, u32[]{:S(2)}, u32[]{:S(2)}) %collective-permute-start.7) | collective-permute-done | bytes 18464 | tf_op jit(solution)/shard_map/ppermute | solution.py:489
  21.9 0.0 collective-permute-done.4.p0.q0
  21.9 0.0 collective-permute-done.5.p1.q1
  21.9 1.2 %shard_map.198 = (f32[64,512]{1,0:T(8,128)S(1)}, f32[32,8,128]{2,1,0:T(8,128)S(1)}) custom-call(f32[128,512]{1,0:T(8,128)S(1)} %get-tuple-element.69.value_ref, f32[64,512]{1,0:T(8,128)S(1)} %get-tuple-element.61.smoothed_ref, f32[1,512]{1,0:T(1,128)S(1)} %get-tuple-element.54.relax_ref, f32[128,448]{1,0:T(8,128)S(1)} %get-tuple-element.55.folded_ref, ...), custom_call_target="tpu_custom_call" | custom-call | flops 58720256 | bytes 735488 | tf_op jit(solution)/shard_map/pallas_call | solution.py:503
  23.2 12.3 %all_to_all.5.message_ref = f32[32,8,128]{2,1,0:T(8,128)S(1)} all-to-all(f32[32,8,128]{2,1,0:T(8,128)S(1)} %get-tuple-element.75), channel_id=1, replica_groups=mesh['wide'=8,'narrow'=4] {'wide','narrow'}, dimensions={0} | all-to-all | bytes 262144 | tf_op jit(solution)/shard_map/all_to_all | solution.py:673
  35.4 2.9 %shard_map.199 = (f32[64,512]{1,0:T(8,128)}, f32[8,64]{1,0:T(8,128)}) custom-call(f32[32,8,128]{2,1,0:T(8,128)S(1)} %all_to_all.5.message_ref, f32[64,512]{1,0:T(8,128)S(1)} %get-tuple-element.76.base_ref, f32[1,512]{1,0:T(1,128)S(1)} %get-tuple-element.54.relax_ref, f32[64,64]{1,0:T(8,128)S(1)} %get-tuple-element.77.prol_ref, ...), custom_call_target="tpu_custom_call" | custom-call | flops 29360128 | bytes 603648 | tf_op jit(solution)/shard_map/pallas_call | solution.py:503
Async XLA Ops:
  2.7 9.5 %collective-permute-start = (f32[72,64]{1,0:T(8,128)S(1)}, f32[72,64]{1,0:T(8,128)S(1)}, u32[]{:S(2)}, u32[]{:S(2)}) collective-permute-start(f32[72,64]{1,0:T(8,128)S(1)} %get-tuple-element.57), channel_id=1, source_target_pairs={{0,4},{4,0},{8,12},{12,8},{16,20},{20,16},{24,28},{28,24},{1,5},{5... | collective-permute-start | bytes 55304 | tf_op jit(solution)/shard_map/ppermute | solution.py:489
  3.3 9.0 %collective-permute-start.1 = (f32[72,64]{1,0:T(8,128)S(1)}, f32[72,64]{1,0:T(8,128)S(1)}, u32[]{:S(2)}, u32[]{:S(2)}) collective-permute-start(f32[72,64]{1,0:T(8,128)S(1)} %get-tuple-element.58), channel_id=1, source_target_pairs={{0,28},{4,8},{8,4},{12,16},{16,12},{20,24},{24,20},{28,0},{1,29},{... | collective-permute-start | bytes 55304 | tf_op jit(solution)/shard_map/ppermute | solution.py:489
  6.8 5.4 %collective-permute-start.2 = (f32[72,64]{1,0:T(8,128)S(1)}, f32[72,64]{1,0:T(8,128)S(1)}, u32[]{:S(2)}, u32[]{:S(2)}) collective-permute-start(f32[72,64]{1,0:T(8,128)S(1)} %get-tuple-element.59), channel_id=1, source_target_pairs={{0,1},{1,0},{2,3},{3,2},{4,5},{5,4},{6,7},{7,6},{8,9},{9,8},{10,11... | collective-permute-start | bytes 55304 | tf_op jit(solution)/shard_map/ppermute | solution.py:489
  8.4 5.8 %collective-permute-start.3 = (f32[72,64]{1,0:T(8,128)S(1)}, f32[72,64]{1,0:T(8,128)S(1)}, u32[]{:S(2)}, u32[]{:S(2)}) collective-permute-start(f32[72,64]{1,0:T(8,128)S(1)} %get-tuple-element.60), channel_id=1, source_target_pairs={{0,3},{1,2},{2,1},{3,0},{4,7},{5,6},{6,5},{7,4},{8,11},{9,10},{10,... | collective-permute-start | bytes 55304 | tf_op jit(solution)/shard_map/ppermute | solution.py:489
  15.4 6.5 %collective-permute-start.4 = (f32[88,64]{1,0:T(8,128)S(1)}, f32[88,64]{1,0:T(8,128)S(1)}, u32[]{:S(2)}, u32[]{:S(2)}) collective-permute-start(f32[88,64]{1,0:T(8,128)S(1)} %get-tuple-element.71), channel_id=1, source_target_pairs={{0,4},{4,0},{8,12},{12,8},{16,20},{20,16},{24,28},{28,24},{1,5},{5... | collective-permute-start | bytes 67592 | tf_op jit(solution)/shard_map/ppermute | solution.py:489
  15.5 6.5 %collective-permute-start.5 = (f32[88,64]{1,0:T(8,128)S(1)}, f32[88,64]{1,0:T(8,128)S(1)}, u32[]{:S(2)}, u32[]{:S(2)}) collective-permute-start(f32[88,64]{1,0:T(8,128)S(1)} %get-tuple-element.72), channel_id=1, source_target_pairs={{0,28},{4,8},{8,4},{12,16},{16,12},{20,24},{24,20},{28,0},{1,29},{... | collective-permute-start | bytes 67592 | tf_op jit(solution)/shard_map/ppermute | solution.py:489
  16.1 4.0 %collective-permute-start.6 = (f32[72,64]{1,0:T(8,128)S(1)}, f32[72,64]{1,0:T(8,128)S(1)}, u32[]{:S(2)}, u32[]{:S(2)}) collective-permute-start(f32[72,64]{1,0:T(8,128)S(1)} %get-tuple-element.73), channel_id=1, source_target_pairs={{0,1},{1,0},{2,3},{3,2},{4,5},{5,4},{6,7},{7,6},{8,9},{9,8},{10,11... | collective-permute-start | bytes 55304 | tf_op jit(solution)/shard_map/ppermute | solution.py:489
  16.1 5.8 %collective-permute-start.7 = (f32[72,64]{1,0:T(8,128)S(1)}, f32[72,64]{1,0:T(8,128)S(1)}, u32[]{:S(2)}, u32[]{:S(2)}) collective-permute-start(f32[72,64]{1,0:T(8,128)S(1)} %get-tuple-element.74), channel_id=1, source_target_pairs={{0,3},{1,2},{2,1},{3,0},{4,7},{5,6},{6,5},{7,4},{8,11},{9,10},{10,... | collective-permute-start | bytes 55304 | tf_op jit(solution)/shard_map/ppermute | solution.py:489

commit v5 on v4

--- a/solution.py
+++ b/solution.py
@@ -143,18 +143,41 @@
                 g_ref[at : at + SUB, cols] = weight * pick(tiles, index)
 
 
-def ghost_blocks(packets, rows, elements, fscale_ref, nbr_ref, g_ref):
-    halves = [received(packets, row) for row in range(0, rows, SUB)]
+def ghost_tables(fscale_ref, nbr_ref, index_ref, early_ref, late_ref, sent):
+    entry = nbr_ref[...] - fscale_ref.shape[1]
+    way = jnp.maximum(entry, 0) // sent
+    narrow = way // 2
+    index_ref[...] = jnp.where(entry >= 0, narrow * sent + way * (-sent) + entry, 0)
+    flips = []
+    for axis in ("wide", "narrow"):
+        even = lax.axis_size(axis) % 2 == 0
+        flips.append(1 - lax.rem(lax.axis_index(axis), 2) if even else jnp.int32(0))
+    swap = (way & 1) ^ jnp.where(narrow == 0, flips[0], flips[1])
+    weight = jnp.where(entry >= 0, fscale_ref[...], 0.0)
+    early_ref[...] = jnp.where(swap == 0, weight, 0.0)
+    late_ref[...] = jnp.where(swap == 0, 0.0, weight)
+
+
+def ghost_blocks(wide_ref, narrow_ref, rows, index_ref, weight_ref, g_ref, before_ref=None):
+    halves = [
+        jnp.concatenate([wide_ref[row : row + SUB, :], narrow_ref[row : row + SUB, :]], axis=1)
+        for row in range(0, rows, SUB)
+    ]
     for face in range(FACES):
-        for c in range(0, elements, LANES):
+        for c in range(0, index_ref.shape[1], LANES):
             cols = slice(c, c + LANES)
-            entry = nbr_ref[face : face + 1, cols]
-            there = entry >= elements
-            weight = rows8(jnp.where(there, fscale_ref[face : face + 1, cols], 0.0))
-            index = rows8(jnp.where(there, entry - elements, 0))
+            weight = rows8(weight_ref[face : face + 1, cols])
+            index = rows8(index_ref[face : face + 1, cols])
             for row in range(0, rows, SUB):
                 at = rows * face + row
-                g_ref[at : at + SUB, cols] = weight * pick(halves[row // SUB], index)
+                value = weight * lane_take(halves[row // SUB], index)
+                if before_ref is not None:
+                    value = value + before_ref[at : at + SUB, cols]
+                g_ref[at : at + SUB, cols] = value
+
+
+def early_kernel(index_ref, weight_ref, wide_ref, narrow_ref, g_ref):
+    ghost_blocks(wide_ref, narrow_ref, g_ref.shape[0] // FACES, index_ref, weight_ref, g_ref)
 
 
 def first_local_kernel(
@@ -174,31 +197,37 @@
     lead_ref,
     relax_ref,
     source_ref,
+    index_ref,
+    early_ref,
+    late_ref,
     g_ref,
+    *,
+    sent,
 ):
     rows, elements = start_ref.shape
+    ghost_tables(fscale_ref, nbr_ref, index_ref, early_ref, late_ref, sent)
     active = activity(counts_ref, elements)
     source_ref[...] = jnp.where(active, right_ref[...], 0.0)
     relax_ref[...] = jnp.where(active, OMEGA / scale_ref[...], 0.0)
     cdof = csmooth_ref.shape[0]
     lead_ref[rows:, :] = smooth_ref[...]
     for at in range(0, prolong_ref.shape[0], cdof):
-        lead_ref[at : at + cdof, :] = dot(csmooth_ref[...], prolong_ref[at : at + cdof, :])
+        lead_ref[at : at + cdof, :] = dot(csmooth_ref[...], prolong_ref[at : at + cdof, :], HIGHEST)
     lead = lead_ref[...]
-    folded_ref[:, 0:rows] = dot(lead, elem_ref[...])
+    folded_ref[:, 0:rows] = dot(lead, elem_ref[...], HIGHEST)
     for face in range(FACES):
-        folded_ref[:, rows * (face + 1) : rows * (face + 2)] = dot(lead, faces_ref[face])
+        folded_ref[:, rows * (face + 1) : rows * (face + 2)] = dot(lead, faces_ref[face], HIGHEST)
     local_blocks(start_ref, scale_ref, fscale_ref, nbr_ref, g_ref)
-    change = dot(smooth_ref[...], source_ref[...]) - dot(folded_ref[rows:, :], g_ref[...])
+    change = dot(smooth_ref[...], source_ref[...], HIGHEST) - dot(folded_ref[rows:, :], g_ref[...], HIGHEST)
     part_ref[...] = start_ref[...] + relax_ref[...] * change
 
 
 def smoothed_kernel(
-    part_ref, relax_ref, folded_ref, fscale_ref, nbr_ref, send_ref, p0, p1, p2, p3, smoothed_ref, *rest
+    part_ref, relax_ref, folded_ref, index_ref, late_ref, early_ref, send_ref, p0, p1, p2, p3, smoothed_ref, *rest
 ):
     outs, g_ref = rest[:4], rest[4]
     rows, elements = part_ref.shape
-    ghost_blocks((p0, p1, p2, p3), rows, elements, fscale_ref, nbr_ref, g_ref)
+    ghost_blocks(p1, p3, rows, index_ref, late_ref, g_ref, early_ref)
     smoothed_ref[...] = part_ref[...] - relax_ref[...] * dot(folded_ref[rows:, rows:], g_ref[...], HIGHEST)
     pack(send_ref[...], smoothed_ref, outs, rows, elements)
     packets = (p0, p1, p2, p3)
@@ -243,13 +272,13 @@
     rows, elements = smoothed_ref.shape
     coarse = cscale_ref.shape[1]
     local_blocks(smoothed_ref, scale_ref, fscale_ref, nbr_ref, g_ref)
-    value_ref[...] = dot(lead_ref[...], source_ref[...]) - dot(folded_ref[...], g_ref[...])
+    value_ref[...] = dot(lead_ref[...], source_ref[...], HIGHEST) - dot(folded_ref[...], g_ref[...], HIGHEST)
 
     prol_ref[...] = prolong_ref[...].T
     prol = prol_ref[...]
     for block in range(FACES + 1):
         cols = slice(rows * block, rows * (block + 1))
-        spread_ref[:, cols] = dot(folded_ref[rows:, cols], prol)
+        spread_ref[:, cols] = dot(folded_ref[rows:, cols], prol, HIGHEST)
 
     active = activity(counts_ref, elements)
     own = jnp.where(active, slot_ref[...], -1)
@@ -285,15 +314,14 @@
     smoothed_ref,
     relax_ref,
     folded_ref,
-    fscale_ref,
-    nbr_ref,
+    index_ref,
+    late_ref,
+    early_ref,
     slot_ref,
     cscale_ref,
     table_ref,
-    p0,
-    p1,
-    p2,
-    p3,
+    wide_ref,
+    narrow_ref,
     base_ref,
     message_ref,
     g_ref,
@@ -302,7 +330,7 @@
 ):
     rows, elements = smoothed_ref.shape
     coarse = cscale_ref.shape[1]
-    ghost_blocks((p0, p1, p2, p3), rows, elements, fscale_ref, nbr_ref, g_ref)
+    ghost_blocks(wide_ref, narrow_ref, rows, index_ref, late_ref, g_ref, early_ref)
     value = value_ref[...] - dot(folded_ref[:, rows:], g_ref[...])
     base_ref[...] = smoothed_ref[...] + relax_ref[...] * value[rows:, :]
     slot = slot_ref[...]
@@ -597,8 +625,8 @@
         send_list,
     ) = brought[4:]
     first_ghosts = exchange(packets)
-    part, folded, lead, relax, source = call(
-        first_local_kernel,
+    part, folded, lead, relax, source, ghost_index, early_weight, late_weight = call(
+        functools.partial(first_local_kernel, sent=sent),
         (counts,),
         (
             start,
@@ -618,14 +646,24 @@
             ((2 * rows, rows), f32),
             ((1, elements), f32),
             ((rows, elements), f32),
+            ((FACES, elements), i32),
+            ((FACES, elements), f32),
+            ((FACES, elements), f32),
         ],
         [(blocks, elements)],
         flops=2 * blocks * rows * elements,
     )
+    early = call(
+        early_kernel,
+        (),
+        (ghost_index, early_weight, first_ghosts[0], first_ghosts[2]),
+        [((blocks - rows, elements), f32)],
+        flops=blocks * elements,
+    )[0]
     smoothed, *packets = call(
         smoothed_kernel,
         (),
-        (part, relax, folded, face_scale, face_nbr, send_list, *first_ghosts),
+        (part, relax, folded, ghost_index, late_weight, early, send_list, *first_ghosts),
         [((rows, elements), f32)] + [((rows + 3 * SUB, sent), f32)] * 2 + [((rows + SUB, sent), f32)] * 2,
         [(blocks - rows, elements)],
         flops=2 * blocks * rows * elements,
@@ -662,10 +700,17 @@
         [(blocks, elements)],
         flops=4 * blocks * rows * elements,
     )
+    early = call(
+        early_kernel,
+        (),
+        (ghost_index, early_weight, second_ghosts[0], second_ghosts[2]),
+        [((blocks - rows, elements), f32)],
+        flops=blocks * elements,
+    )[0]
     base, message = call(
         functools.partial(restrict_kernel, kids=kids),
         (),
-        (value, smoothed, relax, folded, face_scale, face_nbr, slot, cscale, table, *second_ghosts),
+        (value, smoothed, relax, folded, ghost_index, late_weight, early, slot, cscale, table, second_ghosts[1], second_ghosts[3]),
         [((rows, elements), f32), ((devices, SUB, 2 * coarse), f32)],
         [(blocks - rows, elements)],
         flops=4 * blocks * rows * elements,

time: 38.5 us -> 38.1 us (0.990)
  waiting for transfers between devices: 3.8 us -> 2.11 us
  Pallas kernels: 9.6 us -> 10.8 us
    ppermute x8, waiting for transfers between devices: 3.8 us -> 2.11 us  [exchange(): moved.append(lax.ppermute(packets[base + half], axis, route))]
    pallas_call x6 -> x8, Pallas kernels: 9.6 us -> 10.8 us  [call(): pl.pallas_call(kernel, out_shape=outs, in_specs=[SMEM] * len(scalars) + [...]
  transfers between devices with their start and end apart: 8 -> 8, of which waited for: 3 -> 2; matrix products, arithmetic and copies ran while one was open for 0% -> 0% of each run, Pallas kernels for 7% -> 11%
where the time goes in v5:
time: 38.1 us; the launch traced here: 37.9 us
  blocking collectives  12.4 us (33%)
  starting transfers between devices  11.2 us (29%)
  Pallas kernels  10.8 us (28%)
  waiting for transfers between devices  2.11 us (6%)
  between operations  1.38 us (4%)
    all_to_all x1, blocking collectives, body(): gathered = lax.all_to_all(message, ('wide', 'narrow'), 0, 0)  12.4 us
    ppermute x8, starting transfers between devices, exchange(): moved.append(lax.ppermute(packets[base + half], axis, route))  11.2 us
    pallas_call x8, Pallas kernels, call(): pl.pallas_call(kernel, out_shape=outs, in_specs=[SMEM] * len(scalars) + [...  10.8 us
    ppermute x8, waiting for transfers between devices, exchange(): moved.append(lax.ppermute(packets[base + half], axis, route))  2.11 us
  transfers between devices with their start and end apart: 8, of which 2 were waited for; matrix products, arithmetic and copies ran while one was open for 0% of the time, Pallas kernels for 11%

profile of v5, /device:TPU:0, one launch (start us, length us, event | category | flops | bytes accessed | tf_op | source)
XLA Modules:
  0.0 37.9 jit_solution(269476827989551082)
XLA Ops:
  1.3 1.4 %shard_map.194 = (f32[64,512]{1,0:T(8,128)S(1)}, f32[72,64]{1,0:T(8,128)S(1)}, f32[72,64]{1,0:T(8,128)S(1)}, f32[72,64]{1,0:T(8,128)S(1)}, f32[72,64]{1,0:T(8,12...) custom-call(s32[1]{0:T(128)S(6)} %copy.21.counts_ref, ...), custom_call_target="tpu_custom_call" | custom-call | bytes 445952 | tf_op jit(solution)/shard_map/pallas_call | solution.py:531
  2.7 0.6 %collective-permute-start = (f32[72,64]{1,0:T(8,128)S(1)}, f32[72,64]{1,0:T(8,128)S(1)}, u32[]{:S(2)}, u32[]{:S(2)}) collective-permute-start(f32[72,64]{1,0:T(8,128)S(1)} %get-tuple-element.62), channel_id=1, source_target_pairs={{0,4},{4,0},{8,12},{12,8},{16,20},{20,16},{24,28},{28,24},{1,5},{5... | collective-permute-start | bytes 55304 | tf_op jit(solution)/shard_map/ppermute | solution.py:517
  3.3 2.6 %collective-permute-start.1 = (f32[72,64]{1,0:T(8,128)S(1)}, f32[72,64]{1,0:T(8,128)S(1)}, u32[]{:S(2)}, u32[]{:S(2)}) collective-permute-start(f32[72,64]{1,0:T(8,128)S(1)} %get-tuple-element.63), channel_id=1, source_target_pairs={{0,1},{1,0},{2,3},{3,2},{4,5},{5,4},{6,7},{7,6},{8,9},{9,8},{10,11... | collective-permute-start | bytes 55304 | tf_op jit(solution)/shard_map/ppermute | solution.py:517
  5.9 2.2 %collective-permute-start.2 = (f32[72,64]{1,0:T(8,128)S(1)}, f32[72,64]{1,0:T(8,128)S(1)}, u32[]{:S(2)}, u32[]{:S(2)}) collective-permute-start(f32[72,64]{1,0:T(8,128)S(1)} %get-tuple-element.65), channel_id=1, source_target_pairs={{0,28},{4,8},{8,4},{12,16},{16,12},{20,24},{24,20},{28,0},{1,29},{... | collective-permute-start | bytes 55304 | tf_op jit(solution)/shard_map/ppermute | solution.py:517
  8.1 2.5 %collective-permute-start.3 = (f32[72,64]{1,0:T(8,128)S(1)}, f32[72,64]{1,0:T(8,128)S(1)}, u32[]{:S(2)}, u32[]{:S(2)}) collective-permute-start(f32[72,64]{1,0:T(8,128)S(1)} %get-tuple-element.66), channel_id=1, source_target_pairs={{0,3},{1,2},{2,1},{3,0},{4,7},{5,6},{6,5},{7,4},{8,11},{9,10},{10,... | collective-permute-start | bytes 55304 | tf_op jit(solution)/shard_map/ppermute | solution.py:517
  10.6 1.6 %shard_map.195 = (f32[64,512]{1,0:T(8,128)S(1)}, f32[128,448]{1,0:T(8,128)S(1)}, f32[128,64]{1,0:T(8,128)S(1)}, f32[1,512]{1,0:T(1,128)S(1)}, f32[64,512]{1,0:T(...) custom-call(s32[1]{0:T(128)S(6)} %copy.21.counts_ref, ...), custom_call_target="tpu_custom_call" | custom-call | flops 29360128 | bytes 436480 | tf_op jit(solution)/shard_map/pallas_call | solution.py:531
  12.2 0.0 collective-permute-done.wide_ref.p0
  12.2 0.0 collective-permute-done.1.narrow_ref.p2
  12.2 0.4 %shard_map.196.early_ref = f32[384,512]{1,0:T(8,128)S(1)} custom-call(s32[6,512]{1,0:T(8,128)S(1)} %get-tuple-element.59.index_ref, f32[6,512]{1,0:T(8,128)S(1)} %get-tuple-element.61.weight_ref, f32[72,64]{1,0:T(8,128)S(1)} %collective-permute-done.wide_ref.p0, f32[72,64]{1,0:T(8,128)S(1)} %collective-permute-done.1.narrow_ref.p2), custom_call_target="tpu_custom_call" | custom-call | flops 229376 | bytes 61440 | tf_op jit(solution)/shard_map/pallas_call | solution.py:531
  12.7 0.0 collective-permute-done.2.p1
  12.7 1.2 %collective-permute-done.3.p3 = f32[72,64]{1,0:T(8,128)S(1)} collective-permute-done((f32[72,64]{1,0:T(8,128)S(1)}, f32[72,64]{1,0:T(8,128)S(1)}, u32[]{:S(2)}, u32[]{:S(2)}) %collective-permute-start.3) | collective-permute-done | bytes 18464 | tf_op jit(solution)/shard_map/ppermute | solution.py:517
  13.9 1.2 %shard_map.197 = (f32[64,512]{1,0:T(8,128)S(1)}, f32[88,64]{1,0:T(8,128)S(1)}, f32[88,64]{1,0:T(8,128)S(1)}, f32[72,64]{1,0:T(8,128)S(1)}, f32[72,64]{1,0:T(8,128)S(1)}) custom-call(f32[64,512]{1,0:T(8,128)S(1)} %get-tuple-element.56.part_ref, f32[1,512]{1,0:T(1,128)S(1)} %get-tuple-element.57.relax_ref, f32[128,448]{1,0:T(8,128)S(1)} %get-tuple-element.58.folded_ref, ...), custom_call_target="tpu_custom_call" | custom-call | flops 29360128 | bytes 1248256 | tf_op jit(solution)/shard_map/pallas_call | solution.py:531
  15.0 0.0 collective-permute-start.4
  15.1 0.6 %collective-permute-start.6 = (f32[88,64]{1,0:T(8,128)S(1)}, f32[88,64]{1,0:T(8,128)S(1)}, u32[]{:S(2)}, u32[]{:S(2)}) collective-permute-start(f32[88,64]{1,0:T(8,128)S(1)} %get-tuple-element.79), channel_id=1, source_target_pairs={{0,28},{4,8},{8,4},{12,16},{16,12},{20,24},{24,20},{28,0},{1,29},{... | collective-permute-start | bytes 67592 | tf_op jit(solution)/shard_map/ppermute | solution.py:517
  15.7 0.0 collective-permute-start.5
  15.7 2.6 %collective-permute-start.7 = (f32[72,64]{1,0:T(8,128)S(1)}, f32[72,64]{1,0:T(8,128)S(1)}, u32[]{:S(2)}, u32[]{:S(2)}) collective-permute-start(f32[72,64]{1,0:T(8,128)S(1)} %get-tuple-element.80), channel_id=1, source_target_pairs={{0,3},{1,2},{2,1},{3,0},{4,7},{5,6},{6,5},{7,4},{8,11},{9,10},{10,... | collective-permute-start | bytes 55304 | tf_op jit(solution)/shard_map/ppermute | solution.py:517
  18.4 1.8 %shard_map.198 = (f32[128,512]{1,0:T(8,128)S(1)}, f32[64,448]{1,0:T(8,128)S(1)}, f32[64,64]{1,0:T(8,128)S(1)}, s32[8,512]{1,0:T(8,128)S(1)}, s32[8,512]{1,0:T(8,...) custom-call(s32[1]{0:T(128)S(6)} %copy.21.counts_ref, f32[64,512]{1,0:T(8,128)S(1)} %get-tuple-element.67.smoothed_ref, ...), custom_call_target="tpu_custom_call" | custom-call | flops 58720256 | bytes 646656 | tf_op jit(solution)/shard_map/pallas_call | solution.py:531
  20.2 0.0 collective-permute-done.5.narrow_ref.q2
  20.2 0.0 collective-permute-done.4.wide_ref.q0
  20.3 0.4 %shard_map.199.early_ref = f32[384,512]{1,0:T(8,128)S(1)} custom-call(s32[6,512]{1,0:T(8,128)S(1)} %get-tuple-element.59.index_ref, f32[6,512]{1,0:T(8,128)S(1)} %get-tuple-element.61.weight_ref, f32[88,64]{1,0:T(8,128)S(1)} %collective-permute-done.4.wide_ref.q0, f32[72,64]{1,0:T(8,128)S(1)} %collective-permute-done.5.narrow_ref.q2), custom_call_target="tpu_custom_call" | custom-call | flops 229376 | bytes 65536 | tf_op jit(solution)/shard_map/pallas_call | solution.py:531
  20.7 0.9 %collective-permute-done.7.narrow_ref.q3 = f32[72,64]{1,0:T(8,128)S(1)} collective-permute-done((f32[72,64]{1,0:T(8,128)S(1)}, f32[72,64]{1,0:T(8,128)S(1)}, u32[]{:S(2)}, u32[]{:S(2)}) %collective-permute-start.7) | collective-permute-done | bytes 18464 | tf_op jit(solution)/shard_map/ppermute | solution.py:517
  21.5 0.0 collective-permute-done.6.wide_ref.q1
  21.5 1.1 %shard_map.200 = (f32[64,512]{1,0:T(8,128)S(1)}, f32[32,8,128]{2,1,0:T(8,128)S(1)}) custom-call(f32[128,512]{1,0:T(8,128)S(1)} %get-tuple-element.75.value_ref, f32[64,512]{1,0:T(8,128)S(1)} %get-tuple-element.67.smoothed_ref, f32[1,512]{1,0:T(1,128)S(1)} %get-tuple-element.57.relax_ref, f32[128,448]{1,0:T(8,128)S(1)} %get-tuple-element.58.folded_ref, ...), custom_call_target="tpu_custom_call" | custom-call | flops 58720256 | bytes 1480960 | tf_op jit(solution)/shard_map/pallas_call | solution.py:531
  22.6 12.4 %all_to_all.5.message_ref = f32[32,8,128]{2,1,0:T(8,128)S(1)} all-to-all(f32[32,8,128]{2,1,0:T(8,128)S(1)} %get-tuple-element.81), channel_id=1, replica_groups=mesh['wide'=8,'narrow'=4] {'wide','narrow'}, dimensions={0} | all-to-all | bytes 262144 | tf_op jit(solution)/shard_map/all_to_all | solution.py:718
  35.0 2.9 %shard_map.201 = (f32[64,512]{1,0:T(8,128)}, f32[8,64]{1,0:T(8,128)}) custom-call(f32[32,8,128]{2,1,0:T(8,128)S(1)} %all_to_all.5.message_ref, f32[64,512]{1,0:T(8,128)S(1)} %get-tuple-element.82.base_ref, f32[1,512]{1,0:T(1,128)S(1)} %get-tuple-element.57.relax_ref, f32[64,64]{1,0:T(8,128)S(1)} %get-tuple-element.83.prol_ref, ...), custom_call_target="tpu_custom_call" | custom-call | flops 29360128 | bytes 603648 | tf_op jit(solution)/shard_map/pallas_call | solution.py:531
Async XLA Ops:
  2.7 9.5 %collective-permute-start = (f32[72,64]{1,0:T(8,128)S(1)}, f32[72,64]{1,0:T(8,128)S(1)}, u32[]{:S(2)}, u32[]{:S(2)}) collective-permute-start(f32[72,64]{1,0:T(8,128)S(1)} %get-tuple-element.62), channel_id=1, source_target_pairs={{0,4},{4,0},{8,12},{12,8},{16,20},{20,16},{24,28},{28,24},{1,5},{5... | collective-permute-start | bytes 55304 | tf_op jit(solution)/shard_map/ppermute | solution.py:517
  3.3 8.9 %collective-permute-start.1 = (f32[72,64]{1,0:T(8,128)S(1)}, f32[72,64]{1,0:T(8,128)S(1)}, u32[]{:S(2)}, u32[]{:S(2)}) collective-permute-start(f32[72,64]{1,0:T(8,128)S(1)} %get-tuple-element.63), channel_id=1, source_target_pairs={{0,1},{1,0},{2,3},{3,2},{4,5},{5,4},{6,7},{7,6},{8,9},{9,8},{10,11... | collective-permute-start | bytes 55304 | tf_op jit(solution)/shard_map/ppermute | solution.py:517
  5.9 6.7 %collective-permute-start.2 = (f32[72,64]{1,0:T(8,128)S(1)}, f32[72,64]{1,0:T(8,128)S(1)}, u32[]{:S(2)}, u32[]{:S(2)}) collective-permute-start(f32[72,64]{1,0:T(8,128)S(1)} %get-tuple-element.65), channel_id=1, source_target_pairs={{0,28},{4,8},{8,4},{12,16},{16,12},{20,24},{24,20},{28,0},{1,29},{... | collective-permute-start | bytes 55304 | tf_op jit(solution)/shard_map/ppermute | solution.py:517
  8.1 5.8 %collective-permute-start.3 = (f32[72,64]{1,0:T(8,128)S(1)}, f32[72,64]{1,0:T(8,128)S(1)}, u32[]{:S(2)}, u32[]{:S(2)}) collective-permute-start(f32[72,64]{1,0:T(8,128)S(1)} %get-tuple-element.66), channel_id=1, source_target_pairs={{0,3},{1,2},{2,1},{3,0},{4,7},{5,6},{6,5},{7,4},{8,11},{9,10},{10,... | collective-permute-start | bytes 55304 | tf_op jit(solution)/shard_map/ppermute | solution.py:517
  15.0 5.2 %collective-permute-start.4 = (f32[88,64]{1,0:T(8,128)S(1)}, f32[88,64]{1,0:T(8,128)S(1)}, u32[]{:S(2)}, u32[]{:S(2)}) collective-permute-start(f32[88,64]{1,0:T(8,128)S(1)} %get-tuple-element.76), channel_id=1, source_target_pairs={{0,4},{4,0},{8,12},{12,8},{16,20},{20,16},{24,28},{28,24},{1,5},{5... | collective-permute-start | bytes 67592 | tf_op jit(solution)/shard_map/ppermute | solution.py:517
  15.1 6.5 %collective-permute-start.6 = (f32[88,64]{1,0:T(8,128)S(1)}, f32[88,64]{1,0:T(8,128)S(1)}, u32[]{:S(2)}, u32[]{:S(2)}) collective-permute-start(f32[88,64]{1,0:T(8,128)S(1)} %get-tuple-element.79), channel_id=1, source_target_pairs={{0,28},{4,8},{8,4},{12,16},{16,12},{20,24},{24,20},{28,0},{1,29},{... | collective-permute-start | bytes 67592 | tf_op jit(solution)/shard_map/ppermute | solution.py:517
  15.7 4.5 %collective-permute-start.5 = (f32[72,64]{1,0:T(8,128)S(1)}, f32[72,64]{1,0:T(8,128)S(1)}, u32[]{:S(2)}, u32[]{:S(2)}) collective-permute-start(f32[72,64]{1,0:T(8,128)S(1)} %get-tuple-element.77), channel_id=1, source_target_pairs={{0,1},{1,0},{2,3},{3,2},{4,5},{5,4},{6,7},{7,6},{8,9},{9,8},{10,11... | collective-permute-start | bytes 55304 | tf_op jit(solution)/shard_map/ppermute | solution.py:517
  15.7 5.8 %collective-permute-start.7 = (f32[72,64]{1,0:T(8,128)S(1)}, f32[72,64]{1,0:T(8,128)S(1)}, u32[]{:S(2)}, u32[]{:S(2)}) collective-permute-start(f32[72,64]{1,0:T(8,128)S(1)} %get-tuple-element.80), channel_id=1, source_target_pairs={{0,3},{1,2},{2,1},{3,0},{4,7},{5,6},{6,5},{7,4},{8,11},{9,10},{10,... | collective-permute-start | bytes 55304 | tf_op jit(solution)/shard_map/ppermute | solution.py:517

commit v6 on v5

--- a/solution.py
+++ b/solution.py
@@ -218,7 +218,7 @@
     for face in range(FACES):
         folded_ref[:, rows * (face + 1) : rows * (face + 2)] = dot(lead, faces_ref[face], HIGHEST)
     local_blocks(start_ref, scale_ref, fscale_ref, nbr_ref, g_ref)
-    change = dot(smooth_ref[...], source_ref[...], HIGHEST) - dot(folded_ref[rows:, :], g_ref[...], HIGHEST)
+    change = dot(smooth_ref[...], source_ref[...]) - dot(folded_ref[rows:, :], g_ref[...])
     part_ref[...] = start_ref[...] + relax_ref[...] * change
 
 
@@ -272,13 +272,13 @@
     rows, elements = smoothed_ref.shape
     coarse = cscale_ref.shape[1]
     local_blocks(smoothed_ref, scale_ref, fscale_ref, nbr_ref, g_ref)
-    value_ref[...] = dot(lead_ref[...], source_ref[...], HIGHEST) - dot(folded_ref[...], g_ref[...], HIGHEST)
+    value_ref[...] = dot(lead_ref[...], source_ref[...]) - dot(folded_ref[...], g_ref[...])
 
     prol_ref[...] = prolong_ref[...].T
     prol = prol_ref[...]
     for block in range(FACES + 1):
         cols = slice(rows * block, rows * (block + 1))
-        spread_ref[:, cols] = dot(folded_ref[rows:, cols], prol, HIGHEST)
+        spread_ref[:, cols] = dot(folded_ref[rows:, cols], prol)
 
     active = activity(counts_ref, elements)
     own = jnp.where(active, slot_ref[...], -1)
@@ -379,12 +379,6 @@
     for side in range(2):
         found[2 * side - 1, -1], found[2 * side - 1, 1] = in_order("narrow", one[side], two[side])
     return found
-
-
-def paired(pieces):
-    if len(pieces) % 2:
-        pieces = pieces + [pieces[0]]
-    return [jnp.concatenate(pieces[i : i + 2], axis=1) for i in range(0, len(pieces), 2)]
 
 
 def finish_kernel(
@@ -437,47 +431,67 @@
     ranks = {}
     for rank, (w, n) in reversed(list(enumerate(offsets))):
         ranks[w % wides, n % narrows] = rank
-    beside = [
-        [ranks[(w + dw) % wides, (n + dn) % narrows] * coarse for dw, dn in offsets[1:5]] for w, n in offsets[: counts[2]]
-    ]
-    messages = [message_ref[part] for part in parts]
-    first = paired([message[:, :coarse] for message in messages])
-    extras = paired([message[:, coarse:] for message in messages])
-    lists = [rows8(extra[FACES : FACES + 1]) for extra in extras]
-    entries = paired([tables[offset] for offset in offsets[: counts[2]]])
+    beside = [[ranks[(w + dw) % wides, (n + dn) % narrows] for dw, dn in offsets[1:5]] for w, n in offsets[: counts[2]]]
     left = lax.broadcasted_iota(jnp.int32, (SUB, LANES), 1) < coarse
-    indices = []
-    for t, entry in enumerate(entries):
-        pair = [2 * t, min(2 * t + 1, counts[2] - 1)]
+    straight = [message_ref[part] for part in parts]
+    turned = [pltpu.roll(message, coarse, 1) for message in straight]
+
+    def side_by_side(low, high, members, limit):
+        kept = [rank if rank < limit else 0 for rank in members]
+        kept += kept[:1] * (len(kept) % 2)
+        return [jnp.where(left, low[a], high[b]) for a, b in zip(kept[::2], kept[1::2])]
+
+    first, extras, around, indices = [], [], [], []
+    for t in range(-(-counts[2] // 2)):
+        pair = (2 * t, min(2 * t + 1, counts[2] - 1))
+        first += side_by_side(straight, turned, pair, len(parts))
+        extras += side_by_side(turned, straight, pair, len(parts))
+        members = []
+        for one in pair:
+            for rank in (one, *beside[one]):
+                if rank not in members:
+                    members.append(rank)
+        around.append(members)
+        lists = [
+            rows8(extra[FACES : FACES + 1]) for extra in side_by_side(turned, straight, members, len(parts))
+        ]
+        spots = [[members.index(rank) * coarse for rank in (one, *beside[one])] for one in pair]
+        spots = [jnp.where(left, one, two) for one, two in zip(*spots)]
+        entry = jnp.concatenate([tables[offsets[one]] for one in pair], axis=1)
         entry = jnp.maximum(entry.astype(jnp.int32), 0)
         remote = entry - coarse
-        base = [jnp.where(left, beside[pair[0]][d], beside[pair[1]][d]) for d in range(4)]
         owner = jnp.where(
             remote < 2 * sent,
-            jnp.where(remote < sent, base[0], base[1]),
-            jnp.where(remote < 3 * sent, base[2], base[3]),
+            jnp.where(remote < sent, spots[1], spots[2]),
+            jnp.where(remote < 3 * sent, spots[3], spots[4]),
         )
-        home = jnp.where(left, pair[0] * coarse, pair[1] * coarse)
         there = pick(lists, owner + jnp.maximum(remote, 0)).astype(jnp.int32)
-        indices.append(jnp.where(remote < 0, home + entry, owner + there))
-
-    current = first
+        indices.append(jnp.where(remote < 0, spots[0] + entry, owner + there))
+
+    low, high, current = straight, turned, first
     for count in (counts[2], counts[1]):
-        following = []
         tiles = -(-count // 2)
         for t in range(tiles):
+            members = around[t]
+            if 2 * t + 1 >= count:
+                members = members[: 1 + len(set(beside[2 * t]) - {2 * t})]
+            seen = side_by_side(low, high, members, len(low))
             for face in range(FACES):
                 row = SUB - FACES + face
-                chosen = pick(current, rows8(indices[t][row : row + 1]))
+                chosen = pick(seen, rows8(indices[t][row : row + 1]))
                 cg_ref[face * cdof : (face + 1) * cdof, t * LANES : (t + 1) * LANES] = (
                     rows8(extras[t][face : face + 1]) * chosen
                 )
         pulled = dot(folded, cg_ref[:, : tiles * LANES])
         inner = dot(own, jnp.concatenate(current[:tiles], axis=1))
+        following = []
         for t in range(tiles):
             cols = slice(t * LANES, (t + 1) * LANES)
             following.append(current[t] + first[t] - inner[:, cols] - pulled[:, cols])
         current = following
+        flipped = [pltpu.roll(tile, coarse, 1) for tile in current]
+        low = [tile for both in zip(current, flipped) for tile in both]
+        high = [tile for both in zip(flipped, current) for tile in both]
     correction_ref[...] = current[0][:, :coarse]
 
     for c in range(0, elements, LANES):

time: 38.1 us -> 37.6 us (0.987)
  Pallas kernels: 10.8 us -> 9.83 us
  waiting for transfers between devices: 2.11 us -> 2.65 us
    pallas_call x8, Pallas kernels: 10.8 us -> 9.83 us  [call(): pl.pallas_call(kernel, out_shape=outs, in_specs=[SMEM] * len(scalars) + [...]
    ppermute x8, waiting for transfers between devices: 2.11 us -> 2.65 us  [exchange(): moved.append(lax.ppermute(packets[base + half], axis, route))]
  transfers between devices with their start and end apart: 8 -> 8, of which waited for: 2 -> 2; matrix products, arithmetic and copies ran while one was open for 0% -> 0% of each run, Pallas kernels for 11% -> 10%
where the time goes in v6:
time: 37.6 us; the launch traced here: 37.5 us
  blocking collectives  12.4 us (33%)
  starting transfers between devices  11.2 us (30%)
  Pallas kernels  9.83 us (26%)
  waiting for transfers between devices  2.65 us (7%)
  between operations  1.38 us (4%)
    all_to_all x1, blocking collectives, body(): gathered = lax.all_to_all(message, ('wide', 'narrow'), 0, 0)  12.4 us
    ppermute x8, starting transfers between devices, exchange(): moved.append(lax.ppermute(packets[base + half], axis, route))  11.2 us
    pallas_call x8, Pallas kernels, call(): pl.pallas_call(kernel, out_shape=outs, in_specs=[SMEM] * len(scalars) + [...  9.83 us
    ppermute x8, waiting for transfers between devices, exchange(): moved.append(lax.ppermute(packets[base + half], axis, route))  2.65 us
  transfers between devices with their start and end apart: 8, of which 2 were waited for; matrix products, arithmetic and copies ran while one was open for 0% of the time, Pallas kernels for 10%

profile of v6, /device:TPU:0, one launch (start us, length us, event | category | flops | bytes accessed | tf_op | source)
XLA Modules:
  0.0 37.5 jit_solution(15209184028782587501)
XLA Ops:
  1.3 1.4 %shard_map.194 = (f32[64,512]{1,0:T(8,128)S(1)}, f32[72,64]{1,0:T(8,128)S(1)}, f32[72,64]{1,0:T(8,128)S(1)}, f32[72,64]{1,0:T(8,128)S(1)}, f32[72,64]{1,0:T(8,12...) custom-call(s32[1]{0:T(128)S(6)} %copy.21.counts_ref, ...), custom_call_target="tpu_custom_call" | custom-call | bytes 445952 | tf_op jit(solution)/shard_map/pallas_call | solution.py:545
  2.7 0.6 %collective-permute-start = (f32[72,64]{1,0:T(8,128)S(1)}, f32[72,64]{1,0:T(8,128)S(1)}, u32[]{:S(2)}, u32[]{:S(2)}) collective-permute-start(f32[72,64]{1,0:T(8,128)S(1)} %get-tuple-element.62), channel_id=1, source_target_pairs={{0,4},{4,0},{8,12},{12,8},{16,20},{20,16},{24,28},{28,24},{1,5},{5... | collective-permute-start | bytes 55304 | tf_op jit(solution)/shard_map/ppermute | solution.py:531
  3.3 2.6 %collective-permute-start.1 = (f32[72,64]{1,0:T(8,128)S(1)}, f32[72,64]{1,0:T(8,128)S(1)}, u32[]{:S(2)}, u32[]{:S(2)}) collective-permute-start(f32[72,64]{1,0:T(8,128)S(1)} %get-tuple-element.63), channel_id=1, source_target_pairs={{0,1},{1,0},{2,3},{3,2},{4,5},{5,4},{6,7},{7,6},{8,9},{9,8},{10,11... | collective-permute-start | bytes 55304 | tf_op jit(solution)/shard_map/ppermute | solution.py:531
  5.9 2.2 %collective-permute-start.2 = (f32[72,64]{1,0:T(8,128)S(1)}, f32[72,64]{1,0:T(8,128)S(1)}, u32[]{:S(2)}, u32[]{:S(2)}) collective-permute-start(f32[72,64]{1,0:T(8,128)S(1)} %get-tuple-element.65), channel_id=1, source_target_pairs={{0,28},{4,8},{8,4},{12,16},{16,12},{20,24},{24,20},{28,0},{1,29},{... | collective-permute-start | bytes 55304 | tf_op jit(solution)/shard_map/ppermute | solution.py:531
  8.1 2.5 %collective-permute-start.3 = (f32[72,64]{1,0:T(8,128)S(1)}, f32[72,64]{1,0:T(8,128)S(1)}, u32[]{:S(2)}, u32[]{:S(2)}) collective-permute-start(f32[72,64]{1,0:T(8,128)S(1)} %get-tuple-element.66), channel_id=1, source_target_pairs={{0,3},{1,2},{2,1},{3,0},{4,7},{5,6},{6,5},{7,4},{8,11},{9,10},{10,... | collective-permute-start | bytes 55304 | tf_op jit(solution)/shard_map/ppermute | solution.py:531
  10.6 1.5 %shard_map.195 = (f32[64,512]{1,0:T(8,128)S(1)}, f32[128,448]{1,0:T(8,128)S(1)}, f32[128,64]{1,0:T(8,128)S(1)}, f32[1,512]{1,0:T(1,128)S(1)}, f32[64,512]{1,0:T(...) custom-call(s32[1]{0:T(128)S(6)} %copy.21.counts_ref, ...), custom_call_target="tpu_custom_call" | custom-call | flops 29360128 | bytes 436480 | tf_op jit(solution)/shard_map/pallas_call | solution.py:545
  12.1 0.0 collective-permute-done.wide_ref.p0
  12.1 0.0 collective-permute-done.1.narrow_ref.p2
  12.1 0.4 %shard_map.196.early_ref = f32[384,512]{1,0:T(8,128)S(1)} custom-call(s32[6,512]{1,0:T(8,128)S(1)} %get-tuple-element.59.index_ref, f32[6,512]{1,0:T(8,128)S(1)} %get-tuple-element.61.weight_ref, f32[72,64]{1,0:T(8,128)S(1)} %collective-permute-done.wide_ref.p0, f32[72,64]{1,0:T(8,128)S(1)} %collective-permute-done.1.narrow_ref.p2), custom_call_target="tpu_custom_call" | custom-call | flops 229376 | bytes 61440 | tf_op jit(solution)/shard_map/pallas_call | solution.py:545
  12.6 0.0 collective-permute-done.2.p1
  12.6 1.3 %collective-permute-done.3.p3 = f32[72,64]{1,0:T(8,128)S(1)} collective-permute-done((f32[72,64]{1,0:T(8,128)S(1)}, f32[72,64]{1,0:T(8,128)S(1)}, u32[]{:S(2)}, u32[]{:S(2)}) %collective-permute-start.3) | collective-permute-done | bytes 18464 | tf_op jit(solution)/shard_map/ppermute | solution.py:531
  13.9 1.2 %shard_map.197 = (f32[64,512]{1,0:T(8,128)S(1)}, f32[88,64]{1,0:T(8,128)S(1)}, f32[88,64]{1,0:T(8,128)S(1)}, f32[72,64]{1,0:T(8,128)S(1)}, f32[72,64]{1,0:T(8,128)S(1)}) custom-call(f32[64,512]{1,0:T(8,128)S(1)} %get-tuple-element.56.part_ref, f32[1,512]{1,0:T(1,128)S(1)} %get-tuple-element.57.relax_ref, f32[128,448]{1,0:T(8,128)S(1)} %get-tuple-element.58.folded_ref, ...), custom_call_target="tpu_custom_call" | custom-call | flops 29360128 | bytes 1248256 | tf_op jit(solution)/shard_map/pallas_call | solution.py:545
  15.0 0.0 collective-permute-start.4
  15.1 0.6 %collective-permute-start.6 = (f32[88,64]{1,0:T(8,128)S(1)}, f32[88,64]{1,0:T(8,128)S(1)}, u32[]{:S(2)}, u32[]{:S(2)}) collective-permute-start(f32[88,64]{1,0:T(8,128)S(1)} %get-tuple-element.79), channel_id=1, source_target_pairs={{0,28},{4,8},{8,4},{12,16},{16,12},{20,24},{24,20},{28,0},{1,29},{... | collective-permute-start | bytes 67592 | tf_op jit(solution)/shard_map/ppermute | solution.py:531
  15.7 0.0 collective-permute-start.5
  15.7 2.6 %collective-permute-start.7 = (f32[72,64]{1,0:T(8,128)S(1)}, f32[72,64]{1,0:T(8,128)S(1)}, u32[]{:S(2)}, u32[]{:S(2)}) collective-permute-start(f32[72,64]{1,0:T(8,128)S(1)} %get-tuple-element.80), channel_id=1, source_target_pairs={{0,3},{1,2},{2,1},{3,0},{4,7},{5,6},{6,5},{7,4},{8,11},{9,10},{10,... | collective-permute-start | bytes 55304 | tf_op jit(solution)/shard_map/ppermute | solution.py:531
  18.4 1.4 %shard_map.198 = (f32[128,512]{1,0:T(8,128)S(1)}, f32[64,448]{1,0:T(8,128)S(1)}, f32[64,64]{1,0:T(8,128)S(1)}, s32[8,512]{1,0:T(8,128)S(1)}, s32[8,512]{1,0:T(8,...) custom-call(s32[1]{0:T(128)S(6)} %copy.21.counts_ref, f32[64,512]{1,0:T(8,128)S(1)} %get-tuple-element.67.smoothed_ref, ...), custom_call_target="tpu_custom_call" | custom-call | flops 58720256 | bytes 646656 | tf_op jit(solution)/shard_map/pallas_call | solution.py:545
  19.8 0.0 collective-permute-done.5.narrow_ref.q2
  19.8 0.0 collective-permute-done.4.wide_ref.q0
  19.8 0.4 %shard_map.199.early_ref = f32[384,512]{1,0:T(8,128)S(1)} custom-call(s32[6,512]{1,0:T(8,128)S(1)} %get-tuple-element.59.index_ref, f32[6,512]{1,0:T(8,128)S(1)} %get-tuple-element.61.weight_ref, f32[88,64]{1,0:T(8,128)S(1)} %collective-permute-done.4.wide_ref.q0, f32[72,64]{1,0:T(8,128)S(1)} %collective-permute-done.5.narrow_ref.q2), custom_call_target="tpu_custom_call" | custom-call | flops 229376 | bytes 65536 | tf_op jit(solution)/shard_map/pallas_call | solution.py:545
  20.2 1.3 %collective-permute-done.7.narrow_ref.q3 = f32[72,64]{1,0:T(8,128)S(1)} collective-permute-done((f32[72,64]{1,0:T(8,128)S(1)}, f32[72,64]{1,0:T(8,128)S(1)}, u32[]{:S(2)}, u32[]{:S(2)}) %collective-permute-start.7) | collective-permute-done | bytes 18464 | tf_op jit(solution)/shard_map/ppermute | solution.py:531
  21.5 0.0 collective-permute-done.6.wide_ref.q1
  21.5 1.1 %shard_map.200 = (f32[64,512]{1,0:T(8,128)S(1)}, f32[32,8,128]{2,1,0:T(8,128)S(1)}) custom-call(f32[128,512]{1,0:T(8,128)S(1)} %get-tuple-element.75.value_ref, f32[64,512]{1,0:T(8,128)S(1)} %get-tuple-element.67.smoothed_ref, f32[1,512]{1,0:T(1,128)S(1)} %get-tuple-element.57.relax_ref, f32[128,448]{1,0:T(8,128)S(1)} %get-tuple-element.58.folded_ref, ...), custom_call_target="tpu_custom_call" | custom-call | flops 58720256 | bytes 1480960 | tf_op jit(solution)/shard_map/pallas_call | solution.py:545
  22.6 12.4 %all_to_all.5.message_ref = f32[32,8,128]{2,1,0:T(8,128)S(1)} all-to-all(f32[32,8,128]{2,1,0:T(8,128)S(1)} %get-tuple-element.81), channel_id=1, replica_groups=mesh['wide'=8,'narrow'=4] {'wide','narrow'}, dimensions={0} | all-to-all | bytes 262144 | tf_op jit(solution)/shard_map/all_to_all | solution.py:732
  35.0 2.4 %shard_map.201 = (f32[64,512]{1,0:T(8,128)}, f32[8,64]{1,0:T(8,128)}) custom-call(f32[32,8,128]{2,1,0:T(8,128)S(1)} %all_to_all.5.message_ref, f32[64,512]{1,0:T(8,128)S(1)} %get-tuple-element.82.base_ref, f32[1,512]{1,0:T(1,128)S(1)} %get-tuple-element.57.relax_ref, f32[64,64]{1,0:T(8,128)S(1)} %get-tuple-element.83.prol_ref, ...), custom_call_target="tpu_custom_call" | custom-call | flops 29360128 | bytes 603648 | tf_op jit(solution)/shard_map/pallas_call | solution.py:545
Async XLA Ops:
  2.7 9.4 %collective-permute-start = (f32[72,64]{1,0:T(8,128)S(1)}, f32[72,64]{1,0:T(8,128)S(1)}, u32[]{:S(2)}, u32[]{:S(2)}) collective-permute-start(f32[72,64]{1,0:T(8,128)S(1)} %get-tuple-element.62), channel_id=1, source_target_pairs={{0,4},{4,0},{8,12},{12,8},{16,20},{20,16},{24,28},{28,24},{1,5},{5... | collective-permute-start | bytes 55304 | tf_op jit(solution)/shard_map/ppermute | solution.py:531
  3.3 8.8 %collective-permute-start.1 = (f32[72,64]{1,0:T(8,128)S(1)}, f32[72,64]{1,0:T(8,128)S(1)}, u32[]{:S(2)}, u32[]{:S(2)}) collective-permute-start(f32[72,64]{1,0:T(8,128)S(1)} %get-tuple-element.63), channel_id=1, source_target_pairs={{0,1},{1,0},{2,3},{3,2},{4,5},{5,4},{6,7},{7,6},{8,9},{9,8},{10,11... | collective-permute-start | bytes 55304 | tf_op jit(solution)/shard_map/ppermute | solution.py:531
  5.9 6.6 %collective-permute-start.2 = (f32[72,64]{1,0:T(8,128)S(1)}, f32[72,64]{1,0:T(8,128)S(1)}, u32[]{:S(2)}, u32[]{:S(2)}) collective-permute-start(f32[72,64]{1,0:T(8,128)S(1)} %get-tuple-element.65), channel_id=1, source_target_pairs={{0,28},{4,8},{8,4},{12,16},{16,12},{20,24},{24,20},{28,0},{1,29},{... | collective-permute-start | bytes 55304 | tf_op jit(solution)/shard_map/ppermute | solution.py:531
  8.1 5.8 %collective-permute-start.3 = (f32[72,64]{1,0:T(8,128)S(1)}, f32[72,64]{1,0:T(8,128)S(1)}, u32[]{:S(2)}, u32[]{:S(2)}) collective-permute-start(f32[72,64]{1,0:T(8,128)S(1)} %get-tuple-element.66), channel_id=1, source_target_pairs={{0,3},{1,2},{2,1},{3,0},{4,7},{5,6},{6,5},{7,4},{8,11},{9,10},{10,... | collective-permute-start | bytes 55304 | tf_op jit(solution)/shard_map/ppermute | solution.py:531
  15.0 4.8 %collective-permute-start.4 = (f32[88,64]{1,0:T(8,128)S(1)}, f32[88,64]{1,0:T(8,128)S(1)}, u32[]{:S(2)}, u32[]{:S(2)}) collective-permute-start(f32[88,64]{1,0:T(8,128)S(1)} %get-tuple-element.76), channel_id=1, source_target_pairs={{0,4},{4,0},{8,12},{12,8},{16,20},{20,16},{24,28},{28,24},{1,5},{5... | collective-permute-start | bytes 67592 | tf_op jit(solution)/shard_map/ppermute | solution.py:531
  15.1 6.5 %collective-permute-start.6 = (f32[88,64]{1,0:T(8,128)S(1)}, f32[88,64]{1,0:T(8,128)S(1)}, u32[]{:S(2)}, u32[]{:S(2)}) collective-permute-start(f32[88,64]{1,0:T(8,128)S(1)} %get-tuple-element.79), channel_id=1, source_target_pairs={{0,28},{4,8},{8,4},{12,16},{16,12},{20,24},{24,20},{28,0},{1,29},{... | collective-permute-start | bytes 67592 | tf_op jit(solution)/shard_map/ppermute | solution.py:531
  15.7 4.1 %collective-permute-start.5 = (f32[72,64]{1,0:T(8,128)S(1)}, f32[72,64]{1,0:T(8,128)S(1)}, u32[]{:S(2)}, u32[]{:S(2)}) collective-permute-start(f32[72,64]{1,0:T(8,128)S(1)} %get-tuple-element.77), channel_id=1, source_target_pairs={{0,1},{1,0},{2,3},{3,2},{4,5},{5,4},{6,7},{7,6},{8,9},{9,8},{10,11... | collective-permute-start | bytes 55304 | tf_op jit(solution)/shard_map/ppermute | solution.py:531
  15.7 5.8 %collective-permute-start.7 = (f32[72,64]{1,0:T(8,128)S(1)}, f32[72,64]{1,0:T(8,128)S(1)}, u32[]{:S(2)}, u32[]{:S(2)}) collective-permute-start(f32[72,64]{1,0:T(8,128)S(1)} %get-tuple-element.80), channel_id=1, source_target_pairs={{0,3},{1,2},{2,1},{3,0},{4,7},{5,6},{6,5},{7,4},{8,11},{9,10},{10,... | collective-permute-start | bytes 55304 | tf_op jit(solution)/shard_map/ppermute | solution.py:531
